TPU v7x, 512 devices: a whole 4x4x16 slice. The times are simulated.
512 devices in a mesh: ep: 128 (over x, y_lo, z), dp: 4 (over y_hi, core).
Axes of the slice: x: 4, y: 4 (y_hi: 2, y_lo: 2; y = y_hi * 2 + y_lo), z: 16, core: 2. Of those that a mesh axis runs over, the one named last changes fastest.
Arguments:
- tokens: bfloat16 [65536, 2048], P(('ep', 'dp')), may hold values from -6 to 6
- cotangent: bfloat16 [65536, 2048], P(('ep', 'dp')), may hold values from -6 to 6
- experts: int32 [65536, 2], P(('ep', 'dp')), may hold values from 0 to 127, all different within a row; in each aligned block of 128 rows (0 to 127, 128 to 255, ...) at most 3 rows name the same one
- gates: float32 [65536, 2], P(('ep', 'dp')), may hold values from 0.2 to 1
- weights: bfloat16 [128, 3, 2048, 384], P('ep', None, 'dp'), may hold values from -0.1875 to 0.1875
- swap_flags: int32 [64], replicated, may hold values from 0 to 1, as said below
Outputs:
- outputs: bfloat16 [65536, 2048], P(('ep', 'dp'))
- input_grads: bfloat16 [65536, 2048], P(('ep', 'dp'))
- expert_grads: bfloat16 [128, 3, 2048, 384], P('ep', None, 'dp')
Inputs may be any that keep to these rules, and one draw needn't show every extreme that they name: `experts`: in each aligned block of 128 rows (the rows of one device) no expert is named more than 3 times; the two ids of a row differ. `swap_flags`: exactly 16 entries are 1.
All inputs are finite; a program needn't handle non-finite values.
Results may differ from a plain program's by a relative error of at most 0.012.
Values may be sent and summed in bfloat16 or wider, within the bound.
No kernel may reach another device: no remote copies, remote signals or barrier semaphores. Data moves between devices by JAX's collectives and lax.ppermute only.
A program may use at most 64 MiB of HBM per device.

v0:
```python
import jax
import jax.numpy as jnp
from jax import lax
from jax.sharding import PartitionSpec as P


def from_partner(value, axis, distance):
    mask = 2**distance
    pairs = [(source, source ^ mask) for source in range(lax.axis_size(axis))]
    return lax.ppermute(value, axis, pairs)


def body(tokens, cotangent, experts, gates, weights, swap_flags):
    ep_count = lax.axis_size("ep")
    dp_count = lax.axis_size("dp")
    half_ep = ep_count // 2
    flip_bit = ep_count.bit_length() - 2
    tok_rows, feature_dim = tokens.shape
    route_count = experts.shape[1]
    capacity = max(2, (tok_rows * route_count * 3 + 2 * ep_count - 1) // (2 * ep_count))
    slot_count = ep_count * capacity
    routed = experts.reshape(-1)
    pair_lanes = jnp.arange(half_ep, dtype=jnp.int32)
    flagged = (
        jnp.sum(
            jnp.where((routed % half_ep)[:, None] == pair_lanes[None, :], swap_flags[None, :], 0),
            axis=1,
        )
        > 0
    )
    my_index = lax.axis_index("ep")
    my_flag = jnp.sum(jnp.where(pair_lanes == my_index % half_ep, swap_flags, 0)) > 0
    target = jnp.where(flagged, (routed + half_ep) % ep_count, routed)
    dest_hot = (target[:, None] == jnp.arange(ep_count, dtype=jnp.int32)[None, :]).astype(jnp.int32)
    before = jnp.cumsum(dest_hot, axis=0) - dest_hot
    slot_rank = jnp.sum(before * dest_hot, axis=1)
    slot_index = target * capacity + slot_rank
    placer = (jnp.arange(slot_count, dtype=jnp.int32)[:, None] == slot_index[None, :]).astype(
        jnp.bfloat16
    )
    token_placer = jnp.sum(placer.reshape(slot_count, tok_rows, route_count), axis=2)
    send_x = jnp.dot(token_placer, tokens, preferred_element_type=jnp.float32).astype(jnp.bfloat16)
    scaled = (gates[:, :, None] * cotangent[:, None, :].astype(jnp.float32)).astype(jnp.bfloat16)
    scaled = scaled.reshape(tok_rows * route_count, feature_dim)
    send_dy = jnp.dot(placer, scaled, preferred_element_type=jnp.float32).astype(jnp.bfloat16)
    own_weights = weights[0]
    partner = from_partner(own_weights, "ep", flip_bit)
    own_weights = jnp.where(my_flag, partner, own_weights)
    full_weights = lax.all_gather(own_weights, "dp", axis=1, tiled=True)
    recv_x, recv_dy = (
        lax.all_to_all(
            send_x.reshape(ep_count, capacity, feature_dim),
            "ep",
            split_axis=0,
            concat_axis=0,
            tiled=True,
        ),
        lax.all_to_all(
            send_dy.reshape(ep_count, capacity, feature_dim),
            "ep",
            split_axis=0,
            concat_axis=0,
            tiled=True,
        ),
    )
    rows_x = recv_x.reshape(slot_count, feature_dim)
    rows_dy = recv_dy.reshape(slot_count, feature_dim)
    w_gate, w_up, w_down = (full_weights[0], full_weights[1], full_weights[2])
    pre_gate = jnp.dot(rows_x, w_gate, preferred_element_type=jnp.float32)
    pre_up = jnp.dot(rows_x, w_up, preferred_element_type=jnp.float32)
    gate_sig = jax.nn.sigmoid(pre_gate)
    gate_act = pre_gate * gate_sig
    hidden = (gate_act * pre_up).astype(jnp.bfloat16)
    expert_out = jnp.einsum("rf,df->rd", hidden, w_down, preferred_element_type=jnp.float32).astype(
        jnp.bfloat16
    )
    out_back = lax.all_to_all(
        expert_out.reshape(ep_count, capacity, feature_dim),
        "ep",
        split_axis=0,
        concat_axis=0,
        tiled=True,
    )
    hidden_grad = jnp.dot(rows_dy, w_down, preferred_element_type=jnp.float32)
    gate_pre = (hidden_grad * pre_up * gate_sig * (1.0 + pre_gate * (1.0 - gate_sig))).astype(
        jnp.bfloat16
    )
    up_pre = (hidden_grad * gate_act).astype(jnp.bfloat16)
    paired = jnp.concatenate([gate_pre, up_pre], axis=1)
    w_pair = jnp.concatenate([w_gate, w_up], axis=1)
    in_grad = jnp.einsum("rf,df->rd", paired, w_pair, preferred_element_type=jnp.float32).astype(
        jnp.bfloat16
    )
    grad_back = lax.all_to_all(
        in_grad.reshape(ep_count, capacity, feature_dim),
        "ep",
        split_axis=0,
        concat_axis=0,
        tiled=True,
    )
    shard_rows = feature_dim // dp_count
    unit_count = hidden.shape[1]
    pair_grad = lax.psum_scatter(
        jnp.einsum("rc,rf->cf", rows_x, paired, preferred_element_type=jnp.float32).astype(
            jnp.bfloat16
        ),
        "dp",
        scatter_dimension=0,
        tiled=True,
    ).astype(jnp.float32)
    down_term = jnp.einsum("rd,rf->df", rows_dy, hidden, preferred_element_type=jnp.float32)
    down_sum = lax.psum(down_term.astype(jnp.bfloat16), "dp").astype(jnp.float32)
    down_mine = lax.dynamic_slice_in_dim(down_sum, lax.axis_index("dp") * shard_rows, shard_rows, 0)
    weight_grads = jnp.stack(
        [pair_grad[:, :unit_count], pair_grad[:, unit_count:], down_mine]
    ).astype(jnp.bfloat16)[None]
    back_y = out_back.reshape(slot_count, feature_dim)
    back_dx = grad_back.reshape(slot_count, feature_dim)
    per_route = jnp.einsum("ra,rd->ad", placer, back_y, preferred_element_type=jnp.float32)
    per_route = per_route.reshape(tok_rows, route_count, feature_dim)
    outputs = jnp.sum(gates[:, :, None] * per_route, axis=1).astype(jnp.bfloat16)
    input_grads = jnp.einsum(
        "rt,rd->td", token_placer, back_dx, preferred_element_type=jnp.float32
    ).astype(jnp.bfloat16)
    return (outputs, input_grads, weight_grads)


def solution(mesh):
    return jax.shard_map(
        body,
        mesh=mesh,
        in_specs=(
            P(("ep", "dp"), None),
            P(("ep", "dp"), None),
            P(("ep", "dp"), None),
            P(("ep", "dp"), None),
            P("ep", None, "dp", None),
            P(),
        ),
        out_specs=(P(("ep", "dp"), None), P(("ep", "dp"), None), P("ep", None, "dp", None)),
        check_vma=False,
    )
```

profile of v0, /device:TPU:64, one launch (start us, length us, event | category | flops | bytes accessed | tf_op | source)
XLA Modules:
  0.0 500.0 jit_solution(119195241436367931)
XLA Ops:
  7.2 0.8 copy.37
  8.2 0.1 reshape.222
  8.3 0.7 select_reduce_fusion
  9.2 0.2 fusion.16
  9.5 0.2 fusion.18
  9.7 2.1 mul.79
  11.8 2.5 mul.80
  14.4 0.1 mul.77
  14.6 2.3 convolution_convert_fusion.3
  16.8 2.3 reshape.228
  19.2 19.7 %all-to-all-start.2 = ((bf16[128,3,2048]{2,1,0:T(4,128)(2,1)}), bf16[128,3,2048]{2,1,0:T(4,128)(2,1)S(1)}, u32[]{:S(2)}, u32[]{:S(2)}) async-start(bf16[128,3,2048]{2,1,0:T(4,128)(2,1)} %reshape.228), calls=%async_computation.2 | async-start | bytes 4194304 | tf_op jit(solution)/shard_map/all_to_all | solution.py:58
  38.9 5.2 %collective-permute-start = (bf16[3,512,384]{2,1,0:T(8,128)(2,1)}, bf16[3,512,384]{2,1,0:T(8,128)(2,1)}, u32[]{:S(2)}, u32[]{:S(2)}) collective-permute-start(bf16[3,512,384]{2,1,0:T(8,128)(2,1)} %bitcast.47), channel_id=1, source_target_pairs={{0,256},{4,260},{8,264},{12,268},{16,272},{20,276},{24,280},{28,28... | collective-permute-start | bytes 3538952 | tf_op jit(solution)/shard_map/ppermute | solution.py:10
  44.1 0.6 fusion.27
  45.4 32.6 %collective-permute-done = bf16[3,512,384]{2,1,0:T(8,128)(2,1)} collective-permute-done((bf16[3,512,384]{2,1,0:T(8,128)(2,1)}, bf16[3,512,384]{2,1,0:T(8,128)(2,1)}, u32[]{:S(2)}, u32[]{:S(2)}) %collective-permute-start) | collective-permute-done | bytes 1179680 | tf_op jit(solution)/shard_map/ppermute | solution.py:10
  78.1 2.4 broadcast_select_fusion
  80.7 0.2 gt.25
  81.1 1.7 convolution_convert_fusion.4
  82.8 5.2 %reshape.224 = bf16[128,3,2048]{2,1,0:T(4,128)(2,1)} reshape(bf16[384,2048]{1,0:T(8,128)(2,1)} %convolution_convert_fusion.4) | data formatting | bytes 3145728 | tf_op jit(solution)/shard_map/reshape | solution.py:52
  88.0 52.2 %all-to-all-done.2 = bf16[128,3,2048]{2,1,0:T(4,128)(2,1)S(1)} async-done(((bf16[128,3,2048]{2,1,0:T(4,128)(2,1)}), bf16[128,3,2048]{2,1,0:T(4,128)(2,1)S(1)}, u32[]{:S(2)}, u32[]{:S(2)}) %all-to-all-start.2) | async-done | bytes 1572896 | tf_op jit(solution)/shard_map/all_to_all | solution.py:58
  140.2 1.4 copy-done.1
  141.6 6.7 %all-to-all-start = ((bf16[128,3,2048]{2,1,0:T(4,128)(2,1)}), bf16[128,3,2048]{2,1,0:T(4,128)(2,1)}, u32[]{:S(2)}, u32[]{:S(2)}) async-start(bf16[128,3,2048]{2,1,0:T(4,128)(2,1)} %reshape.224), calls=%async_computation | async-start | bytes 4194304 | tf_op jit(solution)/shard_map/all_to_all | solution.py:51
  148.3 3.9 reshape.229
  152.2 96.6 %all-to-all-done = bf16[128,3,2048]{2,1,0:T(4,128)(2,1)} async-done(((bf16[128,3,2048]{2,1,0:T(4,128)(2,1)}), bf16[128,3,2048]{2,1,0:T(4,128)(2,1)}, u32[]{:S(2)}, u32[]{:S(2)}) %all-to-all-start) | async-done | bytes 1572896 | tf_op jit(solution)/shard_map/all_to_all | solution.py:51
  248.8 5.0 %reshape.225 = bf16[384,2048]{1,0:T(8,128)(2,1)} reshape(bf16[128,3,2048]{2,1,0:T(4,128)(2,1)} %all-to-all-done) | data formatting | bytes 3145728 | tf_op jit(solution)/shard_map/reshape | solution.py:66
  253.9 2.3 slice_bitcast_fusion.2
  256.2 0.9 copy-done.3
  257.2 1.0 fusion.8
  258.2 0.4 copy-done.4
  258.6 1.0 fusion.31
  259.6 1.3 multiply_convert_fusion.3
  260.9 0.7 copy-done.9
  261.6 2.6 fusion.4
  264.2 5.2 %reshape.230 = bf16[128,3,2048]{2,1,0:T(4,128)(2,1)} reshape(bf16[384,2048]{1,0:T(8,128)(2,1)} %fusion.4) | data formatting | bytes 3145728 | tf_op jit(solution)/shard_map/reshape | solution.py:95
  269.4 6.7 %all-to-all-start.3 = ((bf16[128,3,2048]{2,1,0:T(4,128)(2,1)}), bf16[128,3,2048]{2,1,0:T(4,128)(2,1)}, u32[]{:S(2)}, u32[]{:S(2)}) async-start(bf16[128,3,2048]{2,1,0:T(4,128)(2,1)} %reshape.230), calls=%async_computation.3 | async-start | bytes 4194304 | tf_op jit(solution)/shard_map/all_to_all | solution.py:94
  276.2 2.3 convolution_convert_fusion.1
  278.5 2.4 convolution_convert_fusion.2
  281.0 2.4 reshape.226
  283.3 93.5 %all-to-all-done.3 = bf16[128,3,2048]{2,1,0:T(4,128)(2,1)} async-done(((bf16[128,3,2048]{2,1,0:T(4,128)(2,1)}), bf16[128,3,2048]{2,1,0:T(4,128)(2,1)}, u32[]{:S(2)}, u32[]{:S(2)}) %all-to-all-start.3) | async-done | bytes 1572896 | tf_op jit(solution)/shard_map/all_to_all | solution.py:94
  376.8 6.2 %all-to-all-start.1 = ((bf16[128,3,2048]{2,1,0:T(4,128)(2,1)}), bf16[128,3,2048]{2,1,0:T(4,128)(2,1)S(1)}, u32[]{:S(2)}, u32[]{:S(2)}) async-start(bf16[128,3,2048]{2,1,0:T(4,128)(2,1)} %reshape.226), calls=%async_computation.1 | async-start | bytes 4194304 | tf_op jit(solution)/shard_map/all_to_all | solution.py:77
  383.1 5.0 %convolution_convert_fusion = bf16[2048,768]{1,0:T(8,128)(2,1)} fusion(bf16[384,2048]{1,0:T(8,128)(2,1)} %reshape.225, bf16[384,384]{0,1:T(8,128)(2,1)} %copy-done.9, bf16[384,384]{0,1:T(8,128)(2,1)} %copy-done.8), kind=kOutput, calls=%fused_computation | convolution fusion | flops 1210712064 | bytes 5308416 | tf_op jit(solution)/shard_map/rc,rf->cf/dot_general | solution.py:104
  388.4 1.0 fusion.11
  389.5 5.0 %reshape.231 = bf16[384,2048]{1,0:T(8,128)(2,1)} reshape(bf16[128,3,2048]{2,1,0:T(4,128)(2,1)} %all-to-all-done.3) | data formatting | bytes 3145728 | tf_op jit(solution)/shard_map/reshape | solution.py:118
  394.5 89.6 %all-to-all-done.1 = bf16[128,3,2048]{2,1,0:T(4,128)(2,1)S(1)} async-done(((bf16[128,3,2048]{2,1,0:T(4,128)(2,1)}), bf16[128,3,2048]{2,1,0:T(4,128)(2,1)S(1)}, u32[]{:S(2)}, u32[]{:S(2)}) %all-to-all-start.1) | async-done | bytes 1572896 | tf_op jit(solution)/shard_map/all_to_all | solution.py:77
  484.1 2.5 reshape.232
  486.6 3.2 fusion.7
  489.8 1.3 convolution_convert_fusion.5
  491.1 1.2 slice_bitcast_fusion.6
  492.3 1.2 pad_maximum_fusion
  (45 shorter events, 1.3 us)
Async XLA Ops:
  7.2 73.9 %copy-start = (bf16[128,2048]{1,0:T(8,128)(2,1)S(1)}, bf16[128,2048]{1,0:T(8,128)(2,1)}, u32[]{:S(2)}) copy-start(bf16[128,2048]{1,0:T(8,128)(2,1)} %param.6) | copy-start | bytes 1572868
  11.8 2.5 copy-start.6
  19.2 25.0 %copy-start.7 = (s32[64]{0:T(128)S(1)}, s32[64]{0:T(128)}, u32[]{:S(2)}) copy-start(s32[64]{0:T(128)} %param.11) | copy-start | bytes 772
  19.2 121.0 %all-to-all-start.2 = ((bf16[128,3,2048]{2,1,0:T(4,128)(2,1)}), bf16[128,3,2048]{2,1,0:T(4,128)(2,1)S(1)}, u32[]{:S(2)}, u32[]{:S(2)}) async-start(bf16[128,3,2048]{2,1,0:T(4,128)(2,1)} %reshape.228), calls=%async_computation.2 | async-start | bytes 4194304 | tf_op jit(solution)/shard_map/all_to_all | solution.py:58
  38.9 215.0 %all-gather.2.cloned.1.call-start = ((), (), s32[]{:S(2)}) async-start(), calls=%async_computation.5 | async-start | bytes 5898240 | tf_op jit(solution)/shard_map/all_gather | solution.py:49
  38.9 39.2 %collective-permute-start = (bf16[3,512,384]{2,1,0:T(8,128)(2,1)}, bf16[3,512,384]{2,1,0:T(8,128)(2,1)}, u32[]{:S(2)}, u32[]{:S(2)}) collective-permute-start(bf16[3,512,384]{2,1,0:T(8,128)(2,1)} %bitcast.47), channel_id=1, source_target_pairs={{0,256},{4,260},{8,264},{12,268},{16,272},{20,276},{24,280},{28,28... | collective-permute-start | bytes 3538952 | tf_op jit(solution)/shard_map/ppermute | solution.py:10
  45.4 35.6 %copy-start.5 = (s32[128,2]{0,1:T(2,128)S(1)}, s32[128,2]{0,1:T(2,128)}, u32[]{:S(2)}) copy-start(s32[128,2]{0,1:T(2,128)} %param.8) | copy-start | bytes 3076
  140.2 1.4 copy-start.1
  141.6 107.2 %all-to-all-start = ((bf16[128,3,2048]{2,1,0:T(4,128)(2,1)}), bf16[128,3,2048]{2,1,0:T(4,128)(2,1)}, u32[]{:S(2)}, u32[]{:S(2)}) async-start(bf16[128,3,2048]{2,1,0:T(4,128)(2,1)} %reshape.224), calls=%async_computation | async-start | bytes 4194304 | tf_op jit(solution)/shard_map/all_to_all | solution.py:51
  253.9 3.3 copy-start.3
  257.2 1.4 copy-start.4
  260.9 0.7 copy-start.9
  260.9 3.3 copy-start.8
  269.4 107.4 %all-to-all-start.3 = ((bf16[128,3,2048]{2,1,0:T(4,128)(2,1)}), bf16[128,3,2048]{2,1,0:T(4,128)(2,1)}, u32[]{:S(2)}, u32[]{:S(2)}) async-start(bf16[128,3,2048]{2,1,0:T(4,128)(2,1)} %reshape.230), calls=%async_computation.3 | async-start | bytes 4194304 | tf_op jit(solution)/shard_map/all_to_all | solution.py:94
  276.1 112.3 %all-reduce.2.cloned.1.call-start = ((), (), s32[]{:S(2)}) async-start(), calls=%async_computation.7 | async-start | bytes 3145728 | tf_op jit(solution)/shard_map/psum | solution.py:112
  376.8 107.3 %all-to-all-start.1 = ((bf16[128,3,2048]{2,1,0:T(4,128)(2,1)}), bf16[128,3,2048]{2,1,0:T(4,128)(2,1)S(1)}, u32[]{:S(2)}, u32[]{:S(2)}) async-start(bf16[128,3,2048]{2,1,0:T(4,128)(2,1)} %reshape.226), calls=%async_computation.1 | async-start | bytes 4194304 | tf_op jit(solution)/shard_map/all_to_all | solution.py:77
  383.0 108.0 %reduce-scatter.2.cloned.1.call-start = ((), (), s32[]{:S(2)}) async-start(), calls=%async_computation.6 | async-start | bytes 3932160 | tf_op jit(solution)/shard_map/reduce_scatter | solution.py:103
  486.6 3.2 copy-start.2
Sparse Core Ops, SparseCore 0:
  80.6 56.3 all-gather.1
  279.9 73.8 all-reduce.1
  388.2 67.8 reduce-scatter.1
where the time goes:
time: 501 us; the launch traced here: 500 us
  waiting for transfers between devices  365 us (73%)
  local copies, waits for them, and re-layouts  45.2 us (9%)
  starting transfers between devices  44.6 us (9%)
  matrix products  24.2 us (5%)
  between operations  14.7 us (3%)
  other arithmetic  6.69 us (1%)
    all_to_all x1, waiting for transfers between devices, body(): lax.all_to_all(send_x.reshape(ep_count, capacity, feature_dim), 'ep', spl...  96.6 us
    all_to_all x1, waiting for transfers between devices, body(): lax.all_to_all(in_grad.reshape(ep_count, capacity, feature_dim), 'ep', sp...  93.5 us
    all_to_all x1, waiting for transfers between devices, body(): lax.all_to_all(expert_out.reshape(ep_count, capacity, feature_dim), 'ep',...  89.6 us
    all_to_all x1, waiting for transfers between devices, body(): lax.all_to_all(send_dy.reshape(ep_count, capacity, feature_dim), 'ep', sp...  52.2 us
    ppermute x1, waiting for transfers between devices, from_partner(): return lax.ppermute(value, axis, pairs)  32.6 us
    all_to_all x1, starting transfers between devices, body(): lax.all_to_all(send_dy.reshape(ep_count, capacity, feature_dim), 'ep', sp...  19.7 us
  transfers between devices with their start and end apart: 8, of which 5 were waited for; matrix products, arithmetic and copies ran while one was open for 9% of the time, Pallas kernels for 0%

commit v1 on v0

v1 whole, which is shorter than its diff:
```python
import jax
import jax.numpy as jnp
from jax import lax
from jax.sharding import PartitionSpec as P

X_COUNT = 4
Y_COUNT = 2
Z_COUNT = 16
XY_COUNT = X_COUNT * Y_COUNT
CAP = 3


def xy_perm(value, dx, dy):
    pairs = []
    for source in range(X_COUNT * Y_COUNT * Z_COUNT):
        z = source % Z_COUNT
        y = (source // Z_COUNT) % Y_COUNT
        x = source // (Z_COUNT * Y_COUNT)
        dest = (((x + dx) % X_COUNT) * Y_COUNT + (y + dy) % Y_COUNT) * Z_COUNT + z
        pairs.append((source, dest))
    return lax.ppermute(value, "ep", pairs)


OFFSETS = [(k // Y_COUNT, k % Y_COUNT) for k in range(XY_COUNT)]


def xy_send(rows, sign):
    chunk = rows.shape[0] // XY_COUNT
    parts = []
    for k, (dx, dy) in enumerate(OFFSETS):
        part = rows[k * chunk : (k + 1) * chunk]
        parts.append(part if k == 0 else xy_perm(part, sign * dx, sign * dy))
    return jnp.concatenate(parts, axis=0)


def z_exchange(rows):
    groups = [[xy * Z_COUNT + z for z in range(Z_COUNT)] for xy in range(XY_COUNT)]
    chunk = rows.shape[0] // Z_COUNT
    moved = lax.all_to_all(
        rows.reshape(Z_COUNT, chunk, rows.shape[1]),
        "ep",
        split_axis=0,
        concat_axis=0,
        tiled=True,
        axis_index_groups=groups,
    )
    return moved.reshape(rows.shape)


def pick(one_hot, rows, contract):
    return lax.dot_general(
        one_hot, rows, (((contract,), (0,)), ((), ())), preferred_element_type=jnp.float32
    )


def body(tokens, cotangent, experts, gates, weights, swap_flags):
    ep_count = lax.axis_size("ep")
    half_ep = ep_count // 2
    tok_rows, feature_dim = tokens.shape
    route_count = experts.shape[1]
    slot_count = ep_count * CAP
    my_index = lax.axis_index("ep")
    pair_lanes = jnp.arange(half_ep, dtype=jnp.int32)

    my_flag = jnp.sum(jnp.where(pair_lanes == my_index % half_ep, swap_flags, 0)) > 0
    own_weights = weights[0]
    swap_pairs = [(source, source ^ half_ep) for source in range(ep_count)]
    partner = lax.ppermute(own_weights, "ep", swap_pairs)
    own_weights = jnp.where(my_flag, partner, own_weights)
    full_weights = lax.all_gather(own_weights, "dp", axis=1, tiled=True)

    routed = experts.reshape(-1)
    flagged = (
        jnp.sum(
            jnp.where((routed % half_ep)[:, None] == pair_lanes[None, :], swap_flags[None, :], 0),
            axis=1,
        )
        > 0
    )
    target = jnp.where(flagged, (routed + half_ep) % ep_count, routed)
    order = jnp.arange(tok_rows * route_count, dtype=jnp.int32)
    same = (target[:, None] == target[None, :]) & (order[:, None] > order[None, :])
    rank = jnp.sum(same.astype(jnp.int32), axis=1)
    slot = (target % Z_COUNT) * (XY_COUNT * CAP) + (target // Z_COUNT) * CAP + rank
    slot = slot.reshape(tok_rows, route_count)
    lanes = jnp.arange(slot_count, dtype=jnp.int32)[:, None]
    hits = [lanes == slot[:, k][None, :] for k in range(route_count)]
    placers = [hit.astype(jnp.bfloat16) for hit in hits]
    token_placer = (hits[0] | hits[1]).astype(jnp.bfloat16)
    slot_gate = sum(
        jnp.sum(jnp.where(hits[k], gates[:, k][None, :], 0.0), axis=1) for k in range(route_count)
    )

    row_id = jnp.arange(slot_count, dtype=jnp.int32)
    my_xy = my_index // Z_COUNT
    k_of = row_id // (Z_COUNT * CAP)
    z_of = (row_id // CAP) % Z_COUNT
    r_of = row_id % CAP
    to_x = (my_xy // Y_COUNT + k_of // Y_COUNT) % X_COUNT
    to_y = (my_xy % Y_COUNT + k_of % Y_COUNT) % Y_COUNT
    from_row = z_of * (XY_COUNT * CAP) + (to_x * Y_COUNT + to_y) * CAP + r_of
    perm = (from_row[:, None] == row_id[None, :]).astype(jnp.bfloat16)

    send_x = pick(token_placer, tokens, 1).astype(jnp.bfloat16)
    z_x = z_exchange(send_x)
    send_dy = (slot_gate[:, None] * pick(token_placer, cotangent, 1)).astype(jnp.bfloat16)
    send_dy, z_x = lax.optimization_barrier((send_dy, z_x))
    z_dy = z_exchange(send_dy)

    rows_x = xy_send(pick(perm, z_x, 1).astype(jnp.bfloat16), 1)
    w_gate, w_up, w_down = (full_weights[0], full_weights[1], full_weights[2])
    pre_gate = jnp.dot(rows_x, w_gate, preferred_element_type=jnp.float32)
    pre_up = jnp.dot(rows_x, w_up, preferred_element_type=jnp.float32)
    gate_sig = jax.nn.sigmoid(pre_gate)
    gate_act = pre_gate * gate_sig
    hidden = (gate_act * pre_up).astype(jnp.bfloat16)
    expert_out = jnp.einsum("rf,df->rd", hidden, w_down, preferred_element_type=jnp.float32).astype(
        jnp.bfloat16
    )
    home_y = pick(perm, xy_send(expert_out, -1), 0).astype(jnp.bfloat16)
    home_y, z_dy = lax.optimization_barrier((home_y, z_dy))
    back_y = z_exchange(home_y)

    rows_dy = xy_send(pick(perm, z_dy, 1).astype(jnp.bfloat16), 1)
    hidden_grad = jnp.dot(rows_dy, w_down, preferred_element_type=jnp.float32)
    gate_pre = (hidden_grad * pre_up * gate_sig * (1.0 + pre_gate * (1.0 - gate_sig))).astype(
        jnp.bfloat16
    )
    up_pre = (hidden_grad * gate_act).astype(jnp.bfloat16)
    paired = jnp.concatenate([gate_pre, up_pre], axis=1)
    w_pair = jnp.concatenate([w_gate, w_up], axis=1)
    in_grad = jnp.einsum("rf,df->rd", paired, w_pair, preferred_element_type=jnp.float32).astype(
        jnp.bfloat16
    )
    home_dx = pick(perm, xy_send(in_grad, -1), 0).astype(jnp.bfloat16)
    home_dx, back_y = lax.optimization_barrier((home_dx, back_y))
    back_dx = z_exchange(home_dx)

    unit_count = hidden.shape[1]
    pair_term = jnp.einsum("rc,rf->cf", rows_x, paired, preferred_element_type=jnp.float32)
    down_term = jnp.einsum("rd,rf->df", rows_dy, hidden, preferred_element_type=jnp.float32)
    pair_grad = lax.psum_scatter(
        pair_term.astype(jnp.bfloat16), "dp", scatter_dimension=0, tiled=True
    )
    down_mine = lax.psum_scatter(
        down_term.astype(jnp.bfloat16), "dp", scatter_dimension=0, tiled=True
    )
    weight_grads = jnp.stack(
        [pair_grad[:, :unit_count], pair_grad[:, unit_count:], down_mine]
    )[None]

    outputs = sum(
        gates[:, k][:, None] * pick(placers[k], back_y, 0) for k in range(route_count)
    ).astype(jnp.bfloat16)
    input_grads = pick(token_placer, back_dx, 0).astype(jnp.bfloat16)
    return (outputs, input_grads, weight_grads)


def solution(mesh):
    return jax.shard_map(
        body,
        mesh=mesh,
        in_specs=(
            P(("ep", "dp"), None),
            P(("ep", "dp"), None),
            P(("ep", "dp"), None),
            P(("ep", "dp"), None),
            P("ep", None, "dp", None),
            P(),
        ),
        out_specs=(P(("ep", "dp"), None), P(("ep", "dp"), None), P("ep", None, "dp", None)),
        check_vma=False,
    )
```

time: 501 us -> 397 us (0.79)
  the two profiles are of different devices: /device:TPU:64 before, /device:TPU:38 now
where the time goes in v1:
time: 397 us; the launch traced here: 395 us
  waiting for transfers between devices  163 us (41%)
  starting transfers between devices  153 us (39%)
  matrix products  38.4 us (10%)
  local copies, waits for them, and re-layouts  19.7 us (5%)
  between operations  15.1 us (4%)
  other arithmetic  5.86 us (1%)
    ppermute x28, starting transfers between devices, xy_perm(): return lax.ppermute(value, 'ep', pairs)  102 us
    all_to_all x4, waiting for transfers between devices, z_exchange(): lax.all_to_all(rows.reshape(Z_COUNT, chunk, rows.shape[1]), 'ep', split_a...  65.7 us
    reduce_scatter x1, waiting for transfers between devices, body(): lax.psum_scatter(down_term.astype(jnp.bfloat16), 'dp', scatter_dimension=...  52.2 us
    all_to_all x4, starting transfers between devices, z_exchange(): lax.all_to_all(rows.reshape(Z_COUNT, chunk, rows.shape[1]), 'ep', split_a...  47.6 us
    ppermute x28, waiting for transfers between devices, xy_perm(): return lax.ppermute(value, 'ep', pairs)  37.7 us
    dot_general x9, matrix products, pick(): lax.dot_general(one_hot, rows, (((contract,), (0,)), ((), ())), preferred...  16 us
    unnamed x43, local copies, waits for them, and re-layouts  12.3 us
  transfers between devices with their start and end apart: 36, of which 13 were waited for; matrix products, arithmetic and copies ran while one was open for 15% of the time, Pallas kernels for 0%

profile of v1, /device:TPU:38, one launch (start us, length us, event | category | flops | bytes accessed | tf_op | source)
XLA Modules:
  0.0 395.4 jit_solution(17617231055369571043)
XLA Ops:
  7.2 3.4 collective-permute-start.7
  15.5 15.3 %all-to-all-start = ((bf16[16,24,2048]{2,1,0:T(8,128)(2,1)}), bf16[16,24,2048]{2,1,0:T(8,128)(2,1)S(1)}, u32[]{:S(2)}, u32[]{:S(2)}) async-start(bf16[16,24,2048]{2,1,0:T(8,128)(2,1)} %bitcast.4), calls=%async_computation | async-start | bytes 3145728 | tf_op jit(solution)/shard_map/all_to_all | solution.py:39
  32.2 6.5 %collective-permute-done.7 = bf16[3,512,384]{2,1,0:T(8,128)(2,1)} collective-permute-done((bf16[3,512,384]{2,1,0:T(8,128)(2,1)}, bf16[3,512,384]{2,1,0:T(8,128)(2,1)}, u32[]{:S(2)}, u32[]{:S(2)}) %collective-permute-start.7) | collective-permute-done | bytes 1179680 | tf_op jit(solution)/shard_map/ppermute | solution.py:68
  42.7 60.1 %all-to-all-done = bf16[16,24,2048]{2,1,0:T(8,128)(2,1)S(1)} async-done(((bf16[16,24,2048]{2,1,0:T(8,128)(2,1)}), bf16[16,24,2048]{2,1,0:T(8,128)(2,1)S(1)}, u32[]{:S(2)}, u32[]{:S(2)}) %all-to-all-start) | async-done | bytes 1572896 | tf_op jit(solution)/shard_map/all_to_all | solution.py:39
  103.9 8.1 %all-to-all-start.1 = ((bf16[16,24,2048]{2,1,0:T(8,128)(2,1)}), bf16[16,24,2048]{2,1,0:T(8,128)(2,1)S(1)}, u32[]{:S(2)}, u32[]{:S(2)}) async-start(bf16[16,24,2048]{2,1,0:T(8,128)(2,1)} %bitcast.10), calls=%async_computation.1 | async-start | bytes 3145728 | tf_op jit(solution)/shard_map/all_to_all | solution.py:39
  112.1 2.4 convolution_convert_fusion.6
  115.4 3.5 collective-permute-start
  120.8 3.9 collective-permute-start.5
  124.7 5.5 %collective-permute-start.4 = (bf16[48,2048]{1,0:T(8,128)(2,1)S(1)}, bf16[48,2048]{1,0:T(8,128)(2,1)S(1)}, u32[]{:S(2)}, u32[]{:S(2)}) collective-permute-start(bf16[48,2048]{1,0:T(8,128)(2,1)S(1)} %get-tuple-element.45), channel_id=1, source_target_pairs={{0,320},{4,324},{8,328},{12,332},{16,336},{20,340},{24,344},{28,34... | collective-permute-start | bytes 589832 | tf_op jit(solution)/shard_map/ppermute | solution.py:21
  130.2 2.8 collective-permute-start.3
  133.0 3.1 collective-permute-start.1
  136.8 5.1 %collective-permute-done.1 = bf16[48,2048]{1,0:T(8,128)(2,1)S(1)} collective-permute-done((bf16[48,2048]{1,0:T(8,128)(2,1)S(1)}, bf16[48,2048]{1,0:T(8,128)(2,1)S(1)}, u32[]{:S(2)}, u32[]{:S(2)}) %collective-permute-start.1) | collective-permute-done | bytes 196640 | tf_op jit(solution)/shard_map/ppermute | solution.py:21
  141.9 4.6 %collective-permute-start.2 = (bf16[48,2048]{1,0:T(8,128)(2,1)S(1)}, bf16[48,2048]{1,0:T(8,128)(2,1)S(1)}, u32[]{:S(2)}, u32[]{:S(2)}) collective-permute-start(bf16[48,2048]{1,0:T(8,128)(2,1)S(1)} %get-tuple-element.47), channel_id=1, source_target_pairs={{0,192},{4,196},{8,200},{12,204},{16,208},{20,212},{24,216},{28,22... | collective-permute-start | bytes 589832 | tf_op jit(solution)/shard_map/ppermute | solution.py:21
  147.2 3.6 collective-permute-done.2
  154.3 2.9 fusion.59
  157.2 3.9 multiply_convert_fusion.3
  161.2 2.4 convolution_convert_fusion.5
  163.8 3.4 collective-permute-start.8
  167.2 5.3 %collective-permute-start.14 = (bf16[48,2048]{1,0:T(8,128)(2,1)S(1)}, bf16[48,2048]{1,0:T(8,128)(2,1)S(1)}, u32[]{:S(2)}, u32[]{:S(2)}) collective-permute-start(bf16[48,2048]{1,0:T(8,128)(2,1)S(1)} %get-tuple-element.35), channel_id=1, source_target_pairs={{0,192},{4,196},{8,200},{12,204},{16,208},{20,212},{24,216},{28,22... | collective-permute-start | bytes 589832 | tf_op jit(solution)/shard_map/ppermute | solution.py:21
  174.5 3.5 collective-permute-start.12
  178.0 3.8 collective-permute-start.11
  181.8 3.9 collective-permute-start.9
  185.8 6.2 %collective-permute-done.9 = bf16[48,2048]{1,0:T(8,128)(2,1)S(1)} collective-permute-done((bf16[48,2048]{1,0:T(8,128)(2,1)S(1)}, bf16[48,2048]{1,0:T(8,128)(2,1)S(1)}, u32[]{:S(2)}, u32[]{:S(2)}) %collective-permute-start.9) | collective-permute-done | bytes 196640 | tf_op jit(solution)/shard_map/ppermute | solution.py:21
  192.0 2.4 collective-permute-start.10
  194.3 7.3 %collective-permute-done.10 = bf16[48,2048]{1,0:T(8,128)(2,1)S(1)} collective-permute-done((bf16[48,2048]{1,0:T(8,128)(2,1)S(1)}, bf16[48,2048]{1,0:T(8,128)(2,1)S(1)}, u32[]{:S(2)}, u32[]{:S(2)}) %collective-permute-start.10) | collective-permute-done | bytes 196640 | tf_op jit(solution)/shard_map/ppermute | solution.py:21
  201.8 2.3 convolution_convert_fusion.4
  206.0 3.2 collective-permute-start.15
  209.2 12.0 %all-to-all-start.2 = ((bf16[16,24,2048]{2,1,0:T(8,128)(2,1)}), bf16[16,24,2048]{2,1,0:T(8,128)(2,1)S(1)}, u32[]{:S(2)}, u32[]{:S(2)}) async-start(bf16[16,24,2048]{2,1,0:T(8,128)(2,1)} %bitcast.57), calls=%async_computation.2 | async-start | bytes 3145728 | tf_op jit(solution)/shard_map/all_to_all | solution.py:39
  225.6 7.2 %collective-permute-start.19 = (bf16[48,2048]{1,0:T(8,128)(2,1)S(1)}, bf16[48,2048]{1,0:T(8,128)(2,1)S(1)}, u32[]{:S(2)}, u32[]{:S(2)}) collective-permute-start(bf16[48,2048]{1,0:T(8,128)(2,1)S(1)} %get-tuple-element.29), channel_id=1, source_target_pairs={{0,320},{4,324},{8,328},{12,332},{16,336},{20,340},{24,344},{28,34... | collective-permute-start | bytes 589832 | tf_op jit(solution)/shard_map/ppermute | solution.py:21
  234.7 4.0 %collective-permute-start.16 = (bf16[48,2048]{1,0:T(8,128)(2,1)}, bf16[48,2048]{1,0:T(8,128)(2,1)S(1)}, u32[]{:S(2)}, u32[]{:S(2)}) collective-permute-start(bf16[48,2048]{1,0:T(8,128)(2,1)} %get-tuple-element.32), channel_id=1, source_target_pairs={{0,128},{4,132},{8,136},{12,140},{16,144},{20,148},{24,152},{28,15... | collective-permute-start | bytes 589832 | tf_op jit(solution)/shard_map/ppermute | solution.py:21
  242.5 5.5 %collective-permute-start.17 = (bf16[48,2048]{1,0:T(8,128)(2,1)S(1)}, bf16[48,2048]{1,0:T(8,128)(2,1)S(1)}, u32[]{:S(2)}, u32[]{:S(2)}) collective-permute-start(bf16[48,2048]{1,0:T(8,128)(2,1)S(1)} %get-tuple-element.31), channel_id=1, source_target_pairs={{0,192},{4,196},{8,200},{12,204},{16,208},{20,212},{24,216},{28,22... | collective-permute-start | bytes 589832 | tf_op jit(solution)/shard_map/ppermute | solution.py:21
  248.7 2.3 collective-permute-done.17
  254.5 3.0 multiply_convert_fusion.2
  257.6 4.9 %convolution_convert_fusion = bf16[2048,768]{1,0:T(8,128)(2,1)} fusion(bf16[384,2048]{1,0:T(8,128)(2,1)} %constant_dynamic-update-slice_fusion, bf16[384,384]{0,1:T(8,128)(2,1)S(1)} %get-tuple-element.52, bf16[384,384]{0,1:T(8,128)(2,1)S(1)} %get-tuple-element.51), kind=kOutput, calls=%fused_computation | convolution fusion | flops 1210712064 | bytes 5308416 | tf_op jit(solution)/shard_map/rc,rf->cf/dot_general | solution.py:140
  266.2 3.2 collective-permute-start.22
  269.4 6.5 %collective-permute-start.28 = (bf16[48,2048]{1,0:T(8,128)(2,1)S(1)}, bf16[48,2048]{1,0:T(8,128)(2,1)S(1)}, u32[]{:S(2)}, u32[]{:S(2)}) collective-permute-start(bf16[48,2048]{1,0:T(8,128)(2,1)S(1)} %get-tuple-element.19), channel_id=1, source_target_pairs={{0,192},{4,196},{8,200},{12,204},{16,208},{20,212},{24,216},{28,22... | collective-permute-start | bytes 589832 | tf_op jit(solution)/shard_map/ppermute | solution.py:21
  277.9 2.3 collective-permute-start.26
  280.2 5.2 %collective-permute-start.25 = (bf16[48,2048]{1,0:T(8,128)(2,1)S(1)}, bf16[48,2048]{1,0:T(8,128)(2,1)S(1)}, u32[]{:S(2)}, u32[]{:S(2)}) collective-permute-start(bf16[48,2048]{1,0:T(8,128)(2,1)S(1)} %get-tuple-element.22), channel_id=1, source_target_pairs={{0,256},{4,260},{8,264},{12,268},{16,272},{20,276},{24,280},{28,28... | collective-permute-start | bytes 589832 | tf_op jit(solution)/shard_map/ppermute | solution.py:21
  285.4 3.9 collective-permute-start.23
  289.4 4.8 %collective-permute-done.23 = bf16[48,2048]{1,0:T(8,128)(2,1)S(1)} collective-permute-done((bf16[48,2048]{1,0:T(8,128)(2,1)S(1)}, bf16[48,2048]{1,0:T(8,128)(2,1)S(1)}, u32[]{:S(2)}, u32[]{:S(2)}) %collective-permute-start.23) | collective-permute-done | bytes 196640 | tf_op jit(solution)/shard_map/ppermute | solution.py:21
  294.2 3.4 collective-permute-start.24
  297.6 6.2 %collective-permute-done.24 = bf16[48,2048]{1,0:T(8,128)(2,1)S(1)} collective-permute-done((bf16[48,2048]{1,0:T(8,128)(2,1)S(1)}, bf16[48,2048]{1,0:T(8,128)(2,1)S(1)}, u32[]{:S(2)}, u32[]{:S(2)}) %collective-permute-start.24) | collective-permute-done | bytes 196640 | tf_op jit(solution)/shard_map/ppermute | solution.py:21
  304.0 2.3 convolution_convert_fusion.2
  306.3 12.0 %all-to-all-start.3 = ((bf16[16,24,2048]{2,1,0:T(8,128)(2,1)}), bf16[16,24,2048]{2,1,0:T(8,128)(2,1)}, u32[]{:S(2)}, u32[]{:S(2)}) async-start(bf16[16,24,2048]{2,1,0:T(8,128)(2,1)} %bitcast.60), calls=%async_computation.3 | async-start | bytes 3145728 | tf_op jit(solution)/shard_map/all_to_all | solution.py:39
  318.4 3.8 convolution_convert_fusion.1
  326.2 52.2 %reduce-scatter.5.cloned.1.call-done = bf16[512,384]{1,0:T(8,128)(2,1)} async-done(((bf16[2048,384]{1,0:T(8,128)(2,1)}), bf16[512,384]{1,0:T(8,128)(2,1)}) %reduce-scatter.5.cloned.1.call-update) | async-done | bytes 393232 | tf_op jit(solution)/shard_map/reduce_scatter | solution.py:145
  380.6 5.6 %all-to-all-done.3 = bf16[16,24,2048]{2,1,0:T(8,128)(2,1)} async-done(((bf16[16,24,2048]{2,1,0:T(8,128)(2,1)}), bf16[16,24,2048]{2,1,0:T(8,128)(2,1)}, u32[]{:S(2)}, u32[]{:S(2)}) %all-to-all-start.3) | async-done | bytes 1572896 | tf_op jit(solution)/shard_map/all_to_all | solution.py:39
  386.2 2.7 convolution_convert_fusion.8
  (114 shorter events, 48.7 us)
Async XLA Ops:
  7.2 6.6 %copy-start = (bf16[128,2048]{1,0:T(8,128)(2,1)S(1)}, bf16[128,2048]{1,0:T(8,128)(2,1)}, u32[]{:S(2)}) copy-start(bf16[128,2048]{1,0:T(8,128)(2,1)} %param.6) | copy-start | bytes 1572868
  7.2 31.6 %collective-permute-start.7 = (bf16[3,512,384]{2,1,0:T(8,128)(2,1)}, bf16[3,512,384]{2,1,0:T(8,128)(2,1)}, u32[]{:S(2)}, u32[]{:S(2)}) collective-permute-start(bf16[3,512,384]{2,1,0:T(8,128)(2,1)} %bitcast.61), channel_id=1, source_target_pairs={{0,256},{4,260},{8,264},{12,268},{16,272},{20,276},{24,280},{28,28... | collective-permute-start | bytes 3538952 | tf_op jit(solution)/shard_map/ppermute | solution.py:68
  15.5 15.4 %copy-start.5 = (s32[64]{0:T(128)S(1)}, s32[64]{0:T(128)}, u32[]{:S(2)}) copy-start(s32[64]{0:T(128)} %param.11) | copy-start | bytes 772
  15.5 23.2 %copy-start.2 = (bf16[1,3,512,384]{3,2,1,0:T(8,128)(2,1)S(1)}, bf16[1,3,512,384]{3,2,1,0:T(8,128)(2,1)}, u32[]{:S(2)}) copy-start(bf16[1,3,512,384]{3,2,1,0:T(8,128)(2,1)} %param.10) | copy-start | bytes 3538948
  15.5 87.3 %all-to-all-start = ((bf16[16,24,2048]{2,1,0:T(8,128)(2,1)}), bf16[16,24,2048]{2,1,0:T(8,128)(2,1)S(1)}, u32[]{:S(2)}, u32[]{:S(2)}) async-start(bf16[16,24,2048]{2,1,0:T(8,128)(2,1)} %bitcast.4), calls=%async_computation | async-start | bytes 3145728 | tf_op jit(solution)/shard_map/all_to_all | solution.py:39
  30.8 123.5 %all-gather.2.cloned.1.call-start = ((), (), s32[]{:S(2)}) async-start(), calls=%async_computation.6 | async-start | bytes 5898240 | tf_op jit(solution)/shard_map/all_gather | solution.py:70
  32.2 7.8 %copy-start.4 = (f32[128,2]{0,1:T(2,128)S(1)}, f32[128,2]{0,1:T(2,128)}, u32[]{:S(2)}) copy-start(f32[128,2]{0,1:T(2,128)} %param.9) | copy-start | bytes 3076
  39.9 1.0 copy-start.3
  102.8 1.2 copy-start.1
  103.9 100.1 %all-to-all-start.1 = ((bf16[16,24,2048]{2,1,0:T(8,128)(2,1)}), bf16[16,24,2048]{2,1,0:T(8,128)(2,1)S(1)}, u32[]{:S(2)}, u32[]{:S(2)}) async-start(bf16[16,24,2048]{2,1,0:T(8,128)(2,1)} %bitcast.10), calls=%async_computation.1 | async-start | bytes 3145728 | tf_op jit(solution)/shard_map/all_to_all | solution.py:39
  115.4 17.7 %collective-permute-start = (bf16[48,2048]{1,0:T(8,128)(2,1)S(1)}, bf16[48,2048]{1,0:T(8,128)(2,1)S(1)}, u32[]{:S(2)}, u32[]{:S(2)}) collective-permute-start(bf16[48,2048]{1,0:T(8,128)(2,1)S(1)} %get-tuple-element.49), channel_id=1, source_target_pairs={{0,64},{4,68},{8,72},{12,76},{16,80},{20,84},{24,88},{28,92},{32,9... | collective-permute-start | bytes 589832 | tf_op jit(solution)/shard_map/ppermute | solution.py:21
  118.9 34.8 %collective-permute-start.6 = (bf16[48,2048]{1,0:T(8,128)(2,1)S(1)}, bf16[48,2048]{1,0:T(8,128)(2,1)S(1)}, u32[]{:S(2)}, u32[]{:S(2)}) collective-permute-start(bf16[48,2048]{1,0:T(8,128)(2,1)S(1)} %get-tuple-element.43), channel_id=1, source_target_pairs={{0,448},{4,452},{8,456},{12,460},{16,464},{20,468},{24,472},{28,47... | collective-permute-start | bytes 589832 | tf_op jit(solution)/shard_map/ppermute | solution.py:21
  120.8 32.1 %collective-permute-start.5 = (bf16[48,2048]{1,0:T(8,128)(2,1)S(1)}, bf16[48,2048]{1,0:T(8,128)(2,1)S(1)}, u32[]{:S(2)}, u32[]{:S(2)}) collective-permute-start(bf16[48,2048]{1,0:T(8,128)(2,1)S(1)} %get-tuple-element.44), channel_id=1, source_target_pairs={{0,384},{4,388},{8,392},{12,396},{16,400},{20,404},{24,408},{28,41... | collective-permute-start | bytes 589832 | tf_op jit(solution)/shard_map/ppermute | solution.py:21
  124.7 27.6 %collective-permute-start.4 = (bf16[48,2048]{1,0:T(8,128)(2,1)S(1)}, bf16[48,2048]{1,0:T(8,128)(2,1)S(1)}, u32[]{:S(2)}, u32[]{:S(2)}) collective-permute-start(bf16[48,2048]{1,0:T(8,128)(2,1)S(1)} %get-tuple-element.45), channel_id=1, source_target_pairs={{0,320},{4,324},{8,328},{12,332},{16,336},{20,340},{24,344},{28,34... | collective-permute-start | bytes 589832 | tf_op jit(solution)/shard_map/ppermute | solution.py:21
  130.2 21.3 %collective-permute-start.3 = (bf16[48,2048]{1,0:T(8,128)(2,1)S(1)}, bf16[48,2048]{1,0:T(8,128)(2,1)S(1)}, u32[]{:S(2)}, u32[]{:S(2)}) collective-permute-start(bf16[48,2048]{1,0:T(8,128)(2,1)S(1)} %get-tuple-element.46), channel_id=1, source_target_pairs={{0,256},{4,260},{8,264},{12,268},{16,272},{20,276},{24,280},{28,28... | collective-permute-start | bytes 589832 | tf_op jit(solution)/shard_map/ppermute | solution.py:21
  133.0 8.9 %collective-permute-start.1 = (bf16[48,2048]{1,0:T(8,128)(2,1)S(1)}, bf16[48,2048]{1,0:T(8,128)(2,1)S(1)}, u32[]{:S(2)}, u32[]{:S(2)}) collective-permute-start(bf16[48,2048]{1,0:T(8,128)(2,1)S(1)} %get-tuple-element.48), channel_id=1, source_target_pairs={{0,128},{4,132},{8,136},{12,140},{16,144},{20,148},{24,152},{28,15... | collective-permute-start | bytes 589832 | tf_op jit(solution)/shard_map/ppermute | solution.py:21
  141.9 8.9 %collective-permute-start.2 = (bf16[48,2048]{1,0:T(8,128)(2,1)S(1)}, bf16[48,2048]{1,0:T(8,128)(2,1)S(1)}, u32[]{:S(2)}, u32[]{:S(2)}) collective-permute-start(bf16[48,2048]{1,0:T(8,128)(2,1)S(1)} %get-tuple-element.47), channel_id=1, source_target_pairs={{0,192},{4,196},{8,200},{12,204},{16,208},{20,212},{24,216},{28,22... | collective-permute-start | bytes 589832 | tf_op jit(solution)/shard_map/ppermute | solution.py:21
  157.2 3.9 copy-start.6
  163.8 18.0 %collective-permute-start.8 = (bf16[48,2048]{1,0:T(8,128)(2,1)S(1)}, bf16[48,2048]{1,0:T(8,128)(2,1)S(1)}, u32[]{:S(2)}, u32[]{:S(2)}) collective-permute-start(bf16[48,2048]{1,0:T(8,128)(2,1)S(1)} %get-tuple-element.41), channel_id=1, source_target_pairs={{0,64},{4,68},{8,72},{12,76},{16,80},{20,84},{24,88},{28,92},{32,9... | collective-permute-start | bytes 589832 | tf_op jit(solution)/shard_map/ppermute | solution.py:21
  167.2 34.5 %collective-permute-start.14 = (bf16[48,2048]{1,0:T(8,128)(2,1)S(1)}, bf16[48,2048]{1,0:T(8,128)(2,1)S(1)}, u32[]{:S(2)}, u32[]{:S(2)}) collective-permute-start(bf16[48,2048]{1,0:T(8,128)(2,1)S(1)} %get-tuple-element.35), channel_id=1, source_target_pairs={{0,192},{4,196},{8,200},{12,204},{16,208},{20,212},{24,216},{28,22... | collective-permute-start | bytes 589832 | tf_op jit(solution)/shard_map/ppermute | solution.py:21
  172.5 29.2 %collective-permute-start.13 = (bf16[48,2048]{1,0:T(8,128)(2,1)S(1)}, bf16[48,2048]{1,0:T(8,128)(2,1)S(1)}, u32[]{:S(2)}, u32[]{:S(2)}) collective-permute-start(bf16[48,2048]{1,0:T(8,128)(2,1)S(1)} %get-tuple-element.36), channel_id=1, source_target_pairs={{0,128},{4,132},{8,136},{12,140},{16,144},{20,148},{24,152},{28,15... | collective-permute-start | bytes 589832 | tf_op jit(solution)/shard_map/ppermute | solution.py:21
  174.5 27.2 %collective-permute-start.12 = (bf16[48,2048]{1,0:T(8,128)(2,1)S(1)}, bf16[48,2048]{1,0:T(8,128)(2,1)S(1)}, u32[]{:S(2)}, u32[]{:S(2)}) collective-permute-start(bf16[48,2048]{1,0:T(8,128)(2,1)S(1)} %get-tuple-element.37), channel_id=1, source_target_pairs={{0,320},{4,324},{8,328},{12,332},{16,336},{20,340},{24,344},{28,34... | collective-permute-start | bytes 589832 | tf_op jit(solution)/shard_map/ppermute | solution.py:21
  178.0 23.7 %collective-permute-start.11 = (bf16[48,2048]{1,0:T(8,128)(2,1)S(1)}, bf16[48,2048]{1,0:T(8,128)(2,1)S(1)}, u32[]{:S(2)}, u32[]{:S(2)}) collective-permute-start(bf16[48,2048]{1,0:T(8,128)(2,1)S(1)} %get-tuple-element.38), channel_id=1, source_target_pairs={{0,256},{4,260},{8,264},{12,268},{16,272},{20,276},{24,280},{28,28... | collective-permute-start | bytes 589832 | tf_op jit(solution)/shard_map/ppermute | solution.py:21
  181.8 10.1 %collective-permute-start.9 = (bf16[48,2048]{1,0:T(8,128)(2,1)S(1)}, bf16[48,2048]{1,0:T(8,128)(2,1)S(1)}, u32[]{:S(2)}, u32[]{:S(2)}) collective-permute-start(bf16[48,2048]{1,0:T(8,128)(2,1)S(1)} %get-tuple-element.40), channel_id=1, source_target_pairs={{0,384},{4,388},{8,392},{12,396},{16,400},{20,404},{24,408},{28,41... | collective-permute-start | bytes 589832 | tf_op jit(solution)/shard_map/ppermute | solution.py:21
  192.0 9.7 %collective-permute-start.10 = (bf16[48,2048]{1,0:T(8,128)(2,1)S(1)}, bf16[48,2048]{1,0:T(8,128)(2,1)S(1)}, u32[]{:S(2)}, u32[]{:S(2)}) collective-permute-start(bf16[48,2048]{1,0:T(8,128)(2,1)S(1)} %get-tuple-element.39), channel_id=1, source_target_pairs={{0,448},{4,452},{8,456},{12,460},{16,464},{20,468},{24,472},{28,47... | collective-permute-start | bytes 589832 | tf_op jit(solution)/shard_map/ppermute | solution.py:21
  206.0 28.7 %collective-permute-start.15 = (bf16[48,2048]{1,0:T(8,128)(2,1)}, bf16[48,2048]{1,0:T(8,128)(2,1)}, u32[]{:S(2)}, u32[]{:S(2)}) collective-permute-start(bf16[48,2048]{1,0:T(8,128)(2,1)} %get-tuple-element.33), channel_id=1, source_target_pairs={{0,64},{4,68},{8,72},{12,76},{16,80},{20,84},{24,88},{28,92},{32,9... | collective-permute-start | bytes 589832 | tf_op jit(solution)/shard_map/ppermute | solution.py:21
  209.2 97.1 %all-to-all-start.2 = ((bf16[16,24,2048]{2,1,0:T(8,128)(2,1)}), bf16[16,24,2048]{2,1,0:T(8,128)(2,1)S(1)}, u32[]{:S(2)}, u32[]{:S(2)}) async-start(bf16[16,24,2048]{2,1,0:T(8,128)(2,1)} %bitcast.57), calls=%async_computation.2 | async-start | bytes 3145728 | tf_op jit(solution)/shard_map/all_to_all | solution.py:39
  221.2 103.8 %reduce-scatter.3.cloned.1.call-start = ((), (), s32[]{:S(2)}) async-start(), calls=%async_computation.7 | async-start | bytes 3932160 | tf_op jit(solution)/shard_map/reduce_scatter | solution.py:142
  221.3 33.3 %copy-start.7 = (f32[384,384]{0,1:T(8,128)S(1)}, f32[384,384]{0,1:T(8,128)}, u32[]{:S(2)}) copy-start(f32[384,384]{0,1:T(8,128)} %copy-done.6) | copy-start | bytes 1769476
  221.3 33.3 %copy-start.8 = (f32[384,384]{0,1:T(8,128)S(1)}, f32[384,384]{0,1:T(8,128)}, u32[]{:S(2)}) copy-start(f32[384,384]{0,1:T(8,128)} %get-tuple-element.60) | copy-start | bytes 1769476
  221.3 32.5 %collective-permute-start.21 = (bf16[48,2048]{1,0:T(8,128)(2,1)S(1)}, bf16[48,2048]{1,0:T(8,128)(2,1)S(1)}, u32[]{:S(2)}, u32[]{:S(2)}) collective-permute-start(bf16[48,2048]{1,0:T(8,128)(2,1)S(1)} %get-tuple-element.27), channel_id=1, source_target_pairs={{0,448},{4,452},{8,456},{12,460},{16,464},{20,468},{24,472},{28,47... | collective-permute-start | bytes 589832 | tf_op jit(solution)/shard_map/ppermute | solution.py:21
  223.3 29.8 %collective-permute-start.20 = (bf16[48,2048]{1,0:T(8,128)(2,1)S(1)}, bf16[48,2048]{1,0:T(8,128)(2,1)S(1)}, u32[]{:S(2)}, u32[]{:S(2)}) collective-permute-start(bf16[48,2048]{1,0:T(8,128)(2,1)S(1)} %get-tuple-element.28), channel_id=1, source_target_pairs={{0,384},{4,388},{8,392},{12,396},{16,400},{20,404},{24,408},{28,41... | collective-permute-start | bytes 589832 | tf_op jit(solution)/shard_map/ppermute | solution.py:21
  225.6 26.8 %collective-permute-start.19 = (bf16[48,2048]{1,0:T(8,128)(2,1)S(1)}, bf16[48,2048]{1,0:T(8,128)(2,1)S(1)}, u32[]{:S(2)}, u32[]{:S(2)}) collective-permute-start(bf16[48,2048]{1,0:T(8,128)(2,1)S(1)} %get-tuple-element.29), channel_id=1, source_target_pairs={{0,320},{4,324},{8,328},{12,332},{16,336},{20,340},{24,344},{28,34... | collective-permute-start | bytes 589832 | tf_op jit(solution)/shard_map/ppermute | solution.py:21
  232.8 19.0 %collective-permute-start.18 = (bf16[48,2048]{1,0:T(8,128)(2,1)S(1)}, bf16[48,2048]{1,0:T(8,128)(2,1)S(1)}, u32[]{:S(2)}, u32[]{:S(2)}) collective-permute-start(bf16[48,2048]{1,0:T(8,128)(2,1)S(1)} %get-tuple-element.30), channel_id=1, source_target_pairs={{0,256},{4,260},{8,264},{12,268},{16,272},{20,276},{24,280},{28,28... | collective-permute-start | bytes 589832 | tf_op jit(solution)/shard_map/ppermute | solution.py:21
  234.7 7.8 %collective-permute-start.16 = (bf16[48,2048]{1,0:T(8,128)(2,1)}, bf16[48,2048]{1,0:T(8,128)(2,1)S(1)}, u32[]{:S(2)}, u32[]{:S(2)}) collective-permute-start(bf16[48,2048]{1,0:T(8,128)(2,1)} %get-tuple-element.32), channel_id=1, source_target_pairs={{0,128},{4,132},{8,136},{12,140},{16,144},{20,148},{24,152},{28,15... | collective-permute-start | bytes 589832 | tf_op jit(solution)/shard_map/ppermute | solution.py:21
  242.5 8.5 %collective-permute-start.17 = (bf16[48,2048]{1,0:T(8,128)(2,1)S(1)}, bf16[48,2048]{1,0:T(8,128)(2,1)S(1)}, u32[]{:S(2)}, u32[]{:S(2)}) collective-permute-start(bf16[48,2048]{1,0:T(8,128)(2,1)S(1)} %get-tuple-element.31), channel_id=1, source_target_pairs={{0,192},{4,196},{8,200},{12,204},{16,208},{20,212},{24,216},{28,22... | collective-permute-start | bytes 589832 | tf_op jit(solution)/shard_map/ppermute | solution.py:21
  266.2 19.2 %collective-permute-start.22 = (bf16[48,2048]{1,0:T(8,128)(2,1)S(1)}, bf16[48,2048]{1,0:T(8,128)(2,1)S(1)}, u32[]{:S(2)}, u32[]{:S(2)}) collective-permute-start(bf16[48,2048]{1,0:T(8,128)(2,1)S(1)} %get-tuple-element.25), channel_id=1, source_target_pairs={{0,64},{4,68},{8,72},{12,76},{16,80},{20,84},{24,88},{28,92},{32,9... | collective-permute-start | bytes 589832 | tf_op jit(solution)/shard_map/ppermute | solution.py:21
  269.4 34.6 %collective-permute-start.28 = (bf16[48,2048]{1,0:T(8,128)(2,1)S(1)}, bf16[48,2048]{1,0:T(8,128)(2,1)S(1)}, u32[]{:S(2)}, u32[]{:S(2)}) collective-permute-start(bf16[48,2048]{1,0:T(8,128)(2,1)S(1)} %get-tuple-element.19), channel_id=1, source_target_pairs={{0,192},{4,196},{8,200},{12,204},{16,208},{20,212},{24,216},{28,22... | collective-permute-start | bytes 589832 | tf_op jit(solution)/shard_map/ppermute | solution.py:21
  275.9 28.0 %collective-permute-start.27 = (bf16[48,2048]{1,0:T(8,128)(2,1)S(1)}, bf16[48,2048]{1,0:T(8,128)(2,1)S(1)}, u32[]{:S(2)}, u32[]{:S(2)}) collective-permute-start(bf16[48,2048]{1,0:T(8,128)(2,1)S(1)} %get-tuple-element.20), channel_id=1, source_target_pairs={{0,128},{4,132},{8,136},{12,140},{16,144},{20,148},{24,152},{28,15... | collective-permute-start | bytes 589832 | tf_op jit(solution)/shard_map/ppermute | solution.py:21
  277.9 26.1 %collective-permute-start.26 = (bf16[48,2048]{1,0:T(8,128)(2,1)S(1)}, bf16[48,2048]{1,0:T(8,128)(2,1)S(1)}, u32[]{:S(2)}, u32[]{:S(2)}) collective-permute-start(bf16[48,2048]{1,0:T(8,128)(2,1)S(1)} %get-tuple-element.21), channel_id=1, source_target_pairs={{0,320},{4,324},{8,328},{12,332},{16,336},{20,340},{24,344},{28,34... | collective-permute-start | bytes 589832 | tf_op jit(solution)/shard_map/ppermute | solution.py:21
  280.2 23.7 %collective-permute-start.25 = (bf16[48,2048]{1,0:T(8,128)(2,1)S(1)}, bf16[48,2048]{1,0:T(8,128)(2,1)S(1)}, u32[]{:S(2)}, u32[]{:S(2)}) collective-permute-start(bf16[48,2048]{1,0:T(8,128)(2,1)S(1)} %get-tuple-element.22), channel_id=1, source_target_pairs={{0,256},{4,260},{8,264},{12,268},{16,272},{20,276},{24,280},{28,28... | collective-permute-start | bytes 589832 | tf_op jit(solution)/shard_map/ppermute | solution.py:21
  285.4 8.8 %collective-permute-start.23 = (bf16[48,2048]{1,0:T(8,128)(2,1)S(1)}, bf16[48,2048]{1,0:T(8,128)(2,1)S(1)}, u32[]{:S(2)}, u32[]{:S(2)}) collective-permute-start(bf16[48,2048]{1,0:T(8,128)(2,1)S(1)} %get-tuple-element.24), channel_id=1, source_target_pairs={{0,384},{4,388},{8,392},{12,396},{16,400},{20,404},{24,408},{28,41... | collective-permute-start | bytes 589832 | tf_op jit(solution)/shard_map/ppermute | solution.py:21
  294.2 9.7 %collective-permute-start.24 = (bf16[48,2048]{1,0:T(8,128)(2,1)S(1)}, bf16[48,2048]{1,0:T(8,128)(2,1)S(1)}, u32[]{:S(2)}, u32[]{:S(2)}) collective-permute-start(bf16[48,2048]{1,0:T(8,128)(2,1)S(1)} %get-tuple-element.23), channel_id=1, source_target_pairs={{0,448},{4,452},{8,456},{12,460},{16,464},{20,468},{24,472},{28,47... | collective-permute-start | bytes 589832 | tf_op jit(solution)/shard_map/ppermute | solution.py:21
  306.3 79.9 %all-to-all-start.3 = ((bf16[16,24,2048]{2,1,0:T(8,128)(2,1)}), bf16[16,24,2048]{2,1,0:T(8,128)(2,1)}, u32[]{:S(2)}, u32[]{:S(2)}) async-start(bf16[16,24,2048]{2,1,0:T(8,128)(2,1)} %bitcast.60), calls=%async_computation.3 | async-start | bytes 3145728 | tf_op jit(solution)/shard_map/all_to_all | solution.py:39
  318.3 60.1 %reduce-scatter.5.cloned.1.call-start = ((), (), s32[]{:S(2)}) async-start(), calls=%async_computation.8 | async-start | bytes 1966080 | tf_op jit(solution)/shard_map/reduce_scatter | solution.py:145
Sparse Core Ops, SparseCore 0:
  40.0 54.4 all-gather.1
  262.6 62.3 reduce-scatter.2
  328.4 49.9 reduce-scatter.4

commit v2 on v1

v2 whole, which is shorter than its diff:
```python
import jax
import jax.numpy as jnp
import numpy as np
from jax import lax
from jax.experimental import pallas as pl
from jax.experimental.pallas import tpu as pltpu
from jax.sharding import PartitionSpec as P

CAP = 3
QUARTERS = 4
GROUP = 16
CHUNK = 2 * QUARTERS * CAP
BLOCK = GROUP * CHUNK
LANES = GROUP * CAP
MIB = 1 << 20


def unfold_matrix():
    row = np.arange(BLOCK)
    array, quarter = row // (BLOCK // 2), (row // LANES) % QUARTERS
    peer, route = (row % LANES) // CAP, row % CAP
    source = peer * CHUNK + array * (CHUNK // 2) + quarter * CAP + route
    return (source[:, None] == row[None, :]).astype(np.float32)


def fold_block(block, first, second, fold):
    width = first.shape[1] // QUARTERS
    rows = slice(block * LANES, (block + 1) * LANES)
    parts = [
        ref[rows, q * width : (q + 1) * width] for ref in (first, second) for q in range(QUARTERS)
    ]
    stacked = jnp.concatenate(parts, axis=0)
    return jnp.dot(fold, stacked, preferred_element_type=jnp.float32).astype(jnp.bfloat16)


def unfold_block(block, chunks, unfold, first, second):
    width = chunks.shape[1]
    rows = slice(block * LANES, (block + 1) * LANES)
    opened = jnp.dot(unfold, chunks, preferred_element_type=jnp.float32).astype(jnp.bfloat16)
    for index, ref in enumerate((first, second)):
        for q in range(QUARTERS):
            start = (index * QUARTERS + q) * LANES
            ref[rows, q * width : (q + 1) * width] = opened[start : start + LANES]


def prep_kernel(
    tok_ref, cot_ref, ecol_ref, erow_ref, grow_ref, fcol_ref, frow_ref, fold_ref,
    send_ref, scol_ref, srow_ref, x_ref, dy_ref, out_ref, sems,
):
    tok_rows, feature_dim = tok_ref.shape
    half = frow_ref.shape[1]
    slot_count = x_ref.shape[0]

    def flag_bit(mask, flags, axis):
        return jnp.sum(jnp.where(mask, flags, 0), axis=axis, keepdims=True) * half

    tcol, trow = [], []
    for k in range(2):
        col, row = ecol_ref[:, k : k + 1], erow_ref[k : k + 1, :]
        lane = lax.broadcasted_iota(jnp.int32, (tok_rows, half), 1)
        sub = lax.broadcasted_iota(jnp.int32, (half, tok_rows), 0)
        tcol.append(col ^ flag_bit((col & (half - 1)) == lane, frow_ref[...], 1))
        trow.append(row ^ flag_bit((row & (half - 1)) == sub, fcol_ref[...], 0))
    sub = lax.broadcasted_iota(jnp.int32, (tok_rows, tok_rows), 0)
    lane = lax.broadcasted_iota(jnp.int32, (tok_rows, tok_rows), 1)
    srows = []
    for k in range(2):
        rank_row = jnp.zeros((1, tok_rows), jnp.int32)
        rank_col = jnp.zeros((tok_rows, 1), jnp.int32)
        for j in range(2):
            above = sub * 2 + j < lane * 2 + k
            hit = (tcol[j] == trow[k]) & above
            rank_row += jnp.sum(jnp.where(hit, 1, 0), axis=0, keepdims=True)
            before = lane * 2 + j < sub * 2 + k
            hit = (tcol[k] == trow[j]) & before
            rank_col += jnp.sum(jnp.where(hit, 1, 0), axis=1, keepdims=True)
        srows.append(trow[k] * CAP + rank_row)
        srow_ref[k : k + 1, :] = srows[k]
        scol_ref[:, k : k + 1] = tcol[k] * CAP + rank_col
    slot = lax.broadcasted_iota(jnp.int32, (slot_count, tok_rows), 0)
    hits = [slot == srows[k] for k in range(2)]
    gate = sum(
        jnp.sum(jnp.where(hits[k], grow_ref[k : k + 1, :], 0.0), axis=1, keepdims=True)
        for k in range(2)
    )
    placer = jnp.where(hits[0] | hits[1], 1.0, 0.0).astype(jnp.bfloat16)
    width = feature_dim // QUARTERS
    for q in range(QUARTERS):
        cols = slice(q * width, (q + 1) * width)
        x = jnp.dot(placer, tok_ref[:, cols], preferred_element_type=jnp.float32)
        x_ref[:, cols] = x.astype(jnp.bfloat16)
        dy = jnp.dot(placer, cot_ref[:, cols], preferred_element_type=jnp.float32)
        dy_ref[:, cols] = (gate * dy).astype(jnp.bfloat16)
    fold = fold_ref[...]
    copies = []
    for b in range(slot_count // LANES):
        out_ref[b] = fold_block(b, x_ref, dy_ref, fold)
        copies.append(pltpu.make_async_copy(out_ref.at[b], send_ref.at[b], sems.at[b]))
        copies[b].start()
    for copy in copies:
        copy.wait()


def expert_kernel(
    recv_ref, w_ref, unfold_ref, fold_ref,
    send_ref, x_out, dy_out, hidden_ref, paired_ref,
    chunk_ref, wv_ref, x_ref, dy_ref, y_ref, dx_ref, r_sems, w_sems, s_sems, u_sems,
):
    blocks = chunk_ref.shape[0]
    feature_dim = x_ref.shape[1]
    units = hidden_ref.shape[1]
    arrivals = [
        pltpu.make_async_copy(recv_ref.at[b], chunk_ref.at[b], r_sems.at[b]) for b in range(blocks)
    ]
    loads = [pltpu.make_async_copy(w_ref.at[i], wv_ref.at[i], w_sems.at[i]) for i in range(3)]
    for copy in arrivals + loads:
        copy.start()
    unfold = unfold_ref[...]
    for b in range(blocks):
        arrivals[b].wait()
        unfold_block(b, chunk_ref[b], unfold, x_ref, dy_ref)
    keeps = [
        pltpu.make_async_copy(x_ref, x_out, u_sems.at[0]),
        pltpu.make_async_copy(dy_ref, dy_out, u_sems.at[1]),
    ]
    for copy in keeps:
        copy.start()
    for copy in loads:
        copy.wait()
    x, dy = x_ref[...], dy_ref[...]
    pre_gate = jnp.dot(x, wv_ref[0], preferred_element_type=jnp.float32)
    pre_up = jnp.dot(x, wv_ref[1], preferred_element_type=jnp.float32)
    hidden_grad = jnp.dot(dy, wv_ref[2], preferred_element_type=jnp.float32)
    gate_sig = jax.nn.sigmoid(pre_gate)
    gate_act = pre_gate * gate_sig
    hidden = (gate_act * pre_up).astype(jnp.bfloat16)
    gate_pre = (hidden_grad * pre_up * gate_sig * (1.0 + pre_gate * (1.0 - gate_sig))).astype(
        jnp.bfloat16
    )
    up_pre = (hidden_grad * gate_act).astype(jnp.bfloat16)
    hidden_ref[...] = hidden
    paired_ref[:, :units] = gate_pre
    paired_ref[:, units:] = up_pre
    across = (((1,), (1,)), ((), ()))
    width = feature_dim // QUARTERS
    for q in range(QUARTERS):
        cols = slice(q * width, (q + 1) * width)
        y = lax.dot_general(hidden, wv_ref[2, cols, :], across, preferred_element_type=jnp.float32)
        y_ref[:, cols] = y.astype(jnp.bfloat16)
        dx = lax.dot_general(
            gate_pre, wv_ref[0, cols, :], across, preferred_element_type=jnp.float32
        ) + lax.dot_general(up_pre, wv_ref[1, cols, :], across, preferred_element_type=jnp.float32)
        dx_ref[:, cols] = dx.astype(jnp.bfloat16)
    fold = fold_ref[...]
    copies = []
    for b in range(blocks):
        chunk_ref[b] = fold_block(b, y_ref, dx_ref, fold)
        copies.append(pltpu.make_async_copy(chunk_ref.at[b], send_ref.at[b], s_sems.at[b]))
        copies[b].start()
    for copy in keeps + copies:
        copy.wait()


def finish_kernel(
    recv_ref, scol_ref, gates_ref, unfold_ref, out_ref, grad_ref, chunk_ref, y_ref, dx_ref, sems,
):
    blocks = chunk_ref.shape[0]
    tok_rows, feature_dim = out_ref.shape
    slot_count = y_ref.shape[0]
    arrivals = [
        pltpu.make_async_copy(recv_ref.at[b], chunk_ref.at[b], sems.at[b]) for b in range(blocks)
    ]
    for copy in arrivals:
        copy.start()
    slot = lax.broadcasted_iota(jnp.int32, (tok_rows, slot_count), 1)
    hits = [slot == scol_ref[:, k : k + 1] for k in range(2)]
    takers = [jnp.where(hit, 1.0, 0.0).astype(jnp.bfloat16) for hit in hits]
    both = jnp.where(hits[0] | hits[1], 1.0, 0.0).astype(jnp.bfloat16)
    unfold = unfold_ref[...]
    for b in range(blocks):
        arrivals[b].wait()
        unfold_block(b, chunk_ref[b], unfold, y_ref, dx_ref)
    width = feature_dim // QUARTERS
    for q in range(QUARTERS):
        cols = slice(q * width, (q + 1) * width)
        total = sum(
            gates_ref[:, k : k + 1]
            * jnp.dot(takers[k], y_ref[:, cols], preferred_element_type=jnp.float32)
            for k in range(2)
        )
        out_ref[:, cols] = total.astype(jnp.bfloat16)
        grad = jnp.dot(both, dx_ref[:, cols], preferred_element_type=jnp.float32)
        grad_ref[:, cols] = grad.astype(jnp.bfloat16)


def exchange(chunks, ep_count):
    width = chunks.shape[-1]
    moved = lax.all_to_all(
        chunks.reshape(ep_count, CHUNK, width), "ep", split_axis=0, concat_axis=0, tiled=True
    )
    return moved.reshape(chunks.shape)


def body(tokens, cotangent, experts, gates, weights, swap_flags):
    ep_count = lax.axis_size("ep")
    half_ep = ep_count // 2
    tok_rows, feature_dim = tokens.shape
    slot_count = ep_count * CAP
    blocks = ep_count // GROUP
    units = weights.shape[3]
    width = feature_dim // QUARTERS
    my_index = lax.axis_index("ep")
    bf16 = jnp.bfloat16
    vmem, hbm = pl.BlockSpec(memory_space=pltpu.VMEM), pl.BlockSpec(memory_space=pl.ANY)
    unfold = unfold_matrix()
    fold = jnp.asarray(unfold.T, bf16)
    unfold = jnp.asarray(unfold, bf16)
    chunks_shape = jax.ShapeDtypeStruct((blocks, BLOCK, width), bf16)
    rows_shape = jax.ShapeDtypeStruct((slot_count, feature_dim), bf16)
    rows_vmem = pltpu.VMEM((slot_count, feature_dim), bf16)
    chunks_vmem = pltpu.VMEM((blocks, BLOCK, width), bf16)
    block_sems = pltpu.SemaphoreType.DMA((blocks,))

    send, slot_col, _ = pl.pallas_call(
        prep_kernel,
        out_shape=(
            chunks_shape,
            jax.ShapeDtypeStruct((tok_rows, 2), jnp.int32),
            jax.ShapeDtypeStruct((2, tok_rows), jnp.int32),
        ),
        in_specs=[vmem] * 8,
        out_specs=(hbm, vmem, vmem),
        scratch_shapes=[rows_vmem, rows_vmem, chunks_vmem, block_sems],
        compiler_params=pltpu.CompilerParams(vmem_limit_bytes=24 * MIB),
        name="prep",
    )(
        tokens, cotangent, experts, experts.T, gates.T,
        swap_flags.reshape(half_ep, 1), swap_flags.reshape(1, half_ep), fold,
    )

    pair_lanes = jnp.arange(half_ep, dtype=jnp.int32)
    my_flag = jnp.sum(jnp.where(pair_lanes == my_index % half_ep, swap_flags, 0)) > 0
    own_weights = weights[0]
    swap_pairs = [(source, source ^ half_ep) for source in range(ep_count)]
    partner = lax.ppermute(own_weights, "ep", swap_pairs)
    own_weights = jnp.where(my_flag, partner, own_weights)
    full_weights = lax.all_gather(own_weights, "dp", axis=1, tiled=True)

    recv = exchange(send, ep_count)

    send_back, rows_x, rows_dy, hidden, paired = pl.pallas_call(
        expert_kernel,
        out_shape=(
            chunks_shape,
            rows_shape,
            rows_shape,
            jax.ShapeDtypeStruct((slot_count, units), bf16),
            jax.ShapeDtypeStruct((slot_count, 2 * units), bf16),
        ),
        in_specs=[hbm, hbm, vmem, vmem],
        out_specs=(hbm, hbm, hbm, vmem, vmem),
        scratch_shapes=[
            chunks_vmem,
            pltpu.VMEM((3, feature_dim, units), bf16),
            rows_vmem,
            rows_vmem,
            rows_vmem,
            rows_vmem,
            block_sems,
            pltpu.SemaphoreType.DMA((3,)),
            block_sems,
            pltpu.SemaphoreType.DMA((2,)),
        ],
        compiler_params=pltpu.CompilerParams(vmem_limit_bytes=44 * MIB),
        name="expert",
    )(recv, full_weights, unfold, fold)

    recv_back = exchange(send_back, ep_count)

    pair_term = jnp.einsum("rc,rf->cf", rows_x, paired, preferred_element_type=jnp.float32)
    down_term = jnp.einsum("rd,rf->df", rows_dy, hidden, preferred_element_type=jnp.float32)
    terms = jnp.concatenate([pair_term.astype(bf16), down_term.astype(bf16)], axis=1)
    mine = lax.psum_scatter(terms, "dp", scatter_dimension=0, tiled=True)
    weight_grads = jnp.stack(
        [mine[:, :units], mine[:, units : 2 * units], mine[:, 2 * units :]]
    )[None]

    outputs, input_grads = pl.pallas_call(
        finish_kernel,
        out_shape=(
            jax.ShapeDtypeStruct((tok_rows, feature_dim), bf16),
            jax.ShapeDtypeStruct((tok_rows, feature_dim), bf16),
        ),
        in_specs=[hbm, vmem, vmem, vmem],
        out_specs=(vmem, vmem),
        scratch_shapes=[chunks_vmem, rows_vmem, rows_vmem, block_sems],
        compiler_params=pltpu.CompilerParams(vmem_limit_bytes=24 * MIB),
        name="finish",
    )(recv_back, slot_col, gates, unfold)
    return (outputs, input_grads, weight_grads)


def solution(mesh):
    return jax.shard_map(
        body,
        mesh=mesh,
        in_specs=(
            P(("ep", "dp"), None),
            P(("ep", "dp"), None),
            P(("ep", "dp"), None),
            P(("ep", "dp"), None),
            P("ep", None, "dp", None),
            P(),
        ),
        out_specs=(P(("ep", "dp"), None), P(("ep", "dp"), None), P("ep", None, "dp", None)),
        check_vma=False,
    )
```

time: 397 us -> 371 us (0.935)
  the two profiles are of different devices: /device:TPU:38 before, /device:TPU:64 now
where the time goes in v2:
time: 371 us; the launch traced here: 370 us
  waiting for transfers between devices  271 us (73%)
  starting transfers between devices  31.8 us (9%)
  Pallas kernels  24.5 us (7%)
  local copies, waits for them, and re-layouts  18 us (5%)
  between operations  14.9 us (4%)
  other arithmetic  5.46 us (1%)
  matrix products  4.46 us (1%)
    all_to_all x2, waiting for transfers between devices, exchange(): lax.all_to_all(chunks.reshape(ep_count, CHUNK, width), 'ep', split_axis=0...  99 us
    reduce_scatter x1, waiting for transfers between devices, body(): mine = lax.psum_scatter(terms, 'dp', scatter_dimension=0, tiled=True)  79.9 us
    all_gather x1, waiting for transfers between devices, body(): full_weights = lax.all_gather(own_weights, 'dp', axis=1, tiled=True)  60.5 us
    ppermute x1, waiting for transfers between devices, body(): partner = lax.ppermute(own_weights, 'ep', swap_pairs)  31.7 us
    all_to_all x2, starting transfers between devices, exchange(): lax.all_to_all(chunks.reshape(ep_count, CHUNK, width), 'ep', split_axis=0...  26.1 us
    unnamed x43, local copies, waits for them, and re-layouts  16 us
    pallas_call x1, Pallas kernels, body(): pl.pallas_call(expert_kernel, out_shape=(chunks_shape, rows_shape, rows_s...  13.8 us
  transfers between devices with their start and end apart: 5, of which 5 were waited for; matrix products, arithmetic and copies ran while one was open for 4% of the time, Pallas kernels for 0%

profile of v2, /device:TPU:64, one launch (start us, length us, event | category | flops | bytes accessed | tf_op | source)
XLA Modules:
  0.0 370.2 jit_solution(8737034702215735577)
XLA Ops:
  7.2 0.8 copy.11.ecol_ref
  8.0 0.7 copy.12.fcol_ref
  8.7 1.0 copy-done.3
  9.7 1.0 copy-done.5
  10.7 1.0 copy-done.6
  11.7 0.7 copy-done.10
  12.4 0.7 copy-done.11
  13.1 0.7 copy-done.13
  13.8 4.4 %prep.1 = (bf16[8,384,512]{2,1,0:T(8,128)(2,1)}, s32[128,2]{1,0:T(8,128)S(1)}, s32[2,128]{1,0:T(2,128)}) custom-call(bf16[128,2048]{1,0:T(8,128)(2,1)S(1)} %copy-done.5, bf16[128,2048]{1,0:T(8,128)(2,1)S(1)} %copy-done.6, s32[128,2]{1,0:T(8,128)S(1)} %copy.11.ecol_ref, s32[2,128]{1,0:T(2,128)S(1)} %bitcast.24, f32[2,128]{1,0:T(2,128)S(1)} %bitcast.25, ...), custom_call_target="tpu_custom_call" | custom-call | tf_op jit(solution)/shard_map/prep/pallas_call | solution.py:224
  18.2 0.0 copy-start.8
  18.2 0.6 copy-done.8
  18.8 20.1 %all-to-all-start = ((bf16[128,24,512]{2,1,0:T(8,128)(2,1)}), bf16[128,24,512]{2,1,0:T(8,128)(2,1)}, u32[]{:S(2)}, u32[]{:S(2)}) async-start(bf16[128,24,512]{2,1,0:T(8,128)(2,1)} %bitcast.4), calls=%async_computation | async-start | bytes 6291456 | tf_op jit(solution)/shard_map/all_to_all | solution.py:198
  38.9 0.0 all-gather.2.cloned.1.call-start
  38.9 0.0 copy-done.19
  39.0 5.4 %collective-permute-start = (bf16[3,512,384]{2,1,0:T(8,128)(2,1)S(1)}, bf16[3,512,384]{2,1,0:T(8,128)(2,1)S(1)}, u32[]{:S(2)}, u32[]{:S(2)}) collective-permute-start(bf16[3,512,384]{2,1,0:T(8,128)(2,1)S(1)} %bitcast.28), channel_id=1, source_target_pairs={{0,256},{4,260},{8,264},{12,268},{16,272},{20,276},{24,280},{28,28... | collective-permute-start | bytes 3538952 | tf_op jit(solution)/shard_map/ppermute | solution.py:245
  44.4 0.0 copy-done.14
  44.4 0.6 fusion
  45.7 0.0 copy-start.2
  45.7 0.0 copy-start.4
  45.7 31.7 %collective-permute-done = bf16[3,512,384]{2,1,0:T(8,128)(2,1)S(1)} collective-permute-done((bf16[3,512,384]{2,1,0:T(8,128)(2,1)S(1)}, bf16[3,512,384]{2,1,0:T(8,128)(2,1)S(1)}, u32[]{:S(2)}, u32[]{:S(2)}) %collective-permute-start) | collective-permute-done | bytes 1179680 | tf_op jit(solution)/shard_map/ppermute | solution.py:245
  77.3 1.2 broadcast_select_fusion
  78.5 0.0 all-gather.2.cloned.1.call-update
  78.5 60.5 %all-gather.2.cloned.1.call-done.w_ref = bf16[3,2048,384]{2,1,0:T(8,128)(2,1)} async-done(((bf16[3,512,384]{2,1,0:T(8,128)(2,1)}), bf16[3,2048,384]{2,1,0:T(8,128)(2,1)}) %all-gather.2.cloned.1.call-update) | async-done | bytes 4718608 | tf_op jit(solution)/shard_map/all_gather | solution.py:247
  139.0 46.0 %all-to-all-done = bf16[128,24,512]{2,1,0:T(8,128)(2,1)} async-done(((bf16[128,24,512]{2,1,0:T(8,128)(2,1)}), bf16[128,24,512]{2,1,0:T(8,128)(2,1)}, u32[]{:S(2)}, u32[]{:S(2)}) %all-to-all-start) | async-done | bytes 3145760 | tf_op jit(solution)/shard_map/all_to_all | solution.py:198
  185.0 0.0 copy-done.2
  185.0 0.0 copy-done.4
  185.0 13.8 %expert.1 = (bf16[8,384,512]{2,1,0:T(8,128)(2,1)S(1)}, bf16[384,2048]{1,0:T(8,128)(2,1)S(1)}, bf16[384,2048]{1,0:T(8,128)(2,1)S(1)}, bf16[384,384]{1,0:T(8,128)(2,1)S(1)}, bf16[384,768]{1,0:T(8,128)(2,1)S(1)}) custom-call(bf16[8,384,512]{2,1,0:T(8,128)(2,1)} %bitcast.5.recv_ref, bf16[3,2048,384]{2,1,0:T(8,128)(2,1)} %all-gather.2.cloned.1.call-done.w_ref, ...), custom_call_target="tpu_custom_call" | custom-call | tf_op jit(solution)/shard_map/expert/pallas_call | solution.py:251
  198.8 1.2 copy-done
  200.0 1.6 copy-done.1
  201.7 0.7 copy-done.7
  202.4 1.1 copy-done.15
  203.5 0.8 copy-done.17
  204.3 6.0 %all-to-all-start.1 = ((bf16[128,24,512]{2,1,0:T(8,128)(2,1)}), bf16[128,24,512]{2,1,0:T(8,128)(2,1)S(1)}, u32[]{:S(2)}, u32[]{:S(2)}) async-start(bf16[128,24,512]{2,1,0:T(8,128)(2,1)} %bitcast.23), calls=%async_computation.1 | async-start | bytes 6291456 | tf_op jit(solution)/shard_map/all_to_all | solution.py:198
  210.3 0.3 reduce-scatter.2.cloned.1.call-start
  210.6 0.0 copy-start.18
  210.6 2.6 convolution_convert_fusion.1
  213.2 1.9 convolution_convert_fusion
  215.1 2.5 pad_maximum_fusion
  217.6 0.0 reduce-scatter.2.cloned.1.call-update
  217.7 0.7 copy-done.12
  218.3 0.1 copy.13.gates_ref
  218.4 79.9 %reduce-scatter.2.cloned.1.call-done = bf16[512,1152]{0,1:T(8,128)(2,1)} async-done(((bf16[2048,1152]{0,1:T(8,128)(2,1)}), bf16[512,1152]{0,1:T(8,128)(2,1)}) %reduce-scatter.2.cloned.1.call-update) | async-done | bytes 1179664 | tf_op jit(solution)/shard_map/reduce_scatter | solution.py:283
  298.4 1.3 slice_bitcast_fusion.2
  299.7 1.2 maximum_bitcast_fusion
  300.8 2.4 copy.14
  303.2 53.0 %all-to-all-done.1 = bf16[128,24,512]{2,1,0:T(8,128)(2,1)S(1)} async-done(((bf16[128,24,512]{2,1,0:T(8,128)(2,1)}), bf16[128,24,512]{2,1,0:T(8,128)(2,1)S(1)}, u32[]{:S(2)}, u32[]{:S(2)}) %all-to-all-start.1) | async-done | bytes 3145760 | tf_op jit(solution)/shard_map/all_to_all | solution.py:198
  356.2 0.8 copy-done.9
  357.0 6.3 %finish.1 = (bf16[128,2048]{1,0:T(8,128)(2,1)}, bf16[128,2048]{1,0:T(8,128)(2,1)}) custom-call(bf16[8,384,512]{2,1,0:T(8,128)(2,1)S(1)} %bitcast.22, s32[128,2]{1,0:T(8,128)S(1)} %copy-done.9, f32[128,2]{1,0:T(8,128)S(1)} %copy.13.gates_ref, bf16[384,384]{1,0:T(8,128)(2,1)S(1)} %copy-done.2), custom_call_target="tpu_custom_call" | custom-call | tf_op jit(solution)/shard_map/finish/pallas_call | solution.py:288
  (18 shorter events, 0.0 us)
Async XLA Ops:
  8.7 1.0 copy-start.3
  9.7 1.0 copy-start.5
  10.7 1.0 copy-start.6
  11.7 0.7 copy-start.10
  12.4 0.7 copy-start.11
  13.1 0.7 copy-start.13
  18.2 0.6 copy-start.8
  18.8 20.2 %copy-start.19 = (bf16[1,3,512,384]{3,2,1,0:T(8,128)(2,1)S(1)}, bf16[1,3,512,384]{3,2,1,0:T(8,128)(2,1)}, u32[]{:S(2)}) copy-start(bf16[1,3,512,384]{3,2,1,0:T(8,128)(2,1)} %param.12) | copy-start | bytes 3538948
  18.8 25.6 %copy-start.14 = (s32[64]{0:T(128)S(1)}, s32[64]{0:T(128)}, u32[]{:S(2)}) copy-start(s32[64]{0:T(128)} %param.13) | copy-start | bytes 772
  18.8 166.2 %all-to-all-start = ((bf16[128,24,512]{2,1,0:T(8,128)(2,1)}), bf16[128,24,512]{2,1,0:T(8,128)(2,1)}, u32[]{:S(2)}, u32[]{:S(2)}) async-start(bf16[128,24,512]{2,1,0:T(8,128)(2,1)} %bitcast.4), calls=%async_computation | async-start | bytes 6291456 | tf_op jit(solution)/shard_map/all_to_all | solution.py:198
  38.9 100.1 %all-gather.2.cloned.1.call-start = ((), (), s32[]{:S(2)}) async-start(), calls=%async_computation.3 | async-start | bytes 5898240 | tf_op jit(solution)/shard_map/all_gather | solution.py:247
  39.0 38.4 %collective-permute-start = (bf16[3,512,384]{2,1,0:T(8,128)(2,1)S(1)}, bf16[3,512,384]{2,1,0:T(8,128)(2,1)S(1)}, u32[]{:S(2)}, u32[]{:S(2)}) collective-permute-start(bf16[3,512,384]{2,1,0:T(8,128)(2,1)S(1)} %bitcast.28), channel_id=1, source_target_pairs={{0,256},{4,260},{8,264},{12,268},{16,272},{20,276},{24,280},{28,28... | collective-permute-start | bytes 3538952 | tf_op jit(solution)/shard_map/ppermute | solution.py:245
  45.7 139.3 %copy-start.2 = (bf16[384,384]{1,0:T(8,128)(2,1)S(1)}, bf16[384,384]{1,0:T(8,128)(2,1)}, u32[]{:S(2)}) copy-start(bf16[384,384]{1,0:T(8,128)(2,1)} %constant.25.clone.unfold_ref) | copy-start | bytes 884740
  45.7 139.3 %copy-start.4 = (bf16[384,384]{1,0:T(8,128)(2,1)S(1)}, bf16[384,384]{1,0:T(8,128)(2,1)}, u32[]{:S(2)}) copy-start(bf16[384,384]{1,0:T(8,128)(2,1)} %constant.24.clone.fold_ref) | copy-start | bytes 884740
  198.8 1.2 copy-start
  200.0 1.6 copy-start.1
  201.6 0.7 copy-start.7
  202.4 1.1 copy-start.15
  203.5 0.8 copy-start.17
  204.3 151.9 %all-to-all-start.1 = ((bf16[128,24,512]{2,1,0:T(8,128)(2,1)}), bf16[128,24,512]{2,1,0:T(8,128)(2,1)S(1)}, u32[]{:S(2)}, u32[]{:S(2)}) async-start(bf16[128,24,512]{2,1,0:T(8,128)(2,1)} %bitcast.23), calls=%async_computation.1 | async-start | bytes 6291456 | tf_op jit(solution)/shard_map/all_to_all | solution.py:198
  210.3 88.0 %reduce-scatter.2.cloned.1.call-start = ((), (), s32[]{:S(2)}) async-start(), calls=%async_computation.4 | async-start | bytes 5898240 | tf_op jit(solution)/shard_map/reduce_scatter | solution.py:283
  210.6 2.6 copy-start.16
  210.6 2.6 copy-start.18
  217.6 0.7 copy-start.12
  356.2 0.8 copy-start.9
Sparse Core Ops, SparseCore 0:
  78.6 60.3 all-gather.1
  217.8 80.5 reduce-scatter.1

commit v3 on v2

v3 whole, which is shorter than its diff:
```python
import jax
import jax.numpy as jnp
import numpy as np
from jax import lax
from jax.experimental import pallas as pl
from jax.experimental.pallas import tpu as pltpu
from jax.sharding import PartitionSpec as P

CAP = 3
QUARTERS = 4
GROUP = 16
CHUNK = 2 * QUARTERS * CAP
BLOCK = GROUP * CHUNK
LANES = GROUP * CAP
MIB = 1 << 20
VMEM_MIB = 60
EXPERT_MIB = 53


def unfold_matrix():
    row = np.arange(BLOCK)
    array, quarter = row // (BLOCK // 2), (row // LANES) % QUARTERS
    peer, route = (row % LANES) // CAP, row % CAP
    source = peer * CHUNK + array * (CHUNK // 2) + quarter * CAP + route
    return (source[:, None] == row[None, :]).astype(np.float32)


def fold_block(block, first, second, fold):
    width = first.shape[1] // QUARTERS
    rows = slice(block * LANES, (block + 1) * LANES)
    parts = [
        ref[rows, q * width : (q + 1) * width] for ref in (first, second) for q in range(QUARTERS)
    ]
    stacked = jnp.concatenate(parts, axis=0)
    return jnp.dot(fold, stacked, preferred_element_type=jnp.float32).astype(jnp.bfloat16)


def unfold_block(block, chunks, unfold, first, second):
    width = chunks.shape[1]
    rows = slice(block * LANES, (block + 1) * LANES)
    opened = jnp.dot(unfold, chunks, preferred_element_type=jnp.float32).astype(jnp.bfloat16)
    for index, ref in enumerate((first, second)):
        for q in range(QUARTERS):
            start = (index * QUARTERS + q) * LANES
            ref[rows, q * width : (q + 1) * width] = opened[start : start + LANES]


def column(row):
    n = row.shape[1]
    same = lax.broadcasted_iota(jnp.int32, (n, n), 0) == lax.broadcasted_iota(jnp.int32, (n, n), 1)
    return jnp.sum(jnp.where(same, row, jnp.zeros_like(row)), axis=1, keepdims=True)


def start_all(copies):
    for copy in copies:
        copy.start()
    return copies


def prep_kernel(
    tok_hbm, cot_hbm, experts_hbm, gates_hbm, flags_hbm, fold_hbm,
    send_hbm, slots_hbm,
    tok_ref, cot_ref, experts_ref, gates_ref, flags_ref, fold_ref, slots_ref, x_ref, dy_ref, out_ref,
    in_sems, out_sems, slot_sem,
):
    tok_rows, feature_dim = tok_ref.shape
    half = flags_ref.shape[1]
    slot_count = x_ref.shape[0]
    pairs = [
        (experts_hbm, experts_ref), (flags_hbm, flags_ref), (gates_hbm, gates_ref),
        (tok_hbm, tok_ref), (cot_hbm, cot_ref), (fold_hbm, fold_ref),
    ]
    loads = start_all(
        [pltpu.make_async_copy(src, dst, in_sems.at[i]) for i, (src, dst) in enumerate(pairs)]
    )
    loads[0].wait()
    loads[1].wait()
    flags = column(flags_ref[...])
    trow = []
    for k in range(2):
        row = experts_ref[k : k + 1, :]
        sub = lax.broadcasted_iota(jnp.int32, (half, tok_rows), 0)
        mine = jnp.sum(jnp.where((row & (half - 1)) == sub, flags, 0), axis=0, keepdims=True)
        trow.append(row ^ (mine * half))
    tcol = [column(row) for row in trow]
    sub = lax.broadcasted_iota(jnp.int32, (tok_rows, tok_rows), 0)
    lane = lax.broadcasted_iota(jnp.int32, (tok_rows, tok_rows), 1)
    slots = []
    for k in range(2):
        rank = jnp.zeros((1, tok_rows), jnp.int32)
        for j in range(2):
            hit = (tcol[j] == trow[k]) & (sub * 2 + j < lane * 2 + k)
            rank += jnp.sum(jnp.where(hit, 1, 0), axis=0, keepdims=True)
        slots.append(trow[k] * CAP + rank)
        slots_ref[k : k + 1, :] = slots[k]
    keep = pltpu.make_async_copy(slots_ref, slots_hbm, slot_sem)
    keep.start()
    slot = lax.broadcasted_iota(jnp.int32, (slot_count, tok_rows), 0)
    hits = [slot == slots[k] for k in range(2)]
    loads[2].wait()
    gate = sum(
        jnp.sum(jnp.where(hits[k], gates_ref[k : k + 1, :], 0.0), axis=1, keepdims=True)
        for k in range(2)
    )
    placer = jnp.where(hits[0] | hits[1], 1.0, 0.0).astype(jnp.bfloat16)
    for copy in loads[3:]:
        copy.wait()
    width = feature_dim // QUARTERS
    for q in range(QUARTERS):
        cols = slice(q * width, (q + 1) * width)
        x = jnp.dot(placer, tok_ref[:, cols], preferred_element_type=jnp.float32)
        x_ref[:, cols] = x.astype(jnp.bfloat16)
        dy = jnp.dot(placer, cot_ref[:, cols], preferred_element_type=jnp.float32)
        dy_ref[:, cols] = (gate * dy).astype(jnp.bfloat16)
    fold = fold_ref[...]
    copies = [keep]
    for b in range(slot_count // LANES):
        out_ref[b] = fold_block(b, x_ref, dy_ref, fold)
        copies += start_all(
            [pltpu.make_async_copy(out_ref.at[b], send_hbm.at[b], out_sems.at[b])]
        )
    for copy in copies:
        copy.wait()


def expert_kernel(
    recv_hbm, ahead_hbm, back_hbm, unfold_hbm, fold_hbm,
    send_hbm, x_hbm, dy_hbm, hidden_hbm, paired_hbm,
    chunk_ref, ahead_ref, back_ref, unfold_ref, fold_ref,
    x_ref, dy_ref, hidden_ref, paired_ref, y_ref, dx_ref,
    recv_sems, load_sems, send_sems, keep_sems,
):
    blocks = chunk_ref.shape[0]
    feature_dim = x_ref.shape[1]
    units = hidden_ref.shape[1]
    pairs = [(unfold_hbm, unfold_ref), (fold_hbm, fold_ref)]
    pairs += [(ahead_hbm.at[i], ahead_ref.at[i]) for i in range(3)] + [(back_hbm, back_ref)]
    loads = [
        pltpu.make_async_copy(src, dst, load_sems.at[i]) for i, (src, dst) in enumerate(pairs)
    ]
    loads[0].start()
    arrivals = start_all(
        [
            pltpu.make_async_copy(recv_hbm.at[b], chunk_ref.at[b], recv_sems.at[b])
            for b in range(blocks)
        ]
    )
    start_all(loads[1:])
    loads[0].wait()
    unfold = unfold_ref[...]
    for b in range(blocks):
        arrivals[b].wait()
        unfold_block(b, chunk_ref[b], unfold, x_ref, dy_ref)
    copies = start_all(
        [
            pltpu.make_async_copy(x_ref, x_hbm, keep_sems.at[0]),
            pltpu.make_async_copy(dy_ref, dy_hbm, keep_sems.at[1]),
        ]
    )
    for copy in loads[1:]:
        copy.wait()
    pre_gate = jnp.dot(x_ref[...], ahead_ref[0], preferred_element_type=jnp.float32)
    pre_up = jnp.dot(x_ref[...], ahead_ref[1], preferred_element_type=jnp.float32)
    hidden_grad = jnp.dot(dy_ref[...], ahead_ref[2], preferred_element_type=jnp.float32)
    gate_sig = jax.nn.sigmoid(pre_gate)
    gate_act = pre_gate * gate_sig
    hidden_ref[...] = (gate_act * pre_up).astype(jnp.bfloat16)
    gate_pre = hidden_grad * pre_up * gate_sig * (1.0 + pre_gate * (1.0 - gate_sig))
    paired_ref[:, :units] = gate_pre.astype(jnp.bfloat16)
    paired_ref[:, units:] = (hidden_grad * gate_act).astype(jnp.bfloat16)
    copies += start_all(
        [
            pltpu.make_async_copy(hidden_ref, hidden_hbm, keep_sems.at[2]),
            pltpu.make_async_copy(paired_ref, paired_hbm, keep_sems.at[3]),
        ]
    )
    width = feature_dim // QUARTERS
    for q in range(QUARTERS):
        cols = slice(q * width, (q + 1) * width)
        y = jnp.dot(
            hidden_ref[...], back_ref[2 * units :, cols], preferred_element_type=jnp.float32
        )
        y_ref[:, cols] = y.astype(jnp.bfloat16)
        dx = jnp.dot(
            paired_ref[...], back_ref[: 2 * units, cols], preferred_element_type=jnp.float32
        )
        dx_ref[:, cols] = dx.astype(jnp.bfloat16)
    fold = fold_ref[...]
    for b in range(blocks):
        chunk_ref[b] = fold_block(b, y_ref, dx_ref, fold)
        copies += start_all(
            [pltpu.make_async_copy(chunk_ref.at[b], send_hbm.at[b], send_sems.at[b])]
        )
    for copy in copies:
        copy.wait()


def finish_kernel(
    recv_hbm, slots_hbm, gates_hbm, unfold_hbm,
    outputs_hbm, grads_hbm,
    chunk_ref, slots_ref, gates_ref, unfold_ref,
    y_ref, dx_ref, outputs_ref, grads_ref, recv_sems, load_sems, sems,
):
    blocks = chunk_ref.shape[0]
    pairs = [(slots_hbm, slots_ref), (gates_hbm, gates_ref), (unfold_hbm, unfold_ref)]
    loads = start_all(
        [pltpu.make_async_copy(src, dst, load_sems.at[i]) for i, (src, dst) in enumerate(pairs)]
    )
    arrivals = start_all(
        [
            pltpu.make_async_copy(recv_hbm.at[b], chunk_ref.at[b], recv_sems.at[b])
            for b in range(blocks)
        ]
    )
    for copy in loads:
        copy.wait()
    tok_rows, feature_dim = outputs_ref.shape
    slot_count = y_ref.shape[0]
    slot = lax.broadcasted_iota(jnp.int32, (tok_rows, slot_count), 1)
    hits = [slot == column(slots_ref[k : k + 1, :]) for k in range(2)]
    gates = [column(gates_ref[k : k + 1, :]) for k in range(2)]
    takers = [jnp.where(hit, 1.0, 0.0).astype(jnp.bfloat16) for hit in hits]
    both = jnp.where(hits[0] | hits[1], 1.0, 0.0).astype(jnp.bfloat16)
    unfold = unfold_ref[...]
    for b in range(blocks):
        arrivals[b].wait()
        unfold_block(b, chunk_ref[b], unfold, y_ref, dx_ref)
    width = feature_dim // QUARTERS
    copies = []
    for q in range(QUARTERS):
        cols = slice(q * width, (q + 1) * width)
        total = sum(
            gates[k] * jnp.dot(takers[k], y_ref[:, cols], preferred_element_type=jnp.float32)
            for k in range(2)
        )
        outputs_ref[:, cols] = total.astype(jnp.bfloat16)
        grad = jnp.dot(both, dx_ref[:, cols], preferred_element_type=jnp.float32)
        grads_ref[:, cols] = grad.astype(jnp.bfloat16)
        copies += start_all(
            [
                pltpu.make_async_copy(
                    outputs_ref.at[:, cols], outputs_hbm.at[:, cols], sems.at[2 * q]
                ),
                pltpu.make_async_copy(
                    grads_ref.at[:, cols], grads_hbm.at[:, cols], sems.at[2 * q + 1]
                ),
            ]
        )
    for copy in copies:
        copy.wait()


def exchange(chunks, ep_count):
    width = chunks.shape[-1]
    moved = lax.all_to_all(
        chunks.reshape(ep_count, CHUNK, width), "ep", split_axis=0, concat_axis=0, tiled=True
    )
    return moved.reshape(chunks.shape)


def body(tokens, cotangent, experts, gates, weights, swap_flags):
    ep_count = lax.axis_size("ep")
    half_ep = ep_count // 2
    tok_rows, feature_dim = tokens.shape
    slot_count = ep_count * CAP
    blocks = ep_count // GROUP
    units = weights.shape[3]
    width = feature_dim // QUARTERS
    my_index = lax.axis_index("ep")
    bf16 = jnp.bfloat16
    hbm = pl.BlockSpec(memory_space=pltpu.HBM)
    dma = pltpu.SemaphoreType.DMA
    unfold = unfold_matrix()
    fold = jnp.asarray(unfold.T, bf16)
    unfold = jnp.asarray(unfold, bf16)
    chunks_shape = jax.ShapeDtypeStruct((blocks, BLOCK, width), bf16)
    rows_shape = jax.ShapeDtypeStruct((slot_count, feature_dim), bf16)
    tok_shape = jax.ShapeDtypeStruct((tok_rows, feature_dim), bf16)
    hidden_shape = jax.ShapeDtypeStruct((slot_count, units), bf16)
    paired_shape = jax.ShapeDtypeStruct((slot_count, 2 * units), bf16)
    slots_shape = jax.ShapeDtypeStruct((2, tok_rows), jnp.int32)

    def scratch(shape):
        return pltpu.VMEM(shape.shape, shape.dtype)

    gate_rows = gates.T
    send, slots = pl.pallas_call(
        prep_kernel,
        out_shape=(chunks_shape, slots_shape),
        in_specs=[hbm] * 6,
        out_specs=(hbm, hbm),
        scratch_shapes=[
            scratch(tok_shape),
            scratch(tok_shape),
            scratch(slots_shape),
            pltpu.VMEM((2, tok_rows), jnp.float32),
            pltpu.VMEM((1, half_ep), jnp.int32),
            pltpu.VMEM((BLOCK, BLOCK), bf16),
            scratch(slots_shape),
            scratch(rows_shape),
            scratch(rows_shape),
            scratch(chunks_shape),
            dma((6,)),
            dma((blocks,)),
            dma,
        ],
        compiler_params=pltpu.CompilerParams(vmem_limit_bytes=VMEM_MIB * MIB),
        name="prep",
    )(tokens, cotangent, experts.T, gate_rows, swap_flags.reshape(1, half_ep), fold)

    pair_lanes = jnp.arange(half_ep, dtype=jnp.int32)
    my_flag = jnp.sum(jnp.where(pair_lanes == my_index % half_ep, swap_flags, 0)) > 0
    own_weights = weights[0]
    swap_pairs = [(source, source ^ half_ep) for source in range(ep_count)]
    partner = lax.ppermute(own_weights, "ep", swap_pairs)
    own_weights = jnp.where(my_flag, partner, own_weights)
    full_weights = lax.all_gather(own_weights, "dp", axis=1, tiled=True)
    back = full_weights.transpose(0, 2, 1).reshape(3 * units, feature_dim)

    recv = exchange(send, ep_count)

    send_back, rows_x, rows_dy, hidden, paired = pl.pallas_call(
        expert_kernel,
        out_shape=(chunks_shape, rows_shape, rows_shape, hidden_shape, paired_shape),
        in_specs=[hbm] * 5,
        out_specs=(hbm,) * 5,
        scratch_shapes=[
            scratch(chunks_shape),
            pltpu.VMEM((3, feature_dim, units), bf16),
            pltpu.VMEM((3 * units, feature_dim), bf16),
            pltpu.VMEM((BLOCK, BLOCK), bf16),
            pltpu.VMEM((BLOCK, BLOCK), bf16),
            scratch(rows_shape),
            scratch(rows_shape),
            scratch(hidden_shape),
            scratch(paired_shape),
            scratch(rows_shape),
            scratch(rows_shape),
            dma((blocks,)),
            dma((6,)),
            dma((blocks,)),
            dma((4,)),
        ],
        compiler_params=pltpu.CompilerParams(vmem_limit_bytes=EXPERT_MIB * MIB),
        name="expert",
    )(recv, full_weights, back, unfold, fold)

    recv_back = exchange(send_back, ep_count)

    pair_term = jnp.einsum("rc,rf->cf", rows_x, paired, preferred_element_type=jnp.float32)
    down_term = jnp.einsum("rd,rf->df", rows_dy, hidden, preferred_element_type=jnp.float32)
    terms = jnp.concatenate([pair_term.astype(bf16), down_term.astype(bf16)], axis=1)
    mine = lax.psum_scatter(terms, "dp", scatter_dimension=0, tiled=True)
    weight_grads = jnp.stack(
        [mine[:, :units], mine[:, units : 2 * units], mine[:, 2 * units :]]
    )[None]

    outputs, input_grads = pl.pallas_call(
        finish_kernel,
        out_shape=(tok_shape, tok_shape),
        in_specs=[hbm] * 4,
        out_specs=(hbm, hbm),
        scratch_shapes=[
            scratch(chunks_shape),
            scratch(slots_shape),
            pltpu.VMEM((2, tok_rows), jnp.float32),
            pltpu.VMEM((BLOCK, BLOCK), bf16),
            scratch(rows_shape),
            scratch(rows_shape),
            scratch(tok_shape),
            scratch(tok_shape),
            dma((blocks,)),
            dma((3,)),
            dma((2 * QUARTERS,)),
        ],
        compiler_params=pltpu.CompilerParams(vmem_limit_bytes=40 * MIB),
        name="finish",
    )(recv_back, slots, gate_rows, unfold)
    return (outputs, input_grads, weight_grads)


def solution(mesh):
    return jax.shard_map(
        body,
        mesh=mesh,
        in_specs=(
            P(("ep", "dp"), None),
            P(("ep", "dp"), None),
            P(("ep", "dp"), None),
            P(("ep", "dp"), None),
            P("ep", None, "dp", None),
            P(),
        ),
        out_specs=(P(("ep", "dp"), None), P(("ep", "dp"), None), P("ep", None, "dp", None)),
        check_vma=False,
    )
```

time: 371 us -> 357 us (0.962)
  local copies, waits for them, and re-layouts: 18 us -> 11.2 us
  waiting for transfers between devices: 271 us -> 265 us
    unnamed x43 -> x19, local copies, waits for them, and re-layouts: 16 us -> 3.14 us
    transpose x0 -> x1, local copies, waits for them, and re-layouts: none -> 6.78 us  [body(): back = full_weights.transpose(0, 2, 1).reshape(3 * units, feature_dim)]
    all_to_all x2, waiting for transfers between devices: 99 us -> 92.5 us  [exchange(): lax.all_to_all(chunks.reshape(ep_count, CHUNK, width), 'ep', split_axis=0...]
  transfers between devices with their start and end apart: 5 -> 5, of which waited for: 5 -> 5; matrix products, arithmetic and copies ran while one was open for 4% -> 6% of each run, Pallas kernels for 0% -> 0%
where the time goes in v3:
time: 357 us
  waiting for transfers between devices  265 us (74%)
  starting transfers between devices  31.6 us (9%)
  Pallas kernels  23.6 us (7%)
  between operations  14.9 us (4%)
  local copies, waits for them, and re-layouts  11.2 us (3%)
  other arithmetic  5.47 us (2%)
  matrix products  4.46 us (1%)
    all_to_all x2, waiting for transfers between devices, exchange(): lax.all_to_all(chunks.reshape(ep_count, CHUNK, width), 'ep', split_axis=0...  92.5 us
    reduce_scatter x1, waiting for transfers between devices, body(): mine = lax.psum_scatter(terms, 'dp', scatter_dimension=0, tiled=True)  80.6 us
    all_gather x1, waiting for transfers between devices, body(): full_weights = lax.all_gather(own_weights, 'dp', axis=1, tiled=True)  60.5 us
    ppermute x1, waiting for transfers between devices, body(): partner = lax.ppermute(own_weights, 'ep', swap_pairs)  31.9 us
    all_to_all x2, starting transfers between devices, exchange(): lax.all_to_all(chunks.reshape(ep_count, CHUNK, width), 'ep', split_axis=0...  26.3 us
    pallas_call x1, Pallas kernels, body(): pl.pallas_call(expert_kernel, out_shape=(chunks_shape, rows_shape, rows_s...  12.4 us
  transfers between devices with their start and end apart: 5, of which 5 were waited for; matrix products, arithmetic and copies ran while one was open for 6% of the time, Pallas kernels for 0%

profile of v3, /device:TPU:64, one launch (start us, length us, event | category | flops | bytes accessed | tf_op | source)
XLA Modules:
  0.0 356.6 jit_solution(16905829793025721410)
XLA Ops:
  7.2 4.8 %prep.1 = (bf16[8,384,512]{2,1,0:T(8,128)(2,1)}, s32[2,128]{1,0:T(2,128)}) custom-call(bf16[128,2048]{1,0:T(8,128)(2,1)} %tok_hbm.1, bf16[128,2048]{1,0:T(8,128)(2,1)} %cot_hbm.1, s32[2,128]{1,0:T(2,128)} %bitcast.31, f32[2,128]{1,0:T(2,128)} %bitcast.24, s32[1,64]{1,0:T(1,128)} %bitcast.32, bf16[384,384]{1,0:T(8,128)(2,1)} %constant.24.clone.fold_hbm), custom_call_target="tpu_custom_call" | custom-call | tf_op jit(solution)/shard_map/prep/pallas_call | solution.py:287
  12.0 0.0 copy-start.5
  12.0 0.0 copy-start.6
  12.0 20.1 %all-to-all-start = ((bf16[128,24,512]{2,1,0:T(8,128)(2,1)}), bf16[128,24,512]{2,1,0:T(8,128)(2,1)}, u32[]{:S(2)}, u32[]{:S(2)}) async-start(bf16[128,24,512]{2,1,0:T(8,128)(2,1)} %bitcast.28), calls=%async_computation | async-start | bytes 6291456 | tf_op jit(solution)/shard_map/all_to_all | solution.py:255
  32.1 0.0 all-gather.2.cloned.1.call-start
  32.2 0.0 copy-done.5
  32.2 5.2 %collective-permute-start = (bf16[3,512,384]{2,1,0:T(8,128)(2,1)S(1)}, bf16[3,512,384]{2,1,0:T(8,128)(2,1)S(1)}, u32[]{:S(2)}, u32[]{:S(2)}) collective-permute-start(bf16[3,512,384]{2,1,0:T(8,128)(2,1)S(1)} %bitcast.30), channel_id=1, source_target_pairs={{0,256},{4,260},{8,264},{12,268},{16,272},{20,276},{24,280},{28,28... | collective-permute-start | bytes 3538952 | tf_op jit(solution)/shard_map/ppermute | solution.py:315
  37.4 0.0 copy-done.6
  37.4 0.6 fusion
  38.7 31.9 %collective-permute-done = bf16[3,512,384]{2,1,0:T(8,128)(2,1)S(1)} collective-permute-done((bf16[3,512,384]{2,1,0:T(8,128)(2,1)S(1)}, bf16[3,512,384]{2,1,0:T(8,128)(2,1)S(1)}, u32[]{:S(2)}, u32[]{:S(2)}) %collective-permute-start) | collective-permute-done | bytes 1179680 | tf_op jit(solution)/shard_map/ppermute | solution.py:315
  70.6 1.2 broadcast_select_fusion
  71.7 0.0 all-gather.2.cloned.1.call-update
  71.8 60.5 %all-gather.2.cloned.1.call-done.ahead_hbm = bf16[3,2048,384]{2,1,0:T(8,128)(2,1)} async-done(((bf16[3,512,384]{2,1,0:T(8,128)(2,1)}), bf16[3,2048,384]{2,1,0:T(8,128)(2,1)}) %all-gather.2.cloned.1.call-update) | async-done | bytes 4718608 | tf_op jit(solution)/shard_map/all_gather | solution.py:317
  132.3 0.0 copy-start
  132.3 0.0 copy-start.1
  132.3 6.8 %copy.11 = bf16[3,384,2048]{2,1,0:T(8,128)(2,1)} copy(bf16[3,384,2048]{1,2,0:T(8,128)(2,1)} %bitcast.26) | data formatting | bytes 9437184 | tf_op jit(solution)/shard_map/transpose | solution.py:318
  139.0 39.2 %all-to-all-done = bf16[128,24,512]{2,1,0:T(8,128)(2,1)} async-done(((bf16[128,24,512]{2,1,0:T(8,128)(2,1)}), bf16[128,24,512]{2,1,0:T(8,128)(2,1)}, u32[]{:S(2)}, u32[]{:S(2)}) %all-to-all-start) | async-done | bytes 3145760 | tf_op jit(solution)/shard_map/all_to_all | solution.py:255
  178.2 0.0 copy-done
  178.2 0.0 copy-done.1
  178.2 12.4 %expert.1 = (bf16[8,384,512]{2,1,0:T(8,128)(2,1)}, bf16[384,2048]{1,0:T(8,128)(2,1)}, bf16[384,2048]{1,0:T(8,128)(2,1)}, bf16[384,384]{1,0:T(8,128)(2,1)S(1)}, bf16[384,768]{1,0:T(8,128)(2,1)}) custom-call(bf16[8,384,512]{2,1,0:T(8,128)(2,1)} %bitcast.4.recv_hbm, bf16[3,2048,384]{2,1,0:T(8,128)(2,1)} %all-gather.2.cloned.1.call-done.ahead_hbm, ...), custom_call_target="tpu_custom_call" | custom-call | tf_op jit(solution)/shard_map/expert/pallas_call | solution.py:322
  190.7 0.0 copy-start.2
  190.7 0.7 copy-done.2
  191.4 6.2 %all-to-all-start.1 = ((bf16[128,24,512]{2,1,0:T(8,128)(2,1)}), bf16[128,24,512]{2,1,0:T(8,128)(2,1)S(1)}, u32[]{:S(2)}, u32[]{:S(2)}) async-start(bf16[128,24,512]{2,1,0:T(8,128)(2,1)} %bitcast.29), calls=%async_computation.1 | async-start | bytes 6291456 | tf_op jit(solution)/shard_map/all_to_all | solution.py:255
  197.6 0.0 reduce-scatter.2.cloned.1.call-start
  197.6 0.0 copy-start.7
  197.6 0.0 copy-start.8
  197.7 2.6 convolution_convert_fusion.1
  200.3 0.0 copy-done.7
  200.3 0.0 copy-done.8
  200.3 1.9 convolution_convert_fusion
  202.1 2.5 pad_maximum_fusion
  204.6 0.0 reduce-scatter.2.cloned.1.call-update
  204.7 80.6 %reduce-scatter.2.cloned.1.call-done = bf16[512,1152]{0,1:T(8,128)(2,1)} async-done(((bf16[2048,1152]{0,1:T(8,128)(2,1)}), bf16[512,1152]{0,1:T(8,128)(2,1)}) %reduce-scatter.2.cloned.1.call-update) | async-done | bytes 1179664 | tf_op jit(solution)/shard_map/reduce_scatter | solution.py:353
  285.2 1.3 slice_bitcast_fusion.2
  286.5 1.2 maximum_bitcast_fusion
  287.7 0.0 copy-start.3
  287.7 0.0 copy-start.4
  287.7 2.4 copy.12
  290.1 53.3 %all-to-all-done.1 = bf16[128,24,512]{2,1,0:T(8,128)(2,1)S(1)} async-done(((bf16[128,24,512]{2,1,0:T(8,128)(2,1)}), bf16[128,24,512]{2,1,0:T(8,128)(2,1)S(1)}, u32[]{:S(2)}, u32[]{:S(2)}) %all-to-all-start.1) | async-done | bytes 3145760 | tf_op jit(solution)/shard_map/all_to_all | solution.py:255
  343.4 0.0 copy-done.3
  343.4 0.0 copy-done.4
  343.4 6.3 %finish.1 = (bf16[128,2048]{1,0:T(8,128)(2,1)}, bf16[128,2048]{1,0:T(8,128)(2,1)}) custom-call(bf16[8,384,512]{2,1,0:T(8,128)(2,1)S(1)} %bitcast.23, s32[2,128]{1,0:T(2,128)S(1)} %copy-done.4, f32[2,128]{1,0:T(2,128)S(1)} %bitcast.25, bf16[384,384]{1,0:T(8,128)(2,1)S(1)} %copy-done), custom_call_target="tpu_custom_call" | custom-call | tf_op jit(solution)/shard_map/finish/pallas_call | solution.py:358
Async XLA Ops:
  12.0 20.2 %copy-start.5 = (bf16[1,3,512,384]{3,2,1,0:T(8,128)(2,1)S(1)}, bf16[1,3,512,384]{3,2,1,0:T(8,128)(2,1)}, u32[]{:S(2)}) copy-start(bf16[1,3,512,384]{3,2,1,0:T(8,128)(2,1)} %param.12) | copy-start | bytes 3538948
  12.0 25.4 %copy-start.6 = (s32[64]{0:T(128)S(1)}, s32[64]{0:T(128)}, u32[]{:S(2)}) copy-start(s32[64]{0:T(128)} %param.13) | copy-start | bytes 772
  12.0 166.2 %all-to-all-start = ((bf16[128,24,512]{2,1,0:T(8,128)(2,1)}), bf16[128,24,512]{2,1,0:T(8,128)(2,1)}, u32[]{:S(2)}, u32[]{:S(2)}) async-start(bf16[128,24,512]{2,1,0:T(8,128)(2,1)} %bitcast.28), calls=%async_computation | async-start | bytes 6291456 | tf_op jit(solution)/shard_map/all_to_all | solution.py:255
  32.1 100.1 %all-gather.2.cloned.1.call-start = ((), (), s32[]{:S(2)}) async-start(), calls=%async_computation.3 | async-start | bytes 5898240 | tf_op jit(solution)/shard_map/all_gather | solution.py:317
  32.2 38.4 %collective-permute-start = (bf16[3,512,384]{2,1,0:T(8,128)(2,1)S(1)}, bf16[3,512,384]{2,1,0:T(8,128)(2,1)S(1)}, u32[]{:S(2)}, u32[]{:S(2)}) collective-permute-start(bf16[3,512,384]{2,1,0:T(8,128)(2,1)S(1)} %bitcast.30), channel_id=1, source_target_pairs={{0,256},{4,260},{8,264},{12,268},{16,272},{20,276},{24,280},{28,28... | collective-permute-start | bytes 3538952 | tf_op jit(solution)/shard_map/ppermute | solution.py:315
  132.3 46.0 %copy-start = (bf16[384,384]{1,0:T(8,128)(2,1)S(1)}, bf16[384,384]{1,0:T(8,128)(2,1)}, u32[]{:S(2)}) copy-start(bf16[384,384]{1,0:T(8,128)(2,1)} %constant.25.clone.unfold_hbm) | copy-start | bytes 884740
  132.3 46.0 %copy-start.1 = (bf16[384,384]{1,0:T(8,128)(2,1)S(1)}, bf16[384,384]{1,0:T(8,128)(2,1)}, u32[]{:S(2)}) copy-start(bf16[384,384]{1,0:T(8,128)(2,1)} %constant.24.clone.fold_hbm) | copy-start | bytes 884740
  190.7 0.7 copy-start.2
  191.4 152.0 %all-to-all-start.1 = ((bf16[128,24,512]{2,1,0:T(8,128)(2,1)}), bf16[128,24,512]{2,1,0:T(8,128)(2,1)S(1)}, u32[]{:S(2)}, u32[]{:S(2)}) async-start(bf16[128,24,512]{2,1,0:T(8,128)(2,1)} %bitcast.29), calls=%async_computation.1 | async-start | bytes 6291456 | tf_op jit(solution)/shard_map/all_to_all | solution.py:255
  197.6 87.6 %reduce-scatter.2.cloned.1.call-start = ((), (), s32[]{:S(2)}) async-start(), calls=%async_computation.4 | async-start | bytes 5898240 | tf_op jit(solution)/shard_map/reduce_scatter | solution.py:353
  197.6 2.6 copy-start.7
  197.6 2.6 copy-start.8
  287.7 55.7 %copy-start.3 = (f32[128,2]{0,1:T(2,128)S(1)}, f32[128,2]{0,1:T(2,128)}, u32[]{:S(2)}) copy-start(f32[128,2]{0,1:T(2,128)} %param.11) | copy-start | bytes 3076
  287.7 55.7 %copy-start.4 = (s32[2,128]{1,0:T(2,128)S(1)}, s32[2,128]{1,0:T(2,128)}, u32[]{:S(2)}) copy-start(s32[2,128]{1,0:T(2,128)} %get-tuple-element.14.slots_hbm) | copy-start | bytes 3076
Sparse Core Ops, SparseCore 0:
  71.9 60.3 all-gather.1
  204.8 80.4 reduce-scatter.1

commit v4 on v3

--- a/solution.py
+++ b/solution.py
@@ -133,8 +133,9 @@
     blocks = chunk_ref.shape[0]
     feature_dim = x_ref.shape[1]
     units = hidden_ref.shape[1]
-    pairs = [(unfold_hbm, unfold_ref), (fold_hbm, fold_ref)]
-    pairs += [(ahead_hbm.at[i], ahead_ref.at[i]) for i in range(3)] + [(back_hbm, back_ref)]
+    pairs = [(unfold_hbm, unfold_ref)]
+    pairs += [(ahead_hbm.at[i], ahead_ref.at[i]) for i in range(3)]
+    pairs += [(back_hbm, back_ref), (fold_hbm, fold_ref)]
     loads = [
         pltpu.make_async_copy(src, dst, load_sems.at[i]) for i, (src, dst) in enumerate(pairs)
     ]
@@ -151,13 +152,7 @@
     for b in range(blocks):
         arrivals[b].wait()
         unfold_block(b, chunk_ref[b], unfold, x_ref, dy_ref)
-    copies = start_all(
-        [
-            pltpu.make_async_copy(x_ref, x_hbm, keep_sems.at[0]),
-            pltpu.make_async_copy(dy_ref, dy_hbm, keep_sems.at[1]),
-        ]
-    )
-    for copy in loads[1:]:
+    for copy in loads[1:4]:
         copy.wait()
     pre_gate = jnp.dot(x_ref[...], ahead_ref[0], preferred_element_type=jnp.float32)
     pre_up = jnp.dot(x_ref[...], ahead_ref[1], preferred_element_type=jnp.float32)
@@ -168,8 +163,11 @@
     gate_pre = hidden_grad * pre_up * gate_sig * (1.0 + pre_gate * (1.0 - gate_sig))
     paired_ref[:, :units] = gate_pre.astype(jnp.bfloat16)
     paired_ref[:, units:] = (hidden_grad * gate_act).astype(jnp.bfloat16)
-    copies += start_all(
+    loads[4].wait()
+    copies = start_all(
         [
+            pltpu.make_async_copy(x_ref, x_hbm, keep_sems.at[0]),
+            pltpu.make_async_copy(dy_ref, dy_hbm, keep_sems.at[1]),
             pltpu.make_async_copy(hidden_ref, hidden_hbm, keep_sems.at[2]),
             pltpu.make_async_copy(paired_ref, paired_hbm, keep_sems.at[3]),
         ]
@@ -185,6 +183,7 @@
             paired_ref[...], back_ref[: 2 * units, cols], preferred_element_type=jnp.float32
         )
         dx_ref[:, cols] = dx.astype(jnp.bfloat16)
+    loads[5].wait()
     fold = fold_ref[...]
     for b in range(blocks):
         chunk_ref[b] = fold_block(b, y_ref, dx_ref, fold)
@@ -196,24 +195,11 @@
 
 
 def finish_kernel(
-    recv_hbm, slots_hbm, gates_hbm, unfold_hbm,
+    recv_ref, slots_ref, gates_ref, unfold_ref,
     outputs_hbm, grads_hbm,
-    chunk_ref, slots_ref, gates_ref, unfold_ref,
-    y_ref, dx_ref, outputs_ref, grads_ref, recv_sems, load_sems, sems,
+    y_ref, dx_ref, outputs_ref, grads_ref, sems,
 ):
-    blocks = chunk_ref.shape[0]
-    pairs = [(slots_hbm, slots_ref), (gates_hbm, gates_ref), (unfold_hbm, unfold_ref)]
-    loads = start_all(
-        [pltpu.make_async_copy(src, dst, load_sems.at[i]) for i, (src, dst) in enumerate(pairs)]
-    )
-    arrivals = start_all(
-        [
-            pltpu.make_async_copy(recv_hbm.at[b], chunk_ref.at[b], recv_sems.at[b])
-            for b in range(blocks)
-        ]
-    )
-    for copy in loads:
-        copy.wait()
+    blocks = recv_ref.shape[0]
     tok_rows, feature_dim = outputs_ref.shape
     slot_count = y_ref.shape[0]
     slot = lax.broadcasted_iota(jnp.int32, (tok_rows, slot_count), 1)
@@ -223,8 +209,7 @@
     both = jnp.where(hits[0] | hits[1], 1.0, 0.0).astype(jnp.bfloat16)
     unfold = unfold_ref[...]
     for b in range(blocks):
-        arrivals[b].wait()
-        unfold_block(b, chunk_ref[b], unfold, y_ref, dx_ref)
+        unfold_block(b, recv_ref[b], unfold, y_ref, dx_ref)
     width = feature_dim // QUARTERS
     copies = []
     for q in range(QUARTERS):
@@ -258,6 +243,11 @@
     return moved.reshape(chunks.shape)
 
 
+def dp_partner(value, mask):
+    pairs = [(source, source ^ mask) for source in range(lax.axis_size("dp"))]
+    return lax.ppermute(value, "dp", pairs)
+
+
 def body(tokens, cotangent, experts, gates, weights, swap_flags):
     ep_count = lax.axis_size("ep")
     half_ep = ep_count // 2
@@ -268,6 +258,7 @@
     width = feature_dim // QUARTERS
     my_index = lax.axis_index("ep")
     bf16 = jnp.bfloat16
+    vmem = pl.BlockSpec(memory_space=pltpu.VMEM)
     hbm = pl.BlockSpec(memory_space=pltpu.HBM)
     dma = pltpu.SemaphoreType.DMA
     unfold = unfold_matrix()
@@ -314,7 +305,14 @@
     swap_pairs = [(source, source ^ half_ep) for source in range(ep_count)]
     partner = lax.ppermute(own_weights, "ep", swap_pairs)
     own_weights = jnp.where(my_flag, partner, own_weights)
-    full_weights = lax.all_gather(own_weights, "dp", axis=1, tiled=True)
+    dp_count = lax.axis_size("dp")
+    my_dp = lax.axis_index("dp")
+    shard_rows = feature_dim // dp_count
+    full_weights = jnp.zeros((3, feature_dim, units), bf16)
+    for mask in range(dp_count):
+        shard = own_weights if mask == 0 else dp_partner(own_weights, mask)
+        start = (my_dp ^ mask) * shard_rows
+        full_weights = lax.dynamic_update_slice_in_dim(full_weights, shard, start, axis=1)
     back = full_weights.transpose(0, 2, 1).reshape(3 * units, feature_dim)
 
     recv = exchange(send, ep_count)
@@ -350,7 +348,12 @@
     pair_term = jnp.einsum("rc,rf->cf", rows_x, paired, preferred_element_type=jnp.float32)
     down_term = jnp.einsum("rd,rf->df", rows_dy, hidden, preferred_element_type=jnp.float32)
     terms = jnp.concatenate([pair_term.astype(bf16), down_term.astype(bf16)], axis=1)
-    mine = lax.psum_scatter(terms, "dp", scatter_dimension=0, tiled=True)
+    total = jnp.zeros((shard_rows, 3 * units), jnp.float32)
+    for mask in range(dp_count):
+        start = (my_dp ^ mask) * shard_rows
+        shard = lax.dynamic_slice_in_dim(terms, start, shard_rows, 0)
+        total += (shard if mask == 0 else dp_partner(shard, mask)).astype(jnp.float32)
+    mine = total.astype(bf16)
     weight_grads = jnp.stack(
         [mine[:, :units], mine[:, units : 2 * units], mine[:, 2 * units :]]
     )[None]
@@ -358,19 +361,13 @@
     outputs, input_grads = pl.pallas_call(
         finish_kernel,
         out_shape=(tok_shape, tok_shape),
-        in_specs=[hbm] * 4,
+        in_specs=[vmem] * 4,
         out_specs=(hbm, hbm),
         scratch_shapes=[
-            scratch(chunks_shape),
-            scratch(slots_shape),
-            pltpu.VMEM((2, tok_rows), jnp.float32),
-            pltpu.VMEM((BLOCK, BLOCK), bf16),
             scratch(rows_shape),
             scratch(rows_shape),
             scratch(tok_shape),
             scratch(tok_shape),
-            dma((blocks,)),
-            dma((3,)),
             dma((2 * QUARTERS,)),
         ],
         compiler_params=pltpu.CompilerParams(vmem_limit_bytes=40 * MIB),

time: 357 us -> 340 us (0.952)
  waiting for transfers between devices: 265 us -> 242 us
  starting transfers between devices: 31.6 us -> 49.9 us
  between operations: 14.9 us -> 1.71 us
  local copies, waits for them, and re-layouts: 11.2 us -> 17.3 us
  Pallas kernels: 23.6 us -> 19.9 us
    ppermute x0 -> x6, waiting for transfers between devices: none -> 126 us  [dp_partner(): return lax.ppermute(value, 'dp', pairs)]
    reduce_scatter x1 -> x0, waiting for transfers between devices: 80.6 us -> none  [body(): mine = lax.psum_scatter(terms, 'dp', scatter_dimension=0, tiled=True)]
    all_gather x1 -> x0, waiting for transfers between devices: 60.5 us -> none  [body(): full_weights = lax.all_gather(own_weights, 'dp', axis=1, tiled=True)]
    ppermute x0 -> x6, starting transfers between devices: none -> 18.6 us  [dp_partner(): return lax.ppermute(value, 'dp', pairs)]
    all_to_all x2, waiting for transfers between devices: 92.5 us -> 84.6 us  [exchange(): lax.all_to_all(chunks.reshape(ep_count, CHUNK, width), 'ep', split_axis=0...]
    dynamic_update_slice x0 -> x3, local copies, waits for them, and re-layouts: none -> 4.74 us  [body(): lax.dynamic_update_slice_in_dim(full_weights, shard, start, axis=1)]
  transfers between devices with their start and end apart: 5 -> 9, of which waited for: 5 -> 7; matrix products, arithmetic and copies ran while one was open for 6% -> 7% of each run, Pallas kernels for 0% -> 0%
where the time goes in v4:
time: 340 us
  waiting for transfers between devices  242 us (71%)
  starting transfers between devices  49.9 us (15%)
  Pallas kernels  19.9 us (6%)
  local copies, waits for them, and re-layouts  17.3 us (5%)
  matrix products  4.47 us (1%)
  other arithmetic  4.4 us (1%)
    ppermute x6, waiting for transfers between devices, dp_partner(): return lax.ppermute(value, 'dp', pairs)  126 us
    all_to_all x2, waiting for transfers between devices, exchange(): lax.all_to_all(chunks.reshape(ep_count, CHUNK, width), 'ep', split_axis=0...  84.6 us
    ppermute x1, waiting for transfers between devices, body(): partner = lax.ppermute(own_weights, 'ep', swap_pairs)  31.8 us
    all_to_all x2, starting transfers between devices, exchange(): lax.all_to_all(chunks.reshape(ep_count, CHUNK, width), 'ep', split_axis=0...  26.1 us
    ppermute x6, starting transfers between devices, dp_partner(): return lax.ppermute(value, 'dp', pairs)  18.6 us
    pallas_call x1, Pallas kernels, body(): pl.pallas_call(expert_kernel, out_shape=(chunks_shape, rows_shape, rows_s...  11.7 us
  transfers between devices with their start and end apart: 9, of which 7 were waited for; matrix products, arithmetic and copies ran while one was open for 7% of the time, Pallas kernels for 0%

profile of v4, /device:TPU:64, one launch (start us, length us, event | category | flops | bytes accessed | tf_op | source)
XLA Modules:
  0.0 339.6 jit_solution(1800323334567968273)
XLA Ops:
  0.6 4.8 %prep.1 = (bf16[8,384,512]{2,1,0:T(8,128)(2,1)}, s32[2,128]{1,0:T(2,128)}) custom-call(bf16[128,2048]{1,0:T(8,128)(2,1)} %tok_hbm.1, bf16[128,2048]{1,0:T(8,128)(2,1)} %cot_hbm.1, s32[2,128]{1,0:T(2,128)} %bitcast.31, f32[2,128]{1,0:T(2,128)} %bitcast.25, s32[1,64]{1,0:T(1,128)} %bitcast.32, bf16[384,384]{1,0:T(8,128)(2,1)} %constant.39.clone.fold_hbm), custom_call_target="tpu_custom_call" | custom-call | tf_op jit(solution)/shard_map/prep/pallas_call | solution.py:278
  5.5 0.0 copy-start.5
  5.5 0.0 copy-start.6
  5.5 20.1 %all-to-all-start = ((bf16[128,24,512]{2,1,0:T(8,128)(2,1)}), bf16[128,24,512]{2,1,0:T(8,128)(2,1)}, u32[]{:S(2)}, u32[]{:S(2)}) async-start(bf16[128,24,512]{2,1,0:T(8,128)(2,1)} %bitcast.28), calls=%async_computation | async-start | bytes 6291456 | tf_op jit(solution)/shard_map/all_to_all | solution.py:240
  25.6 0.0 copy-done.5
  25.6 5.2 %collective-permute-start = (bf16[3,512,384]{2,1,0:T(8,128)(2,1)S(1)}, bf16[3,512,384]{2,1,0:T(8,128)(2,1)S(1)}, u32[]{:S(2)}, u32[]{:S(2)}) collective-permute-start(bf16[3,512,384]{2,1,0:T(8,128)(2,1)S(1)} %bitcast.30), channel_id=1, source_target_pairs={{0,256},{4,260},{8,264},{12,268},{16,272},{20,276},{24,280},{28,28... | collective-permute-start | bytes 3538952 | tf_op jit(solution)/shard_map/ppermute | solution.py:306
  30.8 0.0 copy-done.6
  30.8 0.6 fusion.4
  32.1 31.8 %collective-permute-done = bf16[3,512,384]{2,1,0:T(8,128)(2,1)S(1)} collective-permute-done((bf16[3,512,384]{2,1,0:T(8,128)(2,1)S(1)}, bf16[3,512,384]{2,1,0:T(8,128)(2,1)S(1)}, u32[]{:S(2)}, u32[]{:S(2)}) %collective-permute-start) | collective-permute-done | bytes 1179680 | tf_op jit(solution)/shard_map/ppermute | solution.py:306
  64.0 2.6 broadcast_in_dim.10
  66.5 1.4 constant_dynamic-update-slice_fusion.3
  67.9 1.9 collective-permute-start.1
  69.8 4.8 %collective-permute-start.2 = (bf16[3,512,384]{2,1,0:T(8,128)(2,1)S(1)}, bf16[3,512,384]{2,1,0:T(8,128)(2,1)S(1)}, u32[]{:S(2)}, u32[]{:S(2)}) collective-permute-start(bf16[3,512,384]{2,1,0:T(8,128)(2,1)S(1)} %get-tuple-element.25), channel_id=1, source_target_pairs={{0,2},{1,3},{2,0},{3,1},{4,6},{5,7},{6,4},{7,5},{8,10},{9,11},{10,... | collective-permute-start | bytes 3538952 | tf_op jit(solution)/shard_map/ppermute | solution.py:248
  74.6 2.5 collective-permute-start.3
  77.2 0.0 collective-permute-done.1
  77.2 2.4 constant_dynamic-update-slice_fusion.2
  79.6 31.4 %collective-permute-done.2 = bf16[3,512,384]{2,1,0:T(8,128)(2,1)S(1)} collective-permute-done((bf16[3,512,384]{2,1,0:T(8,128)(2,1)S(1)}, bf16[3,512,384]{2,1,0:T(8,128)(2,1)S(1)}, u32[]{:S(2)}, u32[]{:S(2)}) %collective-permute-start.2) | collective-permute-done | bytes 1179680 | tf_op jit(solution)/shard_map/ppermute | solution.py:248
  111.0 1.2 constant_dynamic-update-slice_fusion.1
  112.2 30.0 %collective-permute-done.3 = bf16[3,512,384]{2,1,0:T(8,128)(2,1)S(1)} collective-permute-done((bf16[3,512,384]{2,1,0:T(8,128)(2,1)S(1)}, bf16[3,512,384]{2,1,0:T(8,128)(2,1)S(1)}, u32[]{:S(2)}, u32[]{:S(2)}) %collective-permute-start.3) | collective-permute-done | bytes 1179680 | tf_op jit(solution)/shard_map/ppermute | solution.py:248
  142.2 1.2 constant_dynamic-update-slice_fusion.ahead_hbm
  143.3 6.8 %copy.11 = bf16[3,384,2048]{2,1,0:T(8,128)(2,1)} copy(bf16[3,384,2048]{1,2,0:T(8,128)(2,1)} %bitcast.6) | data formatting | bytes 9437184 | tf_op jit(solution)/shard_map/transpose | solution.py:316
  150.1 21.6 %all-to-all-done = bf16[128,24,512]{2,1,0:T(8,128)(2,1)} async-done(((bf16[128,24,512]{2,1,0:T(8,128)(2,1)}), bf16[128,24,512]{2,1,0:T(8,128)(2,1)}, u32[]{:S(2)}, u32[]{:S(2)}) %all-to-all-start) | async-done | bytes 3145760 | tf_op jit(solution)/shard_map/all_to_all | solution.py:240
  171.7 0.0 copy-done
  171.7 0.0 copy-done.1
  171.7 11.7 %expert.1 = (bf16[8,384,512]{2,1,0:T(8,128)(2,1)}, bf16[384,2048]{1,0:T(8,128)(2,1)}, bf16[384,2048]{1,0:T(8,128)(2,1)}, bf16[384,384]{1,0:T(8,128)(2,1)S(1)}, bf16[384,768]{1,0:T(8,128)(2,1)}) custom-call(bf16[8,384,512]{2,1,0:T(8,128)(2,1)} %bitcast.4.recv_hbm, bf16[3,2048,384]{2,1,0:T(8,128)(2,1)} %constant_dynamic-update-slice_fusion.ahead_hbm, ...), custom_call_target="tpu_custom_call" | custom-call | tf_op jit(solution)/shard_map/expert/pallas_call | solution.py:320
  183.4 0.0 copy-start.2
  183.5 0.7 copy-done.2
  184.2 6.0 %all-to-all-start.1 = ((bf16[128,24,512]{2,1,0:T(8,128)(2,1)}), bf16[128,24,512]{2,1,0:T(8,128)(2,1)S(1)}, u32[]{:S(2)}, u32[]{:S(2)}) async-start(bf16[128,24,512]{2,1,0:T(8,128)(2,1)} %bitcast.29), calls=%async_computation.1 | async-start | bytes 6291456 | tf_op jit(solution)/shard_map/all_to_all | solution.py:240
  190.2 0.0 copy-start.7
  190.2 0.0 copy-start.8
  190.2 2.6 convolution_convert_fusion.1
  192.8 0.0 copy-done.7
  192.8 0.0 copy-done.8
  192.8 1.9 convolution_convert_fusion
  194.7 0.4 fusion.2
  195.1 1.9 collective-permute-start.4
  197.1 5.0 %collective-permute-start.5 = (bf16[512,1152]{0,1:T(8,128)(2,1)S(1)}, bf16[512,1152]{0,1:T(8,128)(2,1)S(1)}, u32[]{:S(2)}, u32[]{:S(2)}) collective-permute-start(bf16[512,1152]{0,1:T(8,128)(2,1)S(1)} %get-tuple-element.27), channel_id=1, source_target_pairs={{0,2},{1,3},{2,0},{3,1},{4,6},{5,7},{6,4},{7,5},{8,10},{9,11},{10,... | collective-permute-start | bytes 3538952 | tf_op jit(solution)/shard_map/ppermute | solution.py:248
  202.1 2.4 collective-permute-start.6
  204.5 0.0 collective-permute-done.4
  204.5 32.8 %collective-permute-done.5 = bf16[512,1152]{0,1:T(8,128)(2,1)S(1)} collective-permute-done((bf16[512,1152]{0,1:T(8,128)(2,1)S(1)}, bf16[512,1152]{0,1:T(8,128)(2,1)S(1)}, u32[]{:S(2)}, u32[]{:S(2)}) %collective-permute-start.5) | collective-permute-done | bytes 1179680 | tf_op jit(solution)/shard_map/ppermute | solution.py:248
  237.2 31.4 %collective-permute-done.6 = bf16[512,1152]{0,1:T(8,128)(2,1)S(1)} collective-permute-done((bf16[512,1152]{0,1:T(8,128)(2,1)S(1)}, bf16[512,1152]{0,1:T(8,128)(2,1)S(1)}, u32[]{:S(2)}, u32[]{:S(2)}) %collective-permute-start.6) | collective-permute-done | bytes 1179680 | tf_op jit(solution)/shard_map/ppermute | solution.py:248
  268.6 0.8 add_convert_fusion
  269.4 0.1 slice_bitcast_fusion.2
  269.5 1.2 maximum_bitcast_fusion
  270.7 2.4 copy.12
  273.1 63.0 %all-to-all-done.1 = bf16[128,24,512]{2,1,0:T(8,128)(2,1)S(1)} async-done(((bf16[128,24,512]{2,1,0:T(8,128)(2,1)}), bf16[128,24,512]{2,1,0:T(8,128)(2,1)S(1)}, u32[]{:S(2)}, u32[]{:S(2)}) %all-to-all-start.1) | async-done | bytes 3145760 | tf_op jit(solution)/shard_map/all_to_all | solution.py:240
  336.1 0.0 copy-done.3
  336.1 3.3 finish.1
  (5 shorter events, 0.0 us)
Async XLA Ops:
  5.5 20.1 %copy-start.5 = (bf16[1,3,512,384]{3,2,1,0:T(8,128)(2,1)S(1)}, bf16[1,3,512,384]{3,2,1,0:T(8,128)(2,1)}, u32[]{:S(2)}) copy-start(bf16[1,3,512,384]{3,2,1,0:T(8,128)(2,1)} %param.12) | copy-start | bytes 3538948
  5.5 25.4 %copy-start.6 = (s32[64]{0:T(128)S(1)}, s32[64]{0:T(128)}, u32[]{:S(2)}) copy-start(s32[64]{0:T(128)} %param.13) | copy-start | bytes 772
  5.5 166.2 %all-to-all-start = ((bf16[128,24,512]{2,1,0:T(8,128)(2,1)}), bf16[128,24,512]{2,1,0:T(8,128)(2,1)}, u32[]{:S(2)}, u32[]{:S(2)}) async-start(bf16[128,24,512]{2,1,0:T(8,128)(2,1)} %bitcast.28), calls=%async_computation | async-start | bytes 6291456 | tf_op jit(solution)/shard_map/all_to_all | solution.py:240
  25.6 38.3 %collective-permute-start = (bf16[3,512,384]{2,1,0:T(8,128)(2,1)S(1)}, bf16[3,512,384]{2,1,0:T(8,128)(2,1)S(1)}, u32[]{:S(2)}, u32[]{:S(2)}) collective-permute-start(bf16[3,512,384]{2,1,0:T(8,128)(2,1)S(1)} %bitcast.30), channel_id=1, source_target_pairs={{0,256},{4,260},{8,264},{12,268},{16,272},{20,276},{24,280},{28,28... | collective-permute-start | bytes 3538952 | tf_op jit(solution)/shard_map/ppermute | solution.py:306
  67.9 9.3 %collective-permute-start.1 = (bf16[3,512,384]{2,1,0:T(8,128)(2,1)S(1)}, bf16[3,512,384]{2,1,0:T(8,128)(2,1)}, u32[]{:S(2)}, u32[]{:S(2)}) collective-permute-start(bf16[3,512,384]{2,1,0:T(8,128)(2,1)S(1)} %get-tuple-element.25), channel_id=1, source_target_pairs={{0,1},{1,0},{2,3},{3,2},{4,5},{5,4},{6,7},{7,6},{8,9},{9,8},{10,11... | collective-permute-start | bytes 3538952 | tf_op jit(solution)/shard_map/ppermute | solution.py:248
  69.8 41.2 %collective-permute-start.2 = (bf16[3,512,384]{2,1,0:T(8,128)(2,1)S(1)}, bf16[3,512,384]{2,1,0:T(8,128)(2,1)S(1)}, u32[]{:S(2)}, u32[]{:S(2)}) collective-permute-start(bf16[3,512,384]{2,1,0:T(8,128)(2,1)S(1)} %get-tuple-element.25), channel_id=1, source_target_pairs={{0,2},{1,3},{2,0},{3,1},{4,6},{5,7},{6,4},{7,5},{8,10},{9,11},{10,... | collective-permute-start | bytes 3538952 | tf_op jit(solution)/shard_map/ppermute | solution.py:248
  74.6 67.5 %collective-permute-start.3 = (bf16[3,512,384]{2,1,0:T(8,128)(2,1)S(1)}, bf16[3,512,384]{2,1,0:T(8,128)(2,1)S(1)}, u32[]{:S(2)}, u32[]{:S(2)}) collective-permute-start(bf16[3,512,384]{2,1,0:T(8,128)(2,1)S(1)} %get-tuple-element.25), channel_id=1, source_target_pairs={{0,3},{1,2},{2,1},{3,0},{4,7},{5,6},{6,5},{7,4},{8,11},{9,10},{10,... | collective-permute-start | bytes 3538952 | tf_op jit(solution)/shard_map/ppermute | solution.py:248
  143.3 28.4 %copy-start = (bf16[384,384]{1,0:T(8,128)(2,1)S(1)}, bf16[384,384]{1,0:T(8,128)(2,1)}, u32[]{:S(2)}) copy-start(bf16[384,384]{1,0:T(8,128)(2,1)} %constant.40.clone.unfold_hbm.unfold_ref) | copy-start | bytes 884740
  143.3 28.4 %copy-start.1 = (bf16[384,384]{1,0:T(8,128)(2,1)S(1)}, bf16[384,384]{1,0:T(8,128)(2,1)}, u32[]{:S(2)}) copy-start(bf16[384,384]{1,0:T(8,128)(2,1)} %constant.39.clone.fold_hbm) | copy-start | bytes 884740
  183.4 0.7 copy-start.2
  184.2 151.9 %all-to-all-start.1 = ((bf16[128,24,512]{2,1,0:T(8,128)(2,1)}), bf16[128,24,512]{2,1,0:T(8,128)(2,1)S(1)}, u32[]{:S(2)}, u32[]{:S(2)}) async-start(bf16[128,24,512]{2,1,0:T(8,128)(2,1)} %bitcast.29), calls=%async_computation.1 | async-start | bytes 6291456 | tf_op jit(solution)/shard_map/all_to_all | solution.py:240
  190.2 2.6 copy-start.7
  190.2 2.6 copy-start.8
  195.1 9.3 %collective-permute-start.4 = (bf16[512,1152]{0,1:T(8,128)(2,1)S(1)}, bf16[512,1152]{0,1:T(8,128)(2,1)S(1)}, u32[]{:S(2)}, u32[]{:S(2)}) collective-permute-start(bf16[512,1152]{0,1:T(8,128)(2,1)S(1)} %get-tuple-element.26), channel_id=1, source_target_pairs={{0,1},{1,0},{2,3},{3,2},{4,5},{5,4},{6,7},{7,6},{8,9},{9,8},{10,11... | collective-permute-start | bytes 3538952 | tf_op jit(solution)/shard_map/ppermute | solution.py:248
  197.1 40.2 %collective-permute-start.5 = (bf16[512,1152]{0,1:T(8,128)(2,1)S(1)}, bf16[512,1152]{0,1:T(8,128)(2,1)S(1)}, u32[]{:S(2)}, u32[]{:S(2)}) collective-permute-start(bf16[512,1152]{0,1:T(8,128)(2,1)S(1)} %get-tuple-element.27), channel_id=1, source_target_pairs={{0,2},{1,3},{2,0},{3,1},{4,6},{5,7},{6,4},{7,5},{8,10},{9,11},{10,... | collective-permute-start | bytes 3538952 | tf_op jit(solution)/shard_map/ppermute | solution.py:248
  202.1 66.5 %collective-permute-start.6 = (bf16[512,1152]{0,1:T(8,128)(2,1)S(1)}, bf16[512,1152]{0,1:T(8,128)(2,1)S(1)}, u32[]{:S(2)}, u32[]{:S(2)}) collective-permute-start(bf16[512,1152]{0,1:T(8,128)(2,1)S(1)} %get-tuple-element.28), channel_id=1, source_target_pairs={{0,3},{1,2},{2,1},{3,0},{4,7},{5,6},{6,5},{7,4},{8,11},{9,10},{10,... | collective-permute-start | bytes 3538952 | tf_op jit(solution)/shard_map/ppermute | solution.py:248
  270.7 65.4 %copy-start.3 = (f32[128,2]{0,1:T(2,128)S(1)}, f32[128,2]{0,1:T(2,128)}, u32[]{:S(2)}) copy-start(f32[128,2]{0,1:T(2,128)} %param.11) | copy-start | bytes 3076
  270.7 65.4 %copy-start.4 = (s32[2,128]{1,0:T(2,128)S(1)}, s32[2,128]{1,0:T(2,128)}, u32[]{:S(2)}) copy-start(s32[2,128]{1,0:T(2,128)} %get-tuple-element.14.slots_ref) | copy-start | bytes 3076

commit v5 on v4

--- a/solution.py
+++ b/solution.py
@@ -9,40 +9,54 @@
 CAP = 3
 QUARTERS = 4
 GROUP = 16
+HALF = GROUP // 2
 CHUNK = 2 * QUARTERS * CAP
 BLOCK = GROUP * CHUNK
 LANES = GROUP * CAP
 MIB = 1 << 20
 VMEM_MIB = 60
-EXPERT_MIB = 53
+EXPERT_MIB = 107
 
 
 def unfold_matrix():
-    row = np.arange(BLOCK)
-    array, quarter = row // (BLOCK // 2), (row // LANES) % QUARTERS
-    peer, route = (row % LANES) // CAP, row % CAP
+    row = np.arange(HALF * CHUNK)
+    piece, within = row // (HALF * CAP), row % (HALF * CAP)
+    array, quarter = piece // QUARTERS, piece % QUARTERS
+    peer, route = within // CAP, within % CAP
     source = peer * CHUNK + array * (CHUNK // 2) + quarter * CAP + route
     return (source[:, None] == row[None, :]).astype(np.float32)
 
 
 def fold_block(block, first, second, fold):
     width = first.shape[1] // QUARTERS
-    rows = slice(block * LANES, (block + 1) * LANES)
-    parts = [
-        ref[rows, q * width : (q + 1) * width] for ref in (first, second) for q in range(QUARTERS)
-    ]
-    stacked = jnp.concatenate(parts, axis=0)
-    return jnp.dot(fold, stacked, preferred_element_type=jnp.float32).astype(jnp.bfloat16)
+    piece = HALF * CAP
+    halves = []
+    for start in (block * LANES, block * LANES + piece):
+        parts = [
+            ref[start : start + piece, q * width : (q + 1) * width]
+            for ref in (first, second)
+            for q in range(QUARTERS)
+        ]
+        stacked = jnp.concatenate(parts, axis=0).astype(jnp.bfloat16)
+        folded = jnp.dot(fold, stacked, preferred_element_type=jnp.float32)
+        halves.append(folded.astype(jnp.bfloat16))
+    return jnp.concatenate(halves, axis=0)
 
 
 def unfold_block(block, chunks, unfold, first, second):
     width = chunks.shape[1]
+    piece = HALF * CAP
     rows = slice(block * LANES, (block + 1) * LANES)
-    opened = jnp.dot(unfold, chunks, preferred_element_type=jnp.float32).astype(jnp.bfloat16)
+    half = chunks.shape[0] // 2
+    opened = [
+        jnp.dot(unfold, part, preferred_element_type=jnp.float32)
+        for part in (chunks[:half], chunks[half:])
+    ]
     for index, ref in enumerate((first, second)):
         for q in range(QUARTERS):
-            start = (index * QUARTERS + q) * LANES
-            ref[rows, q * width : (q + 1) * width] = opened[start : start + LANES]
+            start = (index * QUARTERS + q) * piece
+            both = jnp.concatenate([part[start : start + piece] for part in opened], axis=0)
+            ref[rows, q * width : (q + 1) * width] = both.astype(jnp.bfloat16)
 
 
 def column(row):
@@ -109,9 +123,9 @@
     for q in range(QUARTERS):
         cols = slice(q * width, (q + 1) * width)
         x = jnp.dot(placer, tok_ref[:, cols], preferred_element_type=jnp.float32)
-        x_ref[:, cols] = x.astype(jnp.bfloat16)
+        x_ref[:, cols] = x
         dy = jnp.dot(placer, cot_ref[:, cols], preferred_element_type=jnp.float32)
-        dy_ref[:, cols] = (gate * dy).astype(jnp.bfloat16)
+        dy_ref[:, cols] = gate * dy
     fold = fold_ref[...]
     copies = [keep]
     for b in range(slot_count // LANES):
@@ -178,11 +192,11 @@
         y = jnp.dot(
             hidden_ref[...], back_ref[2 * units :, cols], preferred_element_type=jnp.float32
         )
-        y_ref[:, cols] = y.astype(jnp.bfloat16)
+        y_ref[:, cols] = y
         dx = jnp.dot(
             paired_ref[...], back_ref[: 2 * units, cols], preferred_element_type=jnp.float32
         )
-        dx_ref[:, cols] = dx.astype(jnp.bfloat16)
+        dx_ref[:, cols] = dx
     loads[5].wait()
     fold = fold_ref[...]
     for b in range(blocks):
@@ -271,6 +285,9 @@
     paired_shape = jax.ShapeDtypeStruct((slot_count, 2 * units), bf16)
     slots_shape = jax.ShapeDtypeStruct((2, tok_rows), jnp.int32)
 
+    wide_vmem = pltpu.VMEM(rows_shape.shape, jnp.float32)
+    fold_vmem = pltpu.VMEM(fold.shape, bf16)
+
     def scratch(shape):
         return pltpu.VMEM(shape.shape, shape.dtype)
 
@@ -286,10 +303,10 @@
             scratch(slots_shape),
             pltpu.VMEM((2, tok_rows), jnp.float32),
             pltpu.VMEM((1, half_ep), jnp.int32),
-            pltpu.VMEM((BLOCK, BLOCK), bf16),
+            fold_vmem,
             scratch(slots_shape),
-            scratch(rows_shape),
-            scratch(rows_shape),
+            wide_vmem,
+            wide_vmem,
             scratch(chunks_shape),
             dma((6,)),
             dma((blocks,)),
@@ -326,20 +343,20 @@
             scratch(chunks_shape),
             pltpu.VMEM((3, feature_dim, units), bf16),
             pltpu.VMEM((3 * units, feature_dim), bf16),
-            pltpu.VMEM((BLOCK, BLOCK), bf16),
-            pltpu.VMEM((BLOCK, BLOCK), bf16),
+            fold_vmem,
+            fold_vmem,
             scratch(rows_shape),
             scratch(rows_shape),
             scratch(hidden_shape),
             scratch(paired_shape),
-            scratch(rows_shape),
-            scratch(rows_shape),
+            wide_vmem,
+            wide_vmem,
             dma((blocks,)),
             dma((6,)),
             dma((blocks,)),
             dma((4,)),
         ],
-        compiler_params=pltpu.CompilerParams(vmem_limit_bytes=EXPERT_MIB * MIB),
+        compiler_params=pltpu.CompilerParams(vmem_limit_bytes=EXPERT_MIB * (MIB // 2)),
         name="expert",
     )(recv, full_weights, back, unfold, fold)
 

time: 340 us -> 339 us (level)
  local copies, waits for them, and re-layouts: 17.3 us -> 20.8 us
  transfers between devices with their start and end apart: 9 -> 9, of which waited for: 7 -> 7; matrix products, arithmetic and copies ran while one was open for 7% -> 8% of each run, Pallas kernels for 0% -> 0%
where the time goes in v5:
time: 339 us; the launch traced here: 338 us
  waiting for transfers between devices  240 us (71%)
  starting transfers between devices  49.1 us (14%)
  local copies, waits for them, and re-layouts  20.8 us (6%)
  Pallas kernels  17.4 us (5%)
  other arithmetic  4.79 us (1%)
  matrix products  4.44 us (1%)
    ppermute x6, waiting for transfers between devices, dp_partner(): return lax.ppermute(value, 'dp', pairs)  125 us
    all_to_all x2, waiting for transfers between devices, exchange(): lax.all_to_all(chunks.reshape(ep_count, CHUNK, width), 'ep', split_axis=0...  82.9 us
    ppermute x1, waiting for transfers between devices, body(): partner = lax.ppermute(own_weights, 'ep', swap_pairs)  32 us
    all_to_all x2, starting transfers between devices, exchange(): lax.all_to_all(chunks.reshape(ep_count, CHUNK, width), 'ep', split_axis=0...  25.8 us
    ppermute x6, starting transfers between devices, dp_partner(): return lax.ppermute(value, 'dp', pairs)  18.2 us
    pallas_call x1, Pallas kernels, body(): pl.pallas_call(expert_kernel, out_shape=(chunks_shape, rows_shape, rows_s...  10.7 us
    dynamic_update_slice x3, local copies, waits for them, and re-layouts, body(): lax.dynamic_update_slice_in_dim(full_weights, shard, start, axis=1)  7.29 us
    transpose x1, local copies, waits for them, and re-layouts, body(): back = full_weights.transpose(0, 2, 1).reshape(3 * units, feature_dim)  6.78 us
  transfers between devices with their start and end apart: 9, of which 7 were waited for; matrix products, arithmetic and copies ran while one was open for 8% of the time, Pallas kernels for 0%

profile of v5, /device:TPU:64, one launch (start us, length us, event | category | flops | bytes accessed | tf_op | source)
XLA Modules:
  0.0 338.0 jit_solution(513538911297304122)
XLA Ops:
  0.6 4.2 %prep.1 = (bf16[8,384,512]{2,1,0:T(8,128)(2,1)}, s32[2,128]{1,0:T(2,128)}) custom-call(bf16[128,2048]{1,0:T(8,128)(2,1)} %tok_hbm.1, bf16[128,2048]{1,0:T(8,128)(2,1)} %cot_hbm.1, s32[2,128]{1,0:T(2,128)} %bitcast.32, f32[2,128]{1,0:T(2,128)} %bitcast.25, s32[1,64]{1,0:T(1,128)} %bitcast.33, bf16[192,192]{1,0:T(8,128)(2,1)} %constant.37.clone.fold_hbm.unfold_hbm.unfold_ref), custom_call_target="tpu_custom_call" | custom-call | tf_op jit(solution)/shard_map/prep/pallas_call | solution.py:295
  4.8 0.0 copy-start.5
  4.8 19.6 %all-to-all-start = ((bf16[128,24,512]{2,1,0:T(8,128)(2,1)}), bf16[128,24,512]{2,1,0:T(8,128)(2,1)S(1)}, u32[]{:S(2)}, u32[]{:S(2)}) async-start(bf16[128,24,512]{2,1,0:T(8,128)(2,1)} %bitcast.29), calls=%async_computation | async-start | bytes 6291456 | tf_op jit(solution)/shard_map/all_to_all | solution.py:254
  24.4 5.2 %collective-permute-start = (bf16[3,512,384]{2,1,0:T(8,128)(2,1)}, bf16[3,512,384]{2,1,0:T(8,128)(2,1)}, u32[]{:S(2)}, u32[]{:S(2)}) collective-permute-start(bf16[3,512,384]{2,1,0:T(8,128)(2,1)} %bitcast.31), channel_id=1, source_target_pairs={{0,256},{4,260},{8,264},{12,268},{16,272},{20,276},{24,280},{28,28... | collective-permute-start | bytes 3538952 | tf_op jit(solution)/shard_map/ppermute | solution.py:323
  29.6 0.0 copy-done.5
  29.6 0.6 fusion.4
  30.9 0.0 copy-start.4
  30.9 32.0 %collective-permute-done = bf16[3,512,384]{2,1,0:T(8,128)(2,1)} collective-permute-done((bf16[3,512,384]{2,1,0:T(8,128)(2,1)}, bf16[3,512,384]{2,1,0:T(8,128)(2,1)}, u32[]{:S(2)}, u32[]{:S(2)}) %collective-permute-start) | collective-permute-done | bytes 1179680 | tf_op jit(solution)/shard_map/ppermute | solution.py:323
  62.9 2.6 broadcast_in_dim.10
  65.5 0.0 copy-done.4
  65.5 1.7 constant_dynamic-update-slice_fusion.3
  67.3 1.9 collective-permute-start.1
  69.2 4.8 %collective-permute-start.2 = (bf16[3,512,384]{2,1,0:T(8,128)(2,1)}, bf16[3,512,384]{2,1,0:T(8,128)(2,1)}, u32[]{:S(2)}, u32[]{:S(2)}) collective-permute-start(bf16[3,512,384]{2,1,0:T(8,128)(2,1)} %get-tuple-element.25), channel_id=1, source_target_pairs={{0,2},{1,3},{2,0},{3,1},{4,6},{5,7},{6,4},{7,5},{8,10},{9,11},{10,... | collective-permute-start | bytes 3538952 | tf_op jit(solution)/shard_map/ppermute | solution.py:262
  74.0 2.4 collective-permute-start.3
  76.4 0.0 collective-permute-done.1
  76.4 2.4 constant_dynamic-update-slice_fusion.2
  78.8 32.1 %collective-permute-done.2 = bf16[3,512,384]{2,1,0:T(8,128)(2,1)} collective-permute-done((bf16[3,512,384]{2,1,0:T(8,128)(2,1)}, bf16[3,512,384]{2,1,0:T(8,128)(2,1)}, u32[]{:S(2)}, u32[]{:S(2)}) %collective-permute-start.2) | collective-permute-done | bytes 1179680 | tf_op jit(solution)/shard_map/ppermute | solution.py:262
  110.9 2.4 constant_dynamic-update-slice_fusion.1
  113.3 28.5 %collective-permute-done.3 = bf16[3,512,384]{2,1,0:T(8,128)(2,1)} collective-permute-done((bf16[3,512,384]{2,1,0:T(8,128)(2,1)}, bf16[3,512,384]{2,1,0:T(8,128)(2,1)}, u32[]{:S(2)}, u32[]{:S(2)}) %collective-permute-start.3) | collective-permute-done | bytes 1179680 | tf_op jit(solution)/shard_map/ppermute | solution.py:262
  141.8 2.4 constant_dynamic-update-slice_fusion.ahead_hbm
  144.3 0.0 copy-start
  144.3 6.8 %copy.11 = bf16[3,384,2048]{2,1,0:T(8,128)(2,1)} copy(bf16[3,384,2048]{1,2,0:T(8,128)(2,1)} %bitcast.6) | data formatting | bytes 9437184 | tf_op jit(solution)/shard_map/transpose | solution.py:333
  151.1 19.7 %all-to-all-done = bf16[128,24,512]{2,1,0:T(8,128)(2,1)S(1)} async-done(((bf16[128,24,512]{2,1,0:T(8,128)(2,1)}), bf16[128,24,512]{2,1,0:T(8,128)(2,1)S(1)}, u32[]{:S(2)}, u32[]{:S(2)}) %all-to-all-start) | async-done | bytes 3145760 | tf_op jit(solution)/shard_map/all_to_all | solution.py:254
  170.8 1.6 copy-done.3
  172.4 0.0 copy-done
  172.4 10.7 %expert.1 = (bf16[8,384,512]{2,1,0:T(8,128)(2,1)}, bf16[384,2048]{1,0:T(8,128)(2,1)}, bf16[384,2048]{1,0:T(8,128)(2,1)}, bf16[384,384]{1,0:T(8,128)(2,1)S(1)}, bf16[384,768]{1,0:T(8,128)(2,1)}) custom-call(bf16[8,384,512]{2,1,0:T(8,128)(2,1)} %bitcast.28, bf16[3,2048,384]{2,1,0:T(8,128)(2,1)} %constant_dynamic-update-slice_fusion.ahead_hbm, ...), custom_call_target="tpu_custom_call" | custom-call | tf_op jit(solution)/shard_map/expert/pallas_call | solution.py:337
  183.1 6.2 %all-to-all-start.1 = ((bf16[128,24,512]{2,1,0:T(8,128)(2,1)}), bf16[128,24,512]{2,1,0:T(8,128)(2,1)S(1)}, u32[]{:S(2)}, u32[]{:S(2)}) async-start(bf16[128,24,512]{2,1,0:T(8,128)(2,1)} %bitcast.30), calls=%async_computation.1 | async-start | bytes 6291456 | tf_op jit(solution)/shard_map/all_to_all | solution.py:254
  189.3 0.0 copy-start.6
  189.3 0.0 copy-start.7
  189.3 2.6 convolution_convert_fusion.1
  191.9 0.0 copy-done.6
  191.9 0.0 copy-done.7
  191.9 1.9 convolution_convert_fusion
  193.8 0.4 fusion.2
  194.2 1.9 collective-permute-start.4
  196.2 4.8 %collective-permute-start.5 = (bf16[512,1152]{0,1:T(8,128)(2,1)S(1)}, bf16[512,1152]{0,1:T(8,128)(2,1)S(1)}, u32[]{:S(2)}, u32[]{:S(2)}) collective-permute-start(bf16[512,1152]{0,1:T(8,128)(2,1)S(1)} %get-tuple-element.27), channel_id=1, source_target_pairs={{0,2},{1,3},{2,0},{3,1},{4,6},{5,7},{6,4},{7,5},{8,10},{9,11},{10,... | collective-permute-start | bytes 3538952 | tf_op jit(solution)/shard_map/ppermute | solution.py:262
  201.0 2.4 collective-permute-start.6
  203.4 0.0 collective-permute-done.4
  203.4 32.7 %collective-permute-done.5 = bf16[512,1152]{0,1:T(8,128)(2,1)S(1)} collective-permute-done((bf16[512,1152]{0,1:T(8,128)(2,1)S(1)}, bf16[512,1152]{0,1:T(8,128)(2,1)S(1)}, u32[]{:S(2)}, u32[]{:S(2)}) %collective-permute-start.5) | collective-permute-done | bytes 1179680 | tf_op jit(solution)/shard_map/ppermute | solution.py:262
  236.1 31.5 %collective-permute-done.6 = bf16[512,1152]{0,1:T(8,128)(2,1)S(1)} collective-permute-done((bf16[512,1152]{0,1:T(8,128)(2,1)S(1)}, bf16[512,1152]{0,1:T(8,128)(2,1)S(1)}, u32[]{:S(2)}, u32[]{:S(2)}) %collective-permute-start.6) | collective-permute-done | bytes 1179680 | tf_op jit(solution)/shard_map/ppermute | solution.py:262
  267.5 0.8 add_convert_fusion
  268.4 0.1 slice_bitcast_fusion.2
  268.4 1.2 maximum_bitcast_fusion
  269.6 2.4 copy.12
  272.0 63.2 %all-to-all-done.1 = bf16[128,24,512]{2,1,0:T(8,128)(2,1)S(1)} async-done(((bf16[128,24,512]{2,1,0:T(8,128)(2,1)}), bf16[128,24,512]{2,1,0:T(8,128)(2,1)S(1)}, u32[]{:S(2)}, u32[]{:S(2)}) %all-to-all-start.1) | async-done | bytes 3145760 | tf_op jit(solution)/shard_map/all_to_all | solution.py:254
  335.2 0.0 copy-done.1
  335.2 0.0 copy-done.2
  335.2 2.6 finish.1
  (3 shorter events, 0.0 us)
Async XLA Ops:
  4.8 24.8 %copy-start.5 = (s32[64]{0:T(128)S(1)}, s32[64]{0:T(128)}, u32[]{:S(2)}) copy-start(s32[64]{0:T(128)} %param.13) | copy-start | bytes 772
  4.8 166.0 %all-to-all-start = ((bf16[128,24,512]{2,1,0:T(8,128)(2,1)}), bf16[128,24,512]{2,1,0:T(8,128)(2,1)S(1)}, u32[]{:S(2)}, u32[]{:S(2)}) async-start(bf16[128,24,512]{2,1,0:T(8,128)(2,1)} %bitcast.29), calls=%async_computation | async-start | bytes 6291456 | tf_op jit(solution)/shard_map/all_to_all | solution.py:254
  24.4 38.5 %collective-permute-start = (bf16[3,512,384]{2,1,0:T(8,128)(2,1)}, bf16[3,512,384]{2,1,0:T(8,128)(2,1)}, u32[]{:S(2)}, u32[]{:S(2)}) collective-permute-start(bf16[3,512,384]{2,1,0:T(8,128)(2,1)} %bitcast.31), channel_id=1, source_target_pairs={{0,256},{4,260},{8,264},{12,268},{16,272},{20,276},{24,280},{28,28... | collective-permute-start | bytes 3538952 | tf_op jit(solution)/shard_map/ppermute | solution.py:323
  30.9 34.6 %copy-start.4 = (bf16[1,3,512,384]{3,2,1,0:T(8,128)(2,1)S(1)}, bf16[1,3,512,384]{3,2,1,0:T(8,128)(2,1)}, u32[]{:S(2)}) copy-start(bf16[1,3,512,384]{3,2,1,0:T(8,128)(2,1)} %param.12) | copy-start | bytes 3538948
  67.3 9.1 %collective-permute-start.1 = (bf16[3,512,384]{2,1,0:T(8,128)(2,1)}, bf16[3,512,384]{2,1,0:T(8,128)(2,1)}, u32[]{:S(2)}, u32[]{:S(2)}) collective-permute-start(bf16[3,512,384]{2,1,0:T(8,128)(2,1)} %get-tuple-element.25), channel_id=1, source_target_pairs={{0,1},{1,0},{2,3},{3,2},{4,5},{5,4},{6,7},{7,6},{8,9},{9,8},{10,11... | collective-permute-start | bytes 3538952 | tf_op jit(solution)/shard_map/ppermute | solution.py:262
  69.2 41.7 %collective-permute-start.2 = (bf16[3,512,384]{2,1,0:T(8,128)(2,1)}, bf16[3,512,384]{2,1,0:T(8,128)(2,1)}, u32[]{:S(2)}, u32[]{:S(2)}) collective-permute-start(bf16[3,512,384]{2,1,0:T(8,128)(2,1)} %get-tuple-element.25), channel_id=1, source_target_pairs={{0,2},{1,3},{2,0},{3,1},{4,6},{5,7},{6,4},{7,5},{8,10},{9,11},{10,... | collective-permute-start | bytes 3538952 | tf_op jit(solution)/shard_map/ppermute | solution.py:262
  74.0 67.8 %collective-permute-start.3 = (bf16[3,512,384]{2,1,0:T(8,128)(2,1)}, bf16[3,512,384]{2,1,0:T(8,128)(2,1)}, u32[]{:S(2)}, u32[]{:S(2)}) collective-permute-start(bf16[3,512,384]{2,1,0:T(8,128)(2,1)} %get-tuple-element.25), channel_id=1, source_target_pairs={{0,3},{1,2},{2,1},{3,0},{4,7},{5,6},{6,5},{7,4},{8,11},{9,10},{10,... | collective-permute-start | bytes 3538952 | tf_op jit(solution)/shard_map/ppermute | solution.py:262
  144.3 28.2 %copy-start = (bf16[192,192]{1,0:T(8,128)(2,1)S(1)}, bf16[192,192]{1,0:T(8,128)(2,1)}, u32[]{:S(2)}) copy-start(bf16[192,192]{1,0:T(8,128)(2,1)} %constant.37.clone.fold_hbm.unfold_hbm.unfold_ref) | copy-start | bytes 221188
  170.8 1.6 copy-start.3
  183.1 152.1 %all-to-all-start.1 = ((bf16[128,24,512]{2,1,0:T(8,128)(2,1)}), bf16[128,24,512]{2,1,0:T(8,128)(2,1)S(1)}, u32[]{:S(2)}, u32[]{:S(2)}) async-start(bf16[128,24,512]{2,1,0:T(8,128)(2,1)} %bitcast.30), calls=%async_computation.1 | async-start | bytes 6291456 | tf_op jit(solution)/shard_map/all_to_all | solution.py:254
  189.3 2.6 copy-start.6
  189.3 2.6 copy-start.7
  194.2 9.1 %collective-permute-start.4 = (bf16[512,1152]{0,1:T(8,128)(2,1)S(1)}, bf16[512,1152]{0,1:T(8,128)(2,1)S(1)}, u32[]{:S(2)}, u32[]{:S(2)}) collective-permute-start(bf16[512,1152]{0,1:T(8,128)(2,1)S(1)} %get-tuple-element.26), channel_id=1, source_target_pairs={{0,1},{1,0},{2,3},{3,2},{4,5},{5,4},{6,7},{7,6},{8,9},{9,8},{10,11... | collective-permute-start | bytes 3538952 | tf_op jit(solution)/shard_map/ppermute | solution.py:262
  196.2 39.9 %collective-permute-start.5 = (bf16[512,1152]{0,1:T(8,128)(2,1)S(1)}, bf16[512,1152]{0,1:T(8,128)(2,1)S(1)}, u32[]{:S(2)}, u32[]{:S(2)}) collective-permute-start(bf16[512,1152]{0,1:T(8,128)(2,1)S(1)} %get-tuple-element.27), channel_id=1, source_target_pairs={{0,2},{1,3},{2,0},{3,1},{4,6},{5,7},{6,4},{7,5},{8,10},{9,11},{10,... | collective-permute-start | bytes 3538952 | tf_op jit(solution)/shard_map/ppermute | solution.py:262
  201.0 66.5 %collective-permute-start.6 = (bf16[512,1152]{0,1:T(8,128)(2,1)S(1)}, bf16[512,1152]{0,1:T(8,128)(2,1)S(1)}, u32[]{:S(2)}, u32[]{:S(2)}) collective-permute-start(bf16[512,1152]{0,1:T(8,128)(2,1)S(1)} %get-tuple-element.28), channel_id=1, source_target_pairs={{0,3},{1,2},{2,1},{3,0},{4,7},{5,6},{6,5},{7,4},{8,11},{9,10},{10,... | collective-permute-start | bytes 3538952 | tf_op jit(solution)/shard_map/ppermute | solution.py:262
  269.6 65.6 %copy-start.1 = (f32[128,2]{0,1:T(2,128)S(1)}, f32[128,2]{0,1:T(2,128)}, u32[]{:S(2)}) copy-start(f32[128,2]{0,1:T(2,128)} %param.11) | copy-start | bytes 3076
  269.6 65.6 %copy-start.2 = (s32[2,128]{1,0:T(2,128)S(1)}, s32[2,128]{1,0:T(2,128)}, u32[]{:S(2)}) copy-start(s32[2,128]{1,0:T(2,128)} %get-tuple-element.14.slots_ref) | copy-start | bytes 3076

commit v6 on v5

--- a/solution.py
+++ b/solution.py
@@ -15,7 +15,8 @@
 LANES = GROUP * CAP
 MIB = 1 << 20
 VMEM_MIB = 60
-EXPERT_MIB = 107
+EXPERT_MIB = 36
+GRADS_MIB = 24
 
 
 def unfold_matrix():
@@ -137,14 +138,27 @@
         copy.wait()
 
 
+def hidden_units(x_ref, dy_ref, w_ref, hidden_ref, paired_ref):
+    units = hidden_ref.shape[1]
+    pre_gate = jnp.dot(x_ref[...], w_ref[0], preferred_element_type=jnp.float32)
+    pre_up = jnp.dot(x_ref[...], w_ref[1], preferred_element_type=jnp.float32)
+    hidden_grad = jnp.dot(dy_ref[...], w_ref[2], preferred_element_type=jnp.float32)
+    gate_sig = jax.nn.sigmoid(pre_gate)
+    gate_act = pre_gate * gate_sig
+    hidden_ref[...] = (gate_act * pre_up).astype(jnp.bfloat16)
+    gate_pre = hidden_grad * pre_up * gate_sig * (1.0 + pre_gate * (1.0 - gate_sig))
+    paired_ref[:, :units] = gate_pre.astype(jnp.bfloat16)
+    paired_ref[:, units:] = (hidden_grad * gate_act).astype(jnp.bfloat16)
+
+
 def expert_kernel(
-    recv_hbm, ahead_hbm, back_hbm, unfold_hbm, fold_hbm,
-    send_hbm, x_hbm, dy_hbm, hidden_hbm, paired_hbm,
-    chunk_ref, ahead_ref, back_ref, unfold_ref, fold_ref,
+    recv_ref, ahead_hbm, back_hbm, unfold_hbm, fold_hbm,
+    send_ref,
+    ahead_ref, back_ref, unfold_ref, fold_ref,
     x_ref, dy_ref, hidden_ref, paired_ref, y_ref, dx_ref,
-    recv_sems, load_sems, send_sems, keep_sems,
+    load_sems,
 ):
-    blocks = chunk_ref.shape[0]
+    blocks = recv_ref.shape[0]
     feature_dim = x_ref.shape[1]
     units = hidden_ref.shape[1]
     pairs = [(unfold_hbm, unfold_ref)]
@@ -154,38 +168,15 @@
         pltpu.make_async_copy(src, dst, load_sems.at[i]) for i, (src, dst) in enumerate(pairs)
     ]
     loads[0].start()
-    arrivals = start_all(
-        [
-            pltpu.make_async_copy(recv_hbm.at[b], chunk_ref.at[b], recv_sems.at[b])
-            for b in range(blocks)
-        ]
-    )
     start_all(loads[1:])
     loads[0].wait()
     unfold = unfold_ref[...]
     for b in range(blocks):
-        arrivals[b].wait()
-        unfold_block(b, chunk_ref[b], unfold, x_ref, dy_ref)
+        unfold_block(b, recv_ref[b], unfold, x_ref, dy_ref)
     for copy in loads[1:4]:
         copy.wait()
-    pre_gate = jnp.dot(x_ref[...], ahead_ref[0], preferred_element_type=jnp.float32)
-    pre_up = jnp.dot(x_ref[...], ahead_ref[1], preferred_element_type=jnp.float32)
-    hidden_grad = jnp.dot(dy_ref[...], ahead_ref[2], preferred_element_type=jnp.float32)
-    gate_sig = jax.nn.sigmoid(pre_gate)
-    gate_act = pre_gate * gate_sig
-    hidden_ref[...] = (gate_act * pre_up).astype(jnp.bfloat16)
-    gate_pre = hidden_grad * pre_up * gate_sig * (1.0 + pre_gate * (1.0 - gate_sig))
-    paired_ref[:, :units] = gate_pre.astype(jnp.bfloat16)
-    paired_ref[:, units:] = (hidden_grad * gate_act).astype(jnp.bfloat16)
+    hidden_units(x_ref, dy_ref, ahead_ref, hidden_ref, paired_ref)
     loads[4].wait()
-    copies = start_all(
-        [
-            pltpu.make_async_copy(x_ref, x_hbm, keep_sems.at[0]),
-            pltpu.make_async_copy(dy_ref, dy_hbm, keep_sems.at[1]),
-            pltpu.make_async_copy(hidden_ref, hidden_hbm, keep_sems.at[2]),
-            pltpu.make_async_copy(paired_ref, paired_hbm, keep_sems.at[3]),
-        ]
-    )
     width = feature_dim // QUARTERS
     for q in range(QUARTERS):
         cols = slice(q * width, (q + 1) * width)
@@ -200,9 +191,39 @@
     loads[5].wait()
     fold = fold_ref[...]
     for b in range(blocks):
-        chunk_ref[b] = fold_block(b, y_ref, dx_ref, fold)
+        send_ref[b] = fold_block(b, y_ref, dx_ref, fold)
+
+
+def grads_kernel(
+    recv_hbm, w_hbm, unfold_hbm,
+    terms_hbm,
+    chunk_ref, w_ref, unfold_ref, x_ref, dy_ref, hidden_ref, paired_ref, terms_ref, load_sems, out_sems,
+):
+    units = hidden_ref.shape[1]
+    pairs = [(recv_hbm, chunk_ref), (w_hbm, w_ref), (unfold_hbm, unfold_ref)]
+    loads = start_all(
+        [pltpu.make_async_copy(src, dst, load_sems.at[i]) for i, (src, dst) in enumerate(pairs)]
+    )
+    for copy in loads:
+        copy.wait()
+    for b in range(chunk_ref.shape[0]):
+        unfold_block(b, chunk_ref[b], unfold_ref[...], x_ref, dy_ref)
+    hidden_units(x_ref, dy_ref, w_ref, hidden_ref, paired_ref)
+    width = x_ref.shape[1] // QUARTERS
+    over_rows = (((0,), (0,)), ((), ()))
+    copies = []
+    for q in range(QUARTERS):
+        cols = slice(q * width, (q + 1) * width)
+        pair = lax.dot_general(
+            x_ref[:, cols], paired_ref[...], over_rows, preferred_element_type=jnp.float32
+        )
+        terms_ref[cols, : 2 * units] = pair.astype(jnp.bfloat16)
+        down = lax.dot_general(
+            dy_ref[:, cols], hidden_ref[...], over_rows, preferred_element_type=jnp.float32
+        )
+        terms_ref[cols, 2 * units :] = down.astype(jnp.bfloat16)
         copies += start_all(
-            [pltpu.make_async_copy(chunk_ref.at[b], send_hbm.at[b], send_sems.at[b])]
+            [pltpu.make_async_copy(terms_ref.at[cols], terms_hbm.at[cols], out_sems.at[q])]
         )
     for copy in copies:
         copy.wait()
@@ -334,13 +355,12 @@
 
     recv = exchange(send, ep_count)
 
-    send_back, rows_x, rows_dy, hidden, paired = pl.pallas_call(
+    send_back = pl.pallas_call(
         expert_kernel,
-        out_shape=(chunks_shape, rows_shape, rows_shape, hidden_shape, paired_shape),
-        in_specs=[hbm] * 5,
-        out_specs=(hbm,) * 5,
+        out_shape=chunks_shape,
+        in_specs=[vmem] + [hbm] * 4,
+        out_specs=vmem,
         scratch_shapes=[
-            scratch(chunks_shape),
             pltpu.VMEM((3, feature_dim, units), bf16),
             pltpu.VMEM((3 * units, feature_dim), bf16),
             fold_vmem,
@@ -351,20 +371,35 @@
             scratch(paired_shape),
             wide_vmem,
             wide_vmem,
-            dma((blocks,)),
             dma((6,)),
-            dma((blocks,)),
-            dma((4,)),
         ],
-        compiler_params=pltpu.CompilerParams(vmem_limit_bytes=EXPERT_MIB * (MIB // 2)),
+        compiler_params=pltpu.CompilerParams(vmem_limit_bytes=EXPERT_MIB * MIB),
         name="expert",
     )(recv, full_weights, back, unfold, fold)
 
     recv_back = exchange(send_back, ep_count)
 
-    pair_term = jnp.einsum("rc,rf->cf", rows_x, paired, preferred_element_type=jnp.float32)
-    down_term = jnp.einsum("rd,rf->df", rows_dy, hidden, preferred_element_type=jnp.float32)
-    terms = jnp.concatenate([pair_term.astype(bf16), down_term.astype(bf16)], axis=1)
+    terms_shape = jax.ShapeDtypeStruct((feature_dim, 3 * units), bf16)
+    terms = pl.pallas_call(
+        grads_kernel,
+        out_shape=terms_shape,
+        in_specs=[hbm] * 3,
+        out_specs=hbm,
+        scratch_shapes=[
+            scratch(chunks_shape),
+            pltpu.VMEM((3, feature_dim, units), bf16),
+            fold_vmem,
+            scratch(rows_shape),
+            scratch(rows_shape),
+            scratch(hidden_shape),
+            scratch(paired_shape),
+            scratch(terms_shape),
+            dma((3,)),
+            dma((QUARTERS,)),
+        ],
+        compiler_params=pltpu.CompilerParams(vmem_limit_bytes=GRADS_MIB * MIB),
+        name="grads",
+    )(recv, full_weights, unfold)
     total = jnp.zeros((shard_rows, 3 * units), jnp.float32)
     for mask in range(dp_count):
         start = (my_dp ^ mask) * shard_rows

time: 339 us -> 341 us (level)
  Pallas kernels: 17.4 us -> 27.6 us
  waiting for transfers between devices: 240 us -> 235 us
  matrix products: 4.44 us -> 0 us
    pallas_call x1 -> x2, Pallas kernels: 10.7 us -> 18.9 us  [the longest x1 10.5 us: body(): pl.pallas_call(grads_kernel, out_shape=terms_shape, in_specs=[hbm] * 3, o...]
    all_to_all x2, waiting for transfers between devices: 82.9 us -> 78.3 us  [exchange(): lax.all_to_all(chunks.reshape(ep_count, CHUNK, width), 'ep', split_axis=0...]
    dot_general x2 -> x0, matrix products: 4.44 us -> none  [the longest x1 2.58 us: body(): jnp.einsum('rd,rf->df', rows_dy, hidden, preferred_element_type=jnp.float32)]
  transfers between devices with their start and end apart: 9 -> 9, of which waited for: 7 -> 7; matrix products, arithmetic and copies ran while one was open for 8% -> 7% of each run, Pallas kernels for 0% -> 3%
where the time goes in v6:
time: 341 us; the launch traced here: 340 us
  waiting for transfers between devices  235 us (69%)
  starting transfers between devices  49.6 us (15%)
  Pallas kernels  27.6 us (8%)
  local copies, waits for them, and re-layouts  21.1 us (6%)
  other arithmetic  5.38 us (2%)
    ppermute x6, waiting for transfers between devices, dp_partner(): return lax.ppermute(value, 'dp', pairs)  124 us
    all_to_all x2, waiting for transfers between devices, exchange(): lax.all_to_all(chunks.reshape(ep_count, CHUNK, width), 'ep', split_axis=0...  78.3 us
    ppermute x1, waiting for transfers between devices, body(): partner = lax.ppermute(own_weights, 'ep', swap_pairs)  32 us
    all_to_all x2, starting transfers between devices, exchange(): lax.all_to_all(chunks.reshape(ep_count, CHUNK, width), 'ep', split_axis=0...  26.2 us
    ppermute x6, starting transfers between devices, dp_partner(): return lax.ppermute(value, 'dp', pairs)  18.2 us
    pallas_call x1, Pallas kernels, body(): pl.pallas_call(grads_kernel, out_shape=terms_shape, in_specs=[hbm] * 3, o...  10.5 us
    pallas_call x1, Pallas kernels, body(): pl.pallas_call(expert_kernel, out_shape=chunks_shape, in_specs=[vmem] + [...  8.36 us
    dynamic_update_slice x3, local copies, waits for them, and re-layouts, body(): lax.dynamic_update_slice_in_dim(full_weights, shard, start, axis=1)  7.29 us
  transfers between devices with their start and end apart: 9, of which 7 were waited for; matrix products, arithmetic and copies ran while one was open for 7% of the time, Pallas kernels for 3%

profile of v6, /device:TPU:64, one launch (start us, length us, event | category | flops | bytes accessed | tf_op | source)
XLA Modules:
  0.0 339.9 jit_solution(9952301043214180165)
XLA Ops:
  0.6 4.2 %prep.1 = (bf16[8,384,512]{2,1,0:T(8,128)(2,1)}, s32[2,128]{1,0:T(2,128)}) custom-call(bf16[128,2048]{1,0:T(8,128)(2,1)} %tok_hbm.1, bf16[128,2048]{1,0:T(8,128)(2,1)} %cot_hbm.1, s32[2,128]{1,0:T(2,128)} %bitcast.28, f32[2,128]{1,0:T(2,128)} %bitcast.24, s32[1,64]{1,0:T(1,128)} %bitcast.29, bf16[192,192]{1,0:T(8,128)(2,1)} %constant.37.clone.fold_hbm.unfold_hbm.unfold_ref), custom_call_target="tpu_custom_call" | custom-call | tf_op jit(solution)/shard_map/prep/pallas_call | solution.py:316
  4.8 0.0 copy-start.6
  4.8 19.6 %all-to-all-start = ((bf16[128,24,512]{2,1,0:T(8,128)(2,1)}), bf16[128,24,512]{2,1,0:T(8,128)(2,1)S(1)}, u32[]{:S(2)}, u32[]{:S(2)}) async-start(bf16[128,24,512]{2,1,0:T(8,128)(2,1)} %bitcast.26), calls=%async_computation | async-start | bytes 6291456 | tf_op jit(solution)/shard_map/all_to_all | solution.py:275
  24.4 5.2 %collective-permute-start = (bf16[3,512,384]{2,1,0:T(8,128)(2,1)}, bf16[3,512,384]{2,1,0:T(8,128)(2,1)}, u32[]{:S(2)}, u32[]{:S(2)}) collective-permute-start(bf16[3,512,384]{2,1,0:T(8,128)(2,1)} %bitcast.27), channel_id=1, source_target_pairs={{0,256},{4,260},{8,264},{12,268},{16,272},{20,276},{24,280},{28,28... | collective-permute-start | bytes 3538952 | tf_op jit(solution)/shard_map/ppermute | solution.py:344
  29.6 0.0 copy-done.6
  29.6 0.6 fusion
  30.9 0.0 copy-start.5
  30.9 32.0 %collective-permute-done = bf16[3,512,384]{2,1,0:T(8,128)(2,1)} collective-permute-done((bf16[3,512,384]{2,1,0:T(8,128)(2,1)}, bf16[3,512,384]{2,1,0:T(8,128)(2,1)}, u32[]{:S(2)}, u32[]{:S(2)}) %collective-permute-start) | collective-permute-done | bytes 1179680 | tf_op jit(solution)/shard_map/ppermute | solution.py:344
  62.9 2.5 broadcast_in_dim.10
  65.5 0.0 copy-done.5
  65.5 3.0 constant_dynamic-update-slice_fusion.3
  68.4 1.9 collective-permute-start.1
  70.3 4.8 %collective-permute-start.2 = (bf16[3,512,384]{2,1,0:T(8,128)(2,1)}, bf16[3,512,384]{2,1,0:T(8,128)(2,1)}, u32[]{:S(2)}, u32[]{:S(2)}) collective-permute-start(bf16[3,512,384]{2,1,0:T(8,128)(2,1)} %get-tuple-element.12), channel_id=1, source_target_pairs={{0,2},{1,3},{2,0},{3,1},{4,6},{5,7},{6,4},{7,5},{8,10},{9,11},{10,... | collective-permute-start | bytes 3538952 | tf_op jit(solution)/shard_map/ppermute | solution.py:283
  75.2 2.3 collective-permute-start.3
  77.6 0.0 collective-permute-done.1
  77.6 2.4 constant_dynamic-update-slice_fusion.2
  80.0 32.0 %collective-permute-done.2 = bf16[3,512,384]{2,1,0:T(8,128)(2,1)} collective-permute-done((bf16[3,512,384]{2,1,0:T(8,128)(2,1)}, bf16[3,512,384]{2,1,0:T(8,128)(2,1)}, u32[]{:S(2)}, u32[]{:S(2)}) %collective-permute-start.2) | collective-permute-done | bytes 1179680 | tf_op jit(solution)/shard_map/ppermute | solution.py:283
  112.0 2.4 constant_dynamic-update-slice_fusion.1
  114.4 28.9 %collective-permute-done.3 = bf16[3,512,384]{2,1,0:T(8,128)(2,1)} collective-permute-done((bf16[3,512,384]{2,1,0:T(8,128)(2,1)}, bf16[3,512,384]{2,1,0:T(8,128)(2,1)}, u32[]{:S(2)}, u32[]{:S(2)}) %collective-permute-start.3) | collective-permute-done | bytes 1179680 | tf_op jit(solution)/shard_map/ppermute | solution.py:283
  143.3 2.4 constant_dynamic-update-slice_fusion.ahead_hbm.w_hbm
  145.8 0.0 copy-start.2
  145.8 6.8 %copy.11 = bf16[3,384,2048]{2,1,0:T(8,128)(2,1)} copy(bf16[3,384,2048]{1,2,0:T(8,128)(2,1)} %bitcast.6) | data formatting | bytes 9437184 | tf_op jit(solution)/shard_map/transpose | solution.py:354
  152.5 18.3 %all-to-all-done = bf16[128,24,512]{2,1,0:T(8,128)(2,1)S(1)} async-done(((bf16[128,24,512]{2,1,0:T(8,128)(2,1)}), bf16[128,24,512]{2,1,0:T(8,128)(2,1)S(1)}, u32[]{:S(2)}, u32[]{:S(2)}) %all-to-all-start) | async-done | bytes 3145760 | tf_op jit(solution)/shard_map/all_to_all | solution.py:275
  170.8 0.0 copy-done.2
  170.8 0.0 copy-start
  170.8 2.3 copy-done
  173.1 8.4 %expert.1 = bf16[8,384,512]{2,1,0:T(8,128)(2,1)S(1)} custom-call(bf16[8,384,512]{2,1,0:T(8,128)(2,1)S(1)} %bitcast.20, bf16[3,2048,384]{2,1,0:T(8,128)(2,1)} %constant_dynamic-update-slice_fusion.ahead_hbm.w_hbm, bf16[1152,2048]{1,0:T(8,128)(2,1)S(1)} %bitcast.22, bf16[192,192]{1,0:T(8,128)(2,1)S(1)} %copy-done.2, bf16[192,192]{1,0:T(8,128)(2,1)S(1)} %copy-done.2), custom_call_target="tpu_custom_call" | custom-call | tf_op jit(solution)/shard_map/expert/pallas_call | solution.py:358
  181.5 0.0 copy-start.1
  181.5 1.7 copy-done.1
  183.3 6.6 %all-to-all-start.1 = ((bf16[128,24,512]{2,1,0:T(8,128)(2,1)}), bf16[128,24,512]{2,1,0:T(8,128)(2,1)}, u32[]{:S(2)}, u32[]{:S(2)}) async-start(bf16[128,24,512]{2,1,0:T(8,128)(2,1)} %bitcast.23), calls=%async_computation.1 | async-start | bytes 6291456 | tf_op jit(solution)/shard_map/all_to_all | solution.py:275
  189.9 10.5 %grads.1 = bf16[2048,1152]{1,0:T(8,128)(2,1)S(1)} custom-call(bf16[8,384,512]{2,1,0:T(8,128)(2,1)S(1)} %bitcast.21, bf16[3,2048,384]{2,1,0:T(8,128)(2,1)} %constant_dynamic-update-slice_fusion.ahead_hbm.w_hbm, bf16[192,192]{1,0:T(8,128)(2,1)S(1)} %copy-done.2), custom_call_target="tpu_custom_call" | custom-call | tf_op jit(solution)/shard_map/grads/pallas_call | solution.py:383
  200.4 0.3 constant_dynamic-slice_fusion.2
  200.7 3.1 collective-permute-start.6
  203.8 3.6 %collective-permute-start.5 = (bf16[512,1152]{1,0:T(8,128)(2,1)S(1)}, bf16[512,1152]{1,0:T(8,128)(2,1)S(1)}, u32[]{:S(2)}, u32[]{:S(2)}) collective-permute-start(bf16[512,1152]{1,0:T(8,128)(2,1)S(1)} %get-tuple-element.15), channel_id=1, source_target_pairs={{0,2},{1,3},{2,0},{3,1},{4,6},{5,7},{6,4},{7,5},{8,10},{9,11},{10,... | collective-permute-start | bytes 3538952 | tf_op jit(solution)/shard_map/ppermute | solution.py:283
  207.5 2.4 collective-permute-start.4
  209.8 29.8 %collective-permute-done.6 = bf16[512,1152]{1,0:T(8,128)(2,1)S(1)} collective-permute-done((bf16[512,1152]{1,0:T(8,128)(2,1)S(1)}, bf16[512,1152]{1,0:T(8,128)(2,1)S(1)}, u32[]{:S(2)}, u32[]{:S(2)}) %collective-permute-start.6) | collective-permute-done | bytes 1179680 | tf_op jit(solution)/shard_map/ppermute | solution.py:283
  239.7 33.6 %collective-permute-done.5 = bf16[512,1152]{1,0:T(8,128)(2,1)S(1)} collective-permute-done((bf16[512,1152]{1,0:T(8,128)(2,1)S(1)}, bf16[512,1152]{1,0:T(8,128)(2,1)S(1)}, u32[]{:S(2)}, u32[]{:S(2)}) %collective-permute-start.5) | collective-permute-done | bytes 1179680 | tf_op jit(solution)/shard_map/ppermute | solution.py:283
  273.3 0.0 collective-permute-done.4
  273.3 0.6 add_convert_fusion
  273.9 0.1 slice_bitcast_fusion.2
  274.0 0.0 copy-start.3
  274.1 0.0 copy-start.4
  274.1 1.2 maximum_bitcast_fusion
  275.2 60.1 %all-to-all-done.1 = bf16[128,24,512]{2,1,0:T(8,128)(2,1)} async-done(((bf16[128,24,512]{2,1,0:T(8,128)(2,1)}), bf16[128,24,512]{2,1,0:T(8,128)(2,1)}, u32[]{:S(2)}, u32[]{:S(2)}) %all-to-all-start.1) | async-done | bytes 3145760 | tf_op jit(solution)/shard_map/all_to_all | solution.py:275
  335.3 0.0 copy-done.3
  335.3 0.0 copy-done.4
  335.3 4.5 %finish.1 = (bf16[128,2048]{1,0:T(8,128)(2,1)}, bf16[128,2048]{1,0:T(8,128)(2,1)}) custom-call(bf16[8,384,512]{2,1,0:T(8,128)(2,1)} %bitcast.9.recv_ref, s32[2,128]{1,0:T(2,128)S(1)} %copy-done.4, f32[2,128]{1,0:T(2,128)S(1)} %bitcast.25, bf16[192,192]{1,0:T(8,128)(2,1)S(1)} %copy-done.2), custom_call_target="tpu_custom_call" | custom-call | tf_op jit(solution)/shard_map/finish/pallas_call | solution.py:413
Async XLA Ops:
  4.8 24.8 %copy-start.6 = (s32[64]{0:T(128)S(1)}, s32[64]{0:T(128)}, u32[]{:S(2)}) copy-start(s32[64]{0:T(128)} %param.13) | copy-start | bytes 772
  4.8 166.0 %all-to-all-start = ((bf16[128,24,512]{2,1,0:T(8,128)(2,1)}), bf16[128,24,512]{2,1,0:T(8,128)(2,1)S(1)}, u32[]{:S(2)}, u32[]{:S(2)}) async-start(bf16[128,24,512]{2,1,0:T(8,128)(2,1)} %bitcast.26), calls=%async_computation | async-start | bytes 6291456 | tf_op jit(solution)/shard_map/all_to_all | solution.py:275
  24.4 38.5 %collective-permute-start = (bf16[3,512,384]{2,1,0:T(8,128)(2,1)}, bf16[3,512,384]{2,1,0:T(8,128)(2,1)}, u32[]{:S(2)}, u32[]{:S(2)}) collective-permute-start(bf16[3,512,384]{2,1,0:T(8,128)(2,1)} %bitcast.27), channel_id=1, source_target_pairs={{0,256},{4,260},{8,264},{12,268},{16,272},{20,276},{24,280},{28,28... | collective-permute-start | bytes 3538952 | tf_op jit(solution)/shard_map/ppermute | solution.py:344
  30.9 34.5 %copy-start.5 = (bf16[1,3,512,384]{3,2,1,0:T(8,128)(2,1)S(1)}, bf16[1,3,512,384]{3,2,1,0:T(8,128)(2,1)}, u32[]{:S(2)}) copy-start(bf16[1,3,512,384]{3,2,1,0:T(8,128)(2,1)} %param.12) | copy-start | bytes 3538948
  68.4 9.1 %collective-permute-start.1 = (bf16[3,512,384]{2,1,0:T(8,128)(2,1)}, bf16[3,512,384]{2,1,0:T(8,128)(2,1)}, u32[]{:S(2)}, u32[]{:S(2)}) collective-permute-start(bf16[3,512,384]{2,1,0:T(8,128)(2,1)} %get-tuple-element.12), channel_id=1, source_target_pairs={{0,1},{1,0},{2,3},{3,2},{4,5},{5,4},{6,7},{7,6},{8,9},{9,8},{10,11... | collective-permute-start | bytes 3538952 | tf_op jit(solution)/shard_map/ppermute | solution.py:283
  70.3 41.6 %collective-permute-start.2 = (bf16[3,512,384]{2,1,0:T(8,128)(2,1)}, bf16[3,512,384]{2,1,0:T(8,128)(2,1)}, u32[]{:S(2)}, u32[]{:S(2)}) collective-permute-start(bf16[3,512,384]{2,1,0:T(8,128)(2,1)} %get-tuple-element.12), channel_id=1, source_target_pairs={{0,2},{1,3},{2,0},{3,1},{4,6},{5,7},{6,4},{7,5},{8,10},{9,11},{10,... | collective-permute-start | bytes 3538952 | tf_op jit(solution)/shard_map/ppermute | solution.py:283
  75.2 68.1 %collective-permute-start.3 = (bf16[3,512,384]{2,1,0:T(8,128)(2,1)}, bf16[3,512,384]{2,1,0:T(8,128)(2,1)}, u32[]{:S(2)}, u32[]{:S(2)}) collective-permute-start(bf16[3,512,384]{2,1,0:T(8,128)(2,1)} %get-tuple-element.12), channel_id=1, source_target_pairs={{0,3},{1,2},{2,1},{3,0},{4,7},{5,6},{6,5},{7,4},{8,11},{9,10},{10,... | collective-permute-start | bytes 3538952 | tf_op jit(solution)/shard_map/ppermute | solution.py:283
  145.8 25.0 %copy-start.2 = (bf16[192,192]{1,0:T(8,128)(2,1)S(1)}, bf16[192,192]{1,0:T(8,128)(2,1)}, u32[]{:S(2)}) copy-start(bf16[192,192]{1,0:T(8,128)(2,1)} %constant.37.clone.fold_hbm.unfold_hbm.unfold_ref) | copy-start | bytes 221188
  170.8 2.3 copy-start
  181.5 1.8 copy-start.1
  183.3 152.0 %all-to-all-start.1 = ((bf16[128,24,512]{2,1,0:T(8,128)(2,1)}), bf16[128,24,512]{2,1,0:T(8,128)(2,1)}, u32[]{:S(2)}, u32[]{:S(2)}) async-start(bf16[128,24,512]{2,1,0:T(8,128)(2,1)} %bitcast.23), calls=%async_computation.1 | async-start | bytes 6291456 | tf_op jit(solution)/shard_map/all_to_all | solution.py:275
  200.7 39.0 %collective-permute-start.6 = (bf16[512,1152]{1,0:T(8,128)(2,1)S(1)}, bf16[512,1152]{1,0:T(8,128)(2,1)S(1)}, u32[]{:S(2)}, u32[]{:S(2)}) collective-permute-start(bf16[512,1152]{1,0:T(8,128)(2,1)S(1)} %get-tuple-element.14), channel_id=1, source_target_pairs={{0,3},{1,2},{2,1},{3,0},{4,7},{5,6},{6,5},{7,4},{8,11},{9,10},{10,... | collective-permute-start | bytes 3538952 | tf_op jit(solution)/shard_map/ppermute | solution.py:283
  203.8 69.5 %collective-permute-start.5 = (bf16[512,1152]{1,0:T(8,128)(2,1)S(1)}, bf16[512,1152]{1,0:T(8,128)(2,1)S(1)}, u32[]{:S(2)}, u32[]{:S(2)}) collective-permute-start(bf16[512,1152]{1,0:T(8,128)(2,1)S(1)} %get-tuple-element.15), channel_id=1, source_target_pairs={{0,2},{1,3},{2,0},{3,1},{4,6},{5,7},{6,4},{7,5},{8,10},{9,11},{10,... | collective-permute-start | bytes 3538952 | tf_op jit(solution)/shard_map/ppermute | solution.py:283
  207.5 65.8 %collective-permute-start.4 = (bf16[512,1152]{1,0:T(8,128)(2,1)S(1)}, bf16[512,1152]{1,0:T(8,128)(2,1)S(1)}, u32[]{:S(2)}, u32[]{:S(2)}) collective-permute-start(bf16[512,1152]{1,0:T(8,128)(2,1)S(1)} %get-tuple-element.13), channel_id=1, source_target_pairs={{0,1},{1,0},{2,3},{3,2},{4,5},{5,4},{6,7},{7,6},{8,9},{9,8},{10,11... | collective-permute-start | bytes 3538952 | tf_op jit(solution)/shard_map/ppermute | solution.py:283
  274.0 61.3 %copy-start.3 = (f32[128,2]{0,1:T(2,128)S(1)}, f32[128,2]{0,1:T(2,128)}, u32[]{:S(2)}) copy-start(f32[128,2]{0,1:T(2,128)} %param.11) | copy-start | bytes 3076
  274.1 61.2 %copy-start.4 = (s32[2,128]{1,0:T(2,128)S(1)}, s32[2,128]{1,0:T(2,128)}, u32[]{:S(2)}) copy-start(s32[2,128]{1,0:T(2,128)} %get-tuple-element.8.slots_ref) | copy-start | bytes 3076

commit v7 on v6

--- a/solution.py
+++ b/solution.py
@@ -15,8 +15,8 @@
 LANES = GROUP * CAP
 MIB = 1 << 20
 VMEM_MIB = 60
-EXPERT_MIB = 36
-GRADS_MIB = 24
+EXPERT_MIB = 44
+GRADS_MIB = 28
 
 
 def unfold_matrix():

time: 341 us -> 338 us (level)
  transfers between devices with their start and end apart: 9 -> 9, of which waited for: 7 -> 7; matrix products, arithmetic and copies ran while one was open for 7% -> 6% of each run, Pallas kernels for 3% -> 3%
where the time goes in v7:
time: 338 us
  waiting for transfers between devices  236 us (70%)
  starting transfers between devices  49.6 us (15%)
  Pallas kernels  27.6 us (8%)
  local copies, waits for them, and re-layouts  18.8 us (6%)
  other arithmetic  4.12 us (1%)
    ppermute x6, waiting for transfers between devices, dp_partner(): return lax.ppermute(value, 'dp', pairs)  124 us
    all_to_all x2, waiting for transfers between devices, exchange(): lax.all_to_all(chunks.reshape(ep_count, CHUNK, width), 'ep', split_axis=0...  79.9 us
    ppermute x1, waiting for transfers between devices, body(): partner = lax.ppermute(own_weights, 'ep', swap_pairs)  32 us
    all_to_all x2, starting transfers between devices, exchange(): lax.all_to_all(chunks.reshape(ep_count, CHUNK, width), 'ep', split_axis=0...  26.2 us
    ppermute x6, starting transfers between devices, dp_partner(): return lax.ppermute(value, 'dp', pairs)  18.2 us
    pallas_call x1, Pallas kernels, body(): pl.pallas_call(grads_kernel, out_shape=terms_shape, in_specs=[hbm] * 3, o...  10.5 us
    pallas_call x1, Pallas kernels, body(): pl.pallas_call(expert_kernel, out_shape=chunks_shape, in_specs=[vmem] + [...  8.39 us
    dynamic_update_slice x3, local copies, waits for them, and re-layouts, body(): lax.dynamic_update_slice_in_dim(full_weights, shard, start, axis=1)  7.3 us
  transfers between devices with their start and end apart: 9, of which 7 were waited for; matrix products, arithmetic and copies ran while one was open for 6% of the time, Pallas kernels for 3%

profile of v7, /device:TPU:64, one launch (start us, length us, event | category | flops | bytes accessed | tf_op | source)
XLA Modules:
  0.0 337.6 jit_solution(15045561081040253239)
XLA Ops:
  0.6 4.2 %prep.1 = (bf16[8,384,512]{2,1,0:T(8,128)(2,1)}, s32[2,128]{1,0:T(2,128)}) custom-call(bf16[128,2048]{1,0:T(8,128)(2,1)} %tok_hbm.1, bf16[128,2048]{1,0:T(8,128)(2,1)} %cot_hbm.1, s32[2,128]{1,0:T(2,128)} %bitcast.28, f32[2,128]{1,0:T(2,128)} %bitcast.23, s32[1,64]{1,0:T(1,128)} %bitcast.29, bf16[192,192]{1,0:T(8,128)(2,1)} %constant.37.clone.fold_hbm.unfold_hbm.unfold_ref), custom_call_target="tpu_custom_call" | custom-call | tf_op jit(solution)/shard_map/prep/pallas_call | solution.py:316
  4.8 0.0 copy-start.5
  4.8 19.6 %all-to-all-start = ((bf16[128,24,512]{2,1,0:T(8,128)(2,1)}), bf16[128,24,512]{2,1,0:T(8,128)(2,1)S(1)}, u32[]{:S(2)}, u32[]{:S(2)}) async-start(bf16[128,24,512]{2,1,0:T(8,128)(2,1)} %bitcast.26), calls=%async_computation | async-start | bytes 6291456 | tf_op jit(solution)/shard_map/all_to_all | solution.py:275
  24.4 5.2 %collective-permute-start = (bf16[3,512,384]{2,1,0:T(8,128)(2,1)}, bf16[3,512,384]{2,1,0:T(8,128)(2,1)}, u32[]{:S(2)}, u32[]{:S(2)}) collective-permute-start(bf16[3,512,384]{2,1,0:T(8,128)(2,1)} %bitcast.27), channel_id=1, source_target_pairs={{0,256},{4,260},{8,264},{12,268},{16,272},{20,276},{24,280},{28,28... | collective-permute-start | bytes 3538952 | tf_op jit(solution)/shard_map/ppermute | solution.py:344
  29.6 0.0 copy-done.5
  29.6 0.6 fusion
  30.9 0.0 copy-start.4
  30.9 32.0 %collective-permute-done = bf16[3,512,384]{2,1,0:T(8,128)(2,1)} collective-permute-done((bf16[3,512,384]{2,1,0:T(8,128)(2,1)}, bf16[3,512,384]{2,1,0:T(8,128)(2,1)}, u32[]{:S(2)}, u32[]{:S(2)}) %collective-permute-start) | collective-permute-done | bytes 1179680 | tf_op jit(solution)/shard_map/ppermute | solution.py:344
  62.9 2.5 broadcast_in_dim.10
  65.5 0.0 copy-done.4
  65.5 1.7 constant_dynamic-update-slice_fusion.3
  67.2 1.9 collective-permute-start.1
  69.1 4.8 %collective-permute-start.2 = (bf16[3,512,384]{2,1,0:T(8,128)(2,1)}, bf16[3,512,384]{2,1,0:T(8,128)(2,1)}, u32[]{:S(2)}, u32[]{:S(2)}) collective-permute-start(bf16[3,512,384]{2,1,0:T(8,128)(2,1)} %get-tuple-element.12), channel_id=1, source_target_pairs={{0,2},{1,3},{2,0},{3,1},{4,6},{5,7},{6,4},{7,5},{8,10},{9,11},{10,... | collective-permute-start | bytes 3538952 | tf_op jit(solution)/shard_map/ppermute | solution.py:283
  73.9 2.3 collective-permute-start.3
  76.3 0.0 collective-permute-done.1
  76.3 2.4 constant_dynamic-update-slice_fusion.2
  78.7 32.1 %collective-permute-done.2 = bf16[3,512,384]{2,1,0:T(8,128)(2,1)} collective-permute-done((bf16[3,512,384]{2,1,0:T(8,128)(2,1)}, bf16[3,512,384]{2,1,0:T(8,128)(2,1)}, u32[]{:S(2)}, u32[]{:S(2)}) %collective-permute-start.2) | collective-permute-done | bytes 1179680 | tf_op jit(solution)/shard_map/ppermute | solution.py:283
  110.8 2.4 constant_dynamic-update-slice_fusion.1
  113.2 28.5 %collective-permute-done.3 = bf16[3,512,384]{2,1,0:T(8,128)(2,1)} collective-permute-done((bf16[3,512,384]{2,1,0:T(8,128)(2,1)}, bf16[3,512,384]{2,1,0:T(8,128)(2,1)}, u32[]{:S(2)}, u32[]{:S(2)}) %collective-permute-start.3) | collective-permute-done | bytes 1179680 | tf_op jit(solution)/shard_map/ppermute | solution.py:283
  141.7 2.4 constant_dynamic-update-slice_fusion.ahead_hbm.w_hbm
  144.2 0.0 copy-start.1
  144.2 6.8 %copy.11 = bf16[3,384,2048]{2,1,0:T(8,128)(2,1)} copy(bf16[3,384,2048]{1,2,0:T(8,128)(2,1)} %bitcast.6) | data formatting | bytes 9437184 | tf_op jit(solution)/shard_map/transpose | solution.py:354
  151.0 19.9 %all-to-all-done = bf16[128,24,512]{2,1,0:T(8,128)(2,1)S(1)} async-done(((bf16[128,24,512]{2,1,0:T(8,128)(2,1)}), bf16[128,24,512]{2,1,0:T(8,128)(2,1)S(1)}, u32[]{:S(2)}, u32[]{:S(2)}) %all-to-all-start) | async-done | bytes 3145760 | tf_op jit(solution)/shard_map/all_to_all | solution.py:275
  170.8 0.0 copy-done.1
  170.8 8.4 %expert.1 = bf16[8,384,512]{2,1,0:T(8,128)(2,1)S(1)} custom-call(bf16[8,384,512]{2,1,0:T(8,128)(2,1)S(1)} %bitcast.20, bf16[3,2048,384]{2,1,0:T(8,128)(2,1)} %constant_dynamic-update-slice_fusion.ahead_hbm.w_hbm, bf16[1152,2048]{1,0:T(8,128)(2,1)} %bitcast.25, bf16[192,192]{1,0:T(8,128)(2,1)S(1)} %copy-done.1, bf16[192,192]{1,0:T(8,128)(2,1)S(1)} %copy-done.1), custom_call_target="tpu_custom_call" | custom-call | tf_op jit(solution)/shard_map/expert/pallas_call | solution.py:358
  179.2 0.0 copy-start
  179.2 1.7 copy-done
  181.0 6.6 %all-to-all-start.1 = ((bf16[128,24,512]{2,1,0:T(8,128)(2,1)}), bf16[128,24,512]{2,1,0:T(8,128)(2,1)}, u32[]{:S(2)}, u32[]{:S(2)}) async-start(bf16[128,24,512]{2,1,0:T(8,128)(2,1)} %bitcast.22), calls=%async_computation.1 | async-start | bytes 6291456 | tf_op jit(solution)/shard_map/all_to_all | solution.py:275
  187.6 10.5 %grads.1 = bf16[2048,1152]{1,0:T(8,128)(2,1)S(1)} custom-call(bf16[8,384,512]{2,1,0:T(8,128)(2,1)S(1)} %bitcast.21, bf16[3,2048,384]{2,1,0:T(8,128)(2,1)} %constant_dynamic-update-slice_fusion.ahead_hbm.w_hbm, bf16[192,192]{1,0:T(8,128)(2,1)S(1)} %copy-done.1), custom_call_target="tpu_custom_call" | custom-call | tf_op jit(solution)/shard_map/grads/pallas_call | solution.py:383
  198.1 0.3 constant_dynamic-slice_fusion.2
  198.4 3.1 collective-permute-start.6
  201.6 3.6 %collective-permute-start.5 = (bf16[512,1152]{1,0:T(8,128)(2,1)S(1)}, bf16[512,1152]{1,0:T(8,128)(2,1)S(1)}, u32[]{:S(2)}, u32[]{:S(2)}) collective-permute-start(bf16[512,1152]{1,0:T(8,128)(2,1)S(1)} %get-tuple-element.15), channel_id=1, source_target_pairs={{0,2},{1,3},{2,0},{3,1},{4,6},{5,7},{6,4},{7,5},{8,10},{9,11},{10,... | collective-permute-start | bytes 3538952 | tf_op jit(solution)/shard_map/ppermute | solution.py:283
  205.2 2.4 collective-permute-start.4
  207.5 29.8 %collective-permute-done.6 = bf16[512,1152]{1,0:T(8,128)(2,1)S(1)} collective-permute-done((bf16[512,1152]{1,0:T(8,128)(2,1)S(1)}, bf16[512,1152]{1,0:T(8,128)(2,1)S(1)}, u32[]{:S(2)}, u32[]{:S(2)}) %collective-permute-start.6) | collective-permute-done | bytes 1179680 | tf_op jit(solution)/shard_map/ppermute | solution.py:283
  237.4 33.6 %collective-permute-done.5 = bf16[512,1152]{1,0:T(8,128)(2,1)S(1)} collective-permute-done((bf16[512,1152]{1,0:T(8,128)(2,1)S(1)}, bf16[512,1152]{1,0:T(8,128)(2,1)S(1)}, u32[]{:S(2)}, u32[]{:S(2)}) %collective-permute-start.5) | collective-permute-done | bytes 1179680 | tf_op jit(solution)/shard_map/ppermute | solution.py:283
  271.0 0.0 collective-permute-done.4
  271.0 0.6 add_convert_fusion
  271.6 0.1 slice_bitcast_fusion.2
  271.7 0.0 copy-start.2
  271.7 0.0 copy-start.3
  271.7 1.2 maximum_bitcast_fusion
  272.9 60.1 %all-to-all-done.1 = bf16[128,24,512]{2,1,0:T(8,128)(2,1)} async-done(((bf16[128,24,512]{2,1,0:T(8,128)(2,1)}), bf16[128,24,512]{2,1,0:T(8,128)(2,1)}, u32[]{:S(2)}, u32[]{:S(2)}) %all-to-all-start.1) | async-done | bytes 3145760 | tf_op jit(solution)/shard_map/all_to_all | solution.py:275
  333.0 0.0 copy-done.2
  333.0 0.0 copy-done.3
  333.0 4.5 %finish.1 = (bf16[128,2048]{1,0:T(8,128)(2,1)}, bf16[128,2048]{1,0:T(8,128)(2,1)}) custom-call(bf16[8,384,512]{2,1,0:T(8,128)(2,1)} %bitcast.9.recv_ref, s32[2,128]{1,0:T(2,128)S(1)} %copy-done.3, f32[2,128]{1,0:T(2,128)S(1)} %bitcast.24, bf16[192,192]{1,0:T(8,128)(2,1)S(1)} %copy-done.1), custom_call_target="tpu_custom_call" | custom-call | tf_op jit(solution)/shard_map/finish/pallas_call | solution.py:413
Async XLA Ops:
  4.8 24.8 %copy-start.5 = (s32[64]{0:T(128)S(1)}, s32[64]{0:T(128)}, u32[]{:S(2)}) copy-start(s32[64]{0:T(128)} %param.13) | copy-start | bytes 772
  4.8 166.0 %all-to-all-start = ((bf16[128,24,512]{2,1,0:T(8,128)(2,1)}), bf16[128,24,512]{2,1,0:T(8,128)(2,1)S(1)}, u32[]{:S(2)}, u32[]{:S(2)}) async-start(bf16[128,24,512]{2,1,0:T(8,128)(2,1)} %bitcast.26), calls=%async_computation | async-start | bytes 6291456 | tf_op jit(solution)/shard_map/all_to_all | solution.py:275
  24.4 38.5 %collective-permute-start = (bf16[3,512,384]{2,1,0:T(8,128)(2,1)}, bf16[3,512,384]{2,1,0:T(8,128)(2,1)}, u32[]{:S(2)}, u32[]{:S(2)}) collective-permute-start(bf16[3,512,384]{2,1,0:T(8,128)(2,1)} %bitcast.27), channel_id=1, source_target_pairs={{0,256},{4,260},{8,264},{12,268},{16,272},{20,276},{24,280},{28,28... | collective-permute-start | bytes 3538952 | tf_op jit(solution)/shard_map/ppermute | solution.py:344
  30.9 34.5 %copy-start.4 = (bf16[1,3,512,384]{3,2,1,0:T(8,128)(2,1)S(1)}, bf16[1,3,512,384]{3,2,1,0:T(8,128)(2,1)}, u32[]{:S(2)}) copy-start(bf16[1,3,512,384]{3,2,1,0:T(8,128)(2,1)} %param.12) | copy-start | bytes 3538948
  67.2 9.1 %collective-permute-start.1 = (bf16[3,512,384]{2,1,0:T(8,128)(2,1)}, bf16[3,512,384]{2,1,0:T(8,128)(2,1)}, u32[]{:S(2)}, u32[]{:S(2)}) collective-permute-start(bf16[3,512,384]{2,1,0:T(8,128)(2,1)} %get-tuple-element.12), channel_id=1, source_target_pairs={{0,1},{1,0},{2,3},{3,2},{4,5},{5,4},{6,7},{7,6},{8,9},{9,8},{10,11... | collective-permute-start | bytes 3538952 | tf_op jit(solution)/shard_map/ppermute | solution.py:283
  69.1 41.7 %collective-permute-start.2 = (bf16[3,512,384]{2,1,0:T(8,128)(2,1)}, bf16[3,512,384]{2,1,0:T(8,128)(2,1)}, u32[]{:S(2)}, u32[]{:S(2)}) collective-permute-start(bf16[3,512,384]{2,1,0:T(8,128)(2,1)} %get-tuple-element.12), channel_id=1, source_target_pairs={{0,2},{1,3},{2,0},{3,1},{4,6},{5,7},{6,4},{7,5},{8,10},{9,11},{10,... | collective-permute-start | bytes 3538952 | tf_op jit(solution)/shard_map/ppermute | solution.py:283
  73.9 67.8 %collective-permute-start.3 = (bf16[3,512,384]{2,1,0:T(8,128)(2,1)}, bf16[3,512,384]{2,1,0:T(8,128)(2,1)}, u32[]{:S(2)}, u32[]{:S(2)}) collective-permute-start(bf16[3,512,384]{2,1,0:T(8,128)(2,1)} %get-tuple-element.12), channel_id=1, source_target_pairs={{0,3},{1,2},{2,1},{3,0},{4,7},{5,6},{6,5},{7,4},{8,11},{9,10},{10,... | collective-permute-start | bytes 3538952 | tf_op jit(solution)/shard_map/ppermute | solution.py:283
  144.2 26.6 %copy-start.1 = (bf16[192,192]{1,0:T(8,128)(2,1)S(1)}, bf16[192,192]{1,0:T(8,128)(2,1)}, u32[]{:S(2)}) copy-start(bf16[192,192]{1,0:T(8,128)(2,1)} %constant.37.clone.fold_hbm.unfold_hbm.unfold_ref) | copy-start | bytes 221188
  179.2 1.8 copy-start
  181.0 152.0 %all-to-all-start.1 = ((bf16[128,24,512]{2,1,0:T(8,128)(2,1)}), bf16[128,24,512]{2,1,0:T(8,128)(2,1)}, u32[]{:S(2)}, u32[]{:S(2)}) async-start(bf16[128,24,512]{2,1,0:T(8,128)(2,1)} %bitcast.22), calls=%async_computation.1 | async-start | bytes 6291456 | tf_op jit(solution)/shard_map/all_to_all | solution.py:275
  198.4 38.9 %collective-permute-start.6 = (bf16[512,1152]{1,0:T(8,128)(2,1)S(1)}, bf16[512,1152]{1,0:T(8,128)(2,1)S(1)}, u32[]{:S(2)}, u32[]{:S(2)}) collective-permute-start(bf16[512,1152]{1,0:T(8,128)(2,1)S(1)} %get-tuple-element.14), channel_id=1, source_target_pairs={{0,3},{1,2},{2,1},{3,0},{4,7},{5,6},{6,5},{7,4},{8,11},{9,10},{10,... | collective-permute-start | bytes 3538952 | tf_op jit(solution)/shard_map/ppermute | solution.py:283
  201.6 69.4 %collective-permute-start.5 = (bf16[512,1152]{1,0:T(8,128)(2,1)S(1)}, bf16[512,1152]{1,0:T(8,128)(2,1)S(1)}, u32[]{:S(2)}, u32[]{:S(2)}) collective-permute-start(bf16[512,1152]{1,0:T(8,128)(2,1)S(1)} %get-tuple-element.15), channel_id=1, source_target_pairs={{0,2},{1,3},{2,0},{3,1},{4,6},{5,7},{6,4},{7,5},{8,10},{9,11},{10,... | collective-permute-start | bytes 3538952 | tf_op jit(solution)/shard_map/ppermute | solution.py:283
  205.2 65.8 %collective-permute-start.4 = (bf16[512,1152]{1,0:T(8,128)(2,1)S(1)}, bf16[512,1152]{1,0:T(8,128)(2,1)S(1)}, u32[]{:S(2)}, u32[]{:S(2)}) collective-permute-start(bf16[512,1152]{1,0:T(8,128)(2,1)S(1)} %get-tuple-element.13), channel_id=1, source_target_pairs={{0,1},{1,0},{2,3},{3,2},{4,5},{5,4},{6,7},{7,6},{8,9},{9,8},{10,11... | collective-permute-start | bytes 3538952 | tf_op jit(solution)/shard_map/ppermute | solution.py:283
  271.7 61.3 %copy-start.2 = (f32[128,2]{0,1:T(2,128)S(1)}, f32[128,2]{0,1:T(2,128)}, u32[]{:S(2)}) copy-start(f32[128,2]{0,1:T(2,128)} %param.11) | copy-start | bytes 3076
  271.7 61.3 %copy-start.3 = (s32[2,128]{1,0:T(2,128)S(1)}, s32[2,128]{1,0:T(2,128)}, u32[]{:S(2)}) copy-start(s32[2,128]{1,0:T(2,128)} %get-tuple-element.8.slots_ref) | copy-start | bytes 3076
